TPU v7x, 128 devices: a whole 4x4x4 slice. The times are simulated.
128 devices in a mesh: role: 2 (over y_hi), dp: 4 (over y_lo, core), ctx: 16 (over x, z).
Axes of the slice: x: 4, y: 4 (y_hi: 2, y_lo: 2; y = y_hi * 2 + y_lo), z: 4, core: 2. Of those that a mesh axis runs over, the one named last changes fastest.
Arguments:
- teacher_states: bfloat16 [4, 2048, 5120], P('dp', 'ctx'), may hold values from -50 to 50
- student_states: bfloat16 [4, 2048, 3584], P('dp', 'ctx'), may hold values from -50 to 50
- teacher_gain: float32 [5120], replicated, may hold values from 0.25 to 1.75
- student_gain: float32 [3584], replicated, may hold values from 0.25 to 1.75
- mentor_output_weights: bfloat16 [4, 5120, 2048], P(None, None, 'ctx'), may hold values from -2 to 2
- student_heads: bfloat16 [4, 3584, 2048], P(None, None, 'ctx'), may hold values from -2 to 2
- segments: int32 [4, 2048], P('dp', 'ctx'), may hold values from 0 to 31, never falling along the last dimension, each value on 1 to 256 neighbouring positions
- targets: int32 [4, 2048, 4], P('dp', 'ctx'), may hold values from 0 to 2047
Outputs:
- grad_heads: float32 [4, 3584, 2048], P(None, ('role', 'dp'), 'ctx')
- frame_terms: float32 [2, 4, 2048, 4], P('role', 'dp', 'ctx')
All inputs are finite; a program needn't handle non-finite values.
Results may differ from a plain program's by a relative error of at most 0.0048.
Values may be sent and summed in bfloat16 or wider, within the bound.
No kernel may reach another device: no remote copies, remote signals or barrier semaphores. Data moves between devices by JAX's collectives and lax.ppermute only.
A program may use at most 192 MiB of HBM per device.

v0:
```python
import jax
import jax.numpy as jnp
from jax import lax
from jax.sharding import Mesh
from jax.sharding import PartitionSpec as P

QUANTIZER_TOTAL = 4
MBATCH = 4
CTX = ("ctx_0", "ctx_1")


epsilon = 1e-06
sharpness_divisor = 2.0
blend_ratio = 0.5


def sent_together(arrays, axis, dim, along):
    columns = [a.reshape(*a.shape[:along], -1) for a in arrays]
    both = jnp.concatenate(columns, axis=along)
    filled, at, done = (lax.all_gather(both, axis, axis=dim, tiled=True), 0, [])
    for a, column in zip(arrays, columns):
        share = filled[..., at : at + column.shape[along]]
        done.append(share.reshape(*share.shape[:along], *a.shape[along:]))
        at += column.shape[along]
    return tuple(done)


def copy_for_each(array, axis):
    copies = jnp.broadcast_to(array, (lax.axis_size(axis), *array.shape))
    return lax.all_to_all(copies, axis, split_axis=0, concat_axis=0, tiled=True)


def collected_together(array, axis):
    leaves = jax.tree.leaves(array)
    turns = sorted(range(len(leaves)), key=lambda k: -leaves[k].size)
    width = (1, *leaves[turns[0]].shape)[-1]
    lines = [
        jnp.pad(leaves[k].reshape(-1), (0, -leaves[k].size % width)).reshape(-1, width)
        for k in turns
    ]
    both, at, found = (copy_for_each(jnp.concatenate(lines), axis), 0, {})
    for k, line in zip(turns, lines):
        share = both[:, at : at + len(line)].reshape(len(both), -1)
        found[k] = share[:, : leaves[k].size].reshape(-1, *leaves[k].shape)
        at += len(line)
    numbers = iter(range(len(leaves)))
    return jax.tree.map(lambda _: found[next(numbers)], array)


def joined_by_halves(pieces, combine):
    while len(jax.tree.leaves(pieces)[0]) > 1:
        pieces = jax.vmap(combine)(
            *(jax.tree.map(lambda part: part[side::2], pieces) for side in (0, 1))
        )
    return jax.tree.map(lambda part: part[0], pieces)


def combined_all(array, axis, combine):
    pieces = collected_together(array, axis)
    return joined_by_halves(pieces, combine)


def cut_along(array, dim, length):
    lengths = array.shape
    pieces = array.reshape(*lengths[:dim], length, lengths[dim] // length, *lengths[dim + 1 :])
    return jnp.moveaxis(pieces, dim, 0)


def sum_at_owner(array, axis, dim):
    length = lax.axis_size(axis)
    pieces = lax.all_to_all(cut_along(array, dim, length), axis, 0, 0, tiled=True)
    return jnp.sum(pieces, axis=0)


def whole_of(array, axes, dim):
    filled = array
    for number in range(len(axes) - 1, -1, -1):
        filled = lax.all_gather(filled, axes[number], axis=dim, tiled=True)
    return filled


def shifted(value, axis, steps):
    count = lax.axis_size(axis)
    initial, last = (max(0, -steps), min(count, count - steps))
    return lax.ppermute(value, axis, [(source, source + steps) for source in range(initial, last)])


def normalize(states, gain):
    values = states.astype(jnp.float32)
    factor = lax.rsqrt(jnp.mean(values * values, axis=-1, keepdims=True) + epsilon)
    return (values * factor * gain).astype(jnp.bfloat16)


def merge_teacher(first, second):
    largest_activation = jnp.maximum(first[0], second[0])
    return (
        largest_activation,
        first[1] * jnp.exp(first[0] - largest_activation)
        + second[1] * jnp.exp(second[0] - largest_activation),
    )


def merge_student(first, second):
    largest_activation = jnp.maximum(first[0], second[0])
    return (
        largest_activation,
        first[1] * jnp.exp(first[0] - largest_activation)
        + second[1] * jnp.exp(second[0] - largest_activation),
        first[2] * jnp.exp((first[0] - largest_activation) / sharpness_divisor)
        + second[2] * jnp.exp((second[0] - largest_activation) / sharpness_divisor),
    )


def on_device(
    teacher_states,
    student_states,
    teacher_gain,
    student_gain,
    mentor_output_weights,
    student_heads,
    segments,
    targets,
):
    columns = mentor_output_weights.shape[2]
    ctx_count = lax.axis_size(CTX)
    ctx_rank = lax.axis_index(CTX)
    col_start = ctx_rank * columns
    rows_here = teacher_states.shape[1]
    batch_rows = rows_here // MBATCH
    group_rows = batch_rows * ctx_count
    all_segments, all_targets = sent_together((segments, targets), CTX, 1, 2)
    length = all_segments.shape[1]
    documents = 2 * ctx_count
    members = (all_segments[0][None, :] == jnp.arange(documents, dtype=jnp.int32)[:, None]).astype(
        jnp.float32
    )
    counts = jnp.sum(members, axis=1)
    row_sizes = jnp.dot(counts, members, precision=lax.Precision.HIGHEST)
    weights = length / (documents * row_sizes)
    own_targets = all_targets[0] - col_start
    is_teacher = lax.axis_index("role") == 0
    positions = jnp.arange(columns)

    def per_batch(values, batch_index):
        trailing = values.shape[1:]
        return values.reshape((ctx_count, MBATCH, batch_rows) + trailing)[:, batch_index].reshape(
            (group_rows,) + trailing
        )

    gradient = jnp.zeros((QUANTIZER_TOTAL, student_heads.shape[1], columns), jnp.float32)
    frame_parts = []
    blocks = []
    teacher_parts = []
    for batch_index in range(MBATCH):
        teacher_local_rows = normalize(
            teacher_states[0, batch_index * batch_rows : (batch_index + 1) * batch_rows],
            teacher_gain,
        )
        scaled = (
            lax.cond(
                is_teacher,
                lambda piece: jnp.einsum(
                    "rd,qdc->rqc", piece, mentor_output_weights, preferred_element_type=jnp.float32
                ),
                lambda piece: jnp.zeros((piece.shape[0], QUANTIZER_TOTAL, columns), jnp.float32),
                lax.all_gather(teacher_local_rows, CTX, axis=0, tiled=True),
            )
            / sharpness_divisor
        )
        teacher_local_peak = jnp.max(scaled, axis=2)
        teacher_largest_activation, totals = combined_all(
            (teacher_local_peak, jnp.sum(jnp.exp(scaled - teacher_local_peak[:, :, None]), axis=2)),
            CTX,
            merge_teacher,
        )
        log_probs = scaled - (teacher_largest_activation + jnp.log(totals))[:, :, None]
        teacher_hits = positions[None, None, :] == per_batch(own_targets, batch_index)[:, :, None]
        picked = -jnp.sum(jnp.where(teacher_hits, log_probs, 0.0), axis=2)
        teacher_terms = sum_at_owner(picked, CTX, 0)
        block = log_probs.astype(jnp.bfloat16)
        blocks.append(block)
        teacher_parts.append(teacher_terms)
    arrived = shifted(jnp.stack(blocks), "role", 1)
    for batch_index in range(MBATCH):
        received = arrived[batch_index]
        student_gradient = gradient
        local_rows = normalize(
            student_states[0, batch_index * batch_rows : (batch_index + 1) * batch_rows],
            student_gain,
        )
        gathered = whole_of(local_rows, CTX, 0)
        raw_activation_grid = lax.cond(
            is_teacher,
            lambda rows: jnp.zeros((rows.shape[0], QUANTIZER_TOTAL, columns), jnp.float32),
            lambda rows: jnp.einsum(
                "rd,qdc->rqc", rows, student_heads, preferred_element_type=jnp.float32
            ),
            gathered,
        )
        local_peak = jnp.max(raw_activation_grid, axis=2)
        centered_activations = raw_activation_grid - local_peak[:, :, None]
        largest_activation, plain, warmed_totals = combined_all(
            (
                local_peak,
                jnp.sum(jnp.exp(centered_activations), axis=2),
                jnp.sum(jnp.exp(centered_activations / sharpness_divisor), axis=2),
            ),
            CTX,
            merge_student,
        )
        untempered_logdensity = (
            raw_activation_grid - (largest_activation + jnp.log(plain))[:, :, None]
        )
        warmed_logdensity = (
            raw_activation_grid / sharpness_divisor
            - (largest_activation / sharpness_divisor + jnp.log(warmed_totals))[:, :, None]
        )
        teacher_logp = received.astype(jnp.float32)
        mentor_distribution = jnp.exp(teacher_logp)
        hits = (positions[None, None, :] == per_batch(own_targets, batch_index)[:, :, None]).astype(
            jnp.float32
        )
        kullback_gap = jnp.sum(mentor_distribution * (teacher_logp - warmed_logdensity), axis=2)
        mismatch_penalty = -jnp.sum(hits * untempered_logdensity, axis=2)
        loss_values = (
            blend_ratio * sharpness_divisor * sharpness_divisor * kullback_gap
            + (1.0 - blend_ratio) * mismatch_penalty
        )
        terms = sum_at_owner(loss_values, CTX, 0)
        gradient_scaling = per_batch(weights, batch_index)[:, None, None] * (
            blend_ratio * sharpness_divisor * (jnp.exp(warmed_logdensity) - mentor_distribution)
            + (1.0 - blend_ratio) * (jnp.exp(untempered_logdensity) - hits)
        )
        gradient_scaling = gradient_scaling.astype(jnp.bfloat16)
        student_gradient = lax.cond(
            is_teacher,
            lambda total: total,
            lambda total: total
            + jnp.einsum(
                "rd,rqc->qdc", gathered, gradient_scaling, preferred_element_type=jnp.float32
            ),
            student_gradient,
        )
        gradient = student_gradient
        frame_parts.append(jnp.where(is_teacher, teacher_parts[batch_index], terms))
    shares = lax.psum_scatter(gradient, ("role", "dp"), scatter_dimension=1, tiled=True)
    frame_terms = jnp.concatenate(frame_parts, axis=0).reshape(1, 1, rows_here, QUANTIZER_TOTAL)
    return (shares, frame_terms)


def solution(mesh):
    finer = Mesh(
        mesh.devices.reshape(mesh.shape["role"], mesh.shape["dp"], 4, 4),
        ("role", "dp", "ctx_0", "ctx_1"),
    )
    placed = (
        P("dp", CTX, None),
        P("dp", CTX, None),
        P(),
        P(),
        P(None, None, CTX),
        P(None, None, CTX),
        P("dp", CTX),
        P("dp", CTX, None),
    )
    return jax.shard_map(
        on_device,
        mesh=finer,
        in_specs=placed,
        out_specs=(P(None, ("role", "dp"), CTX), P("role", "dp", CTX, None)),
        check_vma=False,
    )
```

profile of v0, /device:TPU:24, one launch (start us, length us, event | category | flops | bytes accessed | tf_op | source)
XLA Modules:
  0.0 725.8 jit_solution(15006021371325651114)
XLA Ops:
  10.4 16.0 %all_gather.40 = bf16[128,3584]{1,0:T(8,128)(2,1)} all-gather(bf16[32,3584]{1,0:T(8,128)(2,1)S(1)} %get-tuple-element.260), channel_id=1, replica_groups=mesh['role'=2,'dp'=4,'ctx_0'=4,'ctx_1'=4] {'ctx_1'}, dimensions={0}, use_global_device_ids=true | all-gather | bytes 1146880 | tf_op jit(solution)/shard_map/all_gather | solution.py:78
  26.5 16.6 %all_gather.48 = bf16[128,3584]{1,0:T(8,128)(2,1)} all-gather(bf16[32,3584]{1,0:T(8,128)(2,1)S(1)} %get-tuple-element.259), channel_id=1, replica_groups=mesh['role'=2,'dp'=4,'ctx_0'=4,'ctx_1'=4] {'ctx_1'}, dimensions={0}, use_global_device_ids=true | all-gather | bytes 1146880 | tf_op jit(solution)/shard_map/all_gather | solution.py:78
  43.2 14.9 %all_gather.46 = bf16[128,3584]{1,0:T(8,128)(2,1)} all-gather(bf16[32,3584]{1,0:T(8,128)(2,1)S(1)} %get-tuple-element.258), channel_id=1, replica_groups=mesh['role'=2,'dp'=4,'ctx_0'=4,'ctx_1'=4] {'ctx_1'}, dimensions={0}, use_global_device_ids=true | all-gather | bytes 1146880 | tf_op jit(solution)/shard_map/all_gather | solution.py:78
  58.2 14.3 %all_gather.50 = bf16[128,3584]{1,0:T(8,128)(2,1)} all-gather(bf16[32,3584]{1,0:T(8,128)(2,1)S(1)} %get-tuple-element.257), channel_id=1, replica_groups=mesh['role'=2,'dp'=4,'ctx_0'=4,'ctx_1'=4] {'ctx_1'}, dimensions={0}, use_global_device_ids=true | all-gather | bytes 1146880 | tf_op jit(solution)/shard_map/all_gather | solution.py:78
  76.5 23.9 %all_gather.39 = s32[1,2048,5]{1,2,0:T(8,128)S(1)} all-gather(s32[1,128,5]{1,2,0:T(8,128)S(1)} %pad_add_fusion), channel_id=1, replica_groups=mesh['role'=2,'dp'=4,'ctx_0'=4,'ctx_1'=4] {'ctx_0','ctx_1'}, dimensions={1}, use_global_device_ids=true | all-gather | bytes 43520 | tf_op jit(solution)/shard_map/all_gather | solution.py:20
  106.8 11.3 %conditional.12 = (f32[512,4,128]{0,2,1:T(8,128)S(1)}, f32[512,4]{0,1:T(4,128)S(1)}) conditional(s32[]{:T(128)} %convert_element_type.149, (bf16[512,3584]{1,0:T(8,128)(2,1)}, bf16[4,3584,128]{2,1,0:T(8,128)(2,1)}) %tuple.96, () %tuple.97), branch_computations={%region_2.4_spmd, %region_4.0_spmd} | conditional | flops 1879308288 | bytes 16785424 | solution.py:192
  124.1 11.9 %conditional.18 = (f32[512,4,128]{0,2,1:T(8,128)S(1)}, f32[512,4]{0,1:T(4,128)S(1)}) conditional(s32[]{:T(128)} %convert_element_type.149, (bf16[512,3584]{1,0:T(8,128)(2,1)}, bf16[4,3584,128]{2,1,0:T(8,128)(2,1)}) %tuple.108, () %tuple.109), branch_computations={%region_34.36_spmd, %region_36.37_spmd} | conditional | flops 1879308288 | bytes 16785424 | solution.py:192
  136.0 30.0 %all-gather.19.cloned.1.call-done = bf16[512,3584]{1,0:T(8,128)(2,1)} async-done(((bf16[128,3584]{1,0:T(8,128)(2,1)}), bf16[512,3584]{1,0:T(8,128)(2,1)}) %all-gather.19.cloned.1.call-update) | async-done | bytes 3670032 | tf_op jit(solution)/shard_map/all_gather | solution.py:78
  166.0 13.5 %conditional.17 = (f32[512,4,128]{0,2,1:T(8,128)}, f32[512,4]{0,1:T(4,128)S(1)}) conditional(s32[]{:T(128)} %convert_element_type.149, (bf16[512,3584]{1,0:T(8,128)(2,1)}, bf16[4,3584,128]{2,1,0:T(8,128)(2,1)}) %tuple.106, () %tuple.107), branch_computations={%region_28.30_spmd, %region_30.31_spmd} | conditional | flops 1879308288 | bytes 16785424 | solution.py:192
  179.5 32.2 %all-gather.23.cloned.1.call-done = bf16[512,3584]{1,0:T(8,128)(2,1)} async-done(((bf16[128,3584]{1,0:T(8,128)(2,1)}), bf16[512,3584]{1,0:T(8,128)(2,1)}) %all-gather.23.cloned.1.call-update) | async-done | bytes 3670032 | tf_op jit(solution)/shard_map/all_gather | solution.py:78
  211.7 11.7 %conditional.19 = (f32[512,4,128]{0,2,1:T(8,128)S(1)}, f32[512,4]{0,1:T(4,128)S(1)}) conditional(s32[]{:T(128)} %convert_element_type.149, (bf16[512,3584]{1,0:T(8,128)(2,1)}, bf16[4,3584,128]{2,1,0:T(8,128)(2,1)}) %tuple.110, () %tuple.111), branch_computations={%region_40.42_spmd, %region_42.43_spmd} | conditional | flops 1879308288 | bytes 16785424 | solution.py:192
  255.3 8.0 %all-to-all-done.6 = f32[16,1536,4]{1,2,0:T(4,128)S(1)} async-done(((f32[16,1536,4]{1,2,0:T(4,128)}), f32[16,1536,4]{1,2,0:T(4,128)S(1)}, u32[]{:S(2)}, u32[]{:S(2)}) %all-to-all-start.6) | async-done | bytes 393248 | tf_op jit(solution)/shard_map/all_to_all | solution.py:30
  264.9 11.1 %all-gather.13.cloned.1.call-done = bf16[512,5120]{1,0:T(8,128)(2,1)} async-done(((bf16[32,5120]{1,0:T(8,128)(2,1)}), bf16[512,5120]{1,0:T(8,128)(2,1)}) %all-gather.13.cloned.1.call-update) | async-done | bytes 5242896 | tf_op jit(solution)/shard_map/all_gather | solution.py:166
  277.1 57.0 %all-gather.15.cloned.1.call-done = bf16[512,5120]{1,0:T(8,128)(2,1)} async-done(((bf16[32,5120]{1,0:T(8,128)(2,1)}), bf16[512,5120]{1,0:T(8,128)(2,1)}) %all-gather.15.cloned.1.call-update) | async-done | bytes 5242896 | tf_op jit(solution)/shard_map/all_gather | solution.py:166
  335.3 57.1 %all-gather.17.cloned.1.call-done = bf16[512,5120]{1,0:T(8,128)(2,1)} async-done(((bf16[32,5120]{1,0:T(8,128)(2,1)}), bf16[512,5120]{1,0:T(8,128)(2,1)}) %all-gather.17.cloned.1.call-update) | async-done | bytes 5242896 | tf_op jit(solution)/shard_map/all_gather | solution.py:166
  396.3 54.3 %all-gather.11.cloned.1.call-done = bf16[512,5120]{1,0:T(8,128)(2,1)} async-done(((bf16[32,5120]{1,0:T(8,128)(2,1)}), bf16[512,5120]{1,0:T(8,128)(2,1)}) %all-gather.11.cloned.1.call-update) | async-done | bytes 5242896 | tf_op jit(solution)/shard_map/all_gather | solution.py:166
  460.8 8.5 %all-to-all-done.4 = f32[16,1024,4]{1,2,0:T(4,128)S(1)} async-done(((f32[16,1024,4]{1,2,0:T(4,128)}), f32[16,1024,4]{1,2,0:T(4,128)S(1)}, u32[]{:S(2)}, u32[]{:S(2)}) %all-to-all-start.4) | async-done | bytes 262176 | tf_op jit(solution)/shard_map/all_to_all | solution.py:30
  475.6 6.7 all-to-all-done.3
  524.1 46.9 %collective-permute-done = bf16[4,512,4,128]{1,3,2,0:T(8,128)(2,1)} collective-permute-done((bf16[4,512,4,128]{1,3,2,0:T(8,128)(2,1)}, bf16[4,512,4,128]{1,3,2,0:T(8,128)(2,1)}, u32[]{:S(2)}, u32[]{:S(2)}) %collective-permute-start) | collective-permute-done | bytes 2097184 | tf_op jit(solution)/shard_map/ppermute | solution.py:85
  580.8 9.7 %conditional.21 = (f32[4,3584,128]{1,2,0:T(8,128)}) conditional(s32[]{:T(128)} %convert_element_type.149, (bf16[512,4,128]{0,2,1:T(8,128)(2,1)}, bf16[512,3584]{1,0:T(8,128)(2,1)}, f32[4,3584,128]{1,2,0:T(8,128)}) %tuple.114, f32[4,3584,128]{1,2,0:T(8,128)} %get-tuple-element.317), branch_computations={%region_47.48_spmd, %region_48.49_spmd} | conditional | flops 1880883200 | bytes 18874376 | solution.py:235
  581.0 9.5 %bitcast_add_fusion = f32[4,3584,128]{1,2,0:T(8,128)} fusion(f32[4,3584,128]{1,2,0:T(8,128)} %get-tuple-element.107, bf16[512,4,128]{0,2,1:T(8,128)(2,1)} %get-tuple-element.108, bf16[512,3584]{1,0:T(8,128)(2,1)} %get-tuple-element.109), kind=kOutput, calls=%fused_computation.10 | convolution fusion | flops 1880883200 | bytes 18874368 | tf_op jit(solution)/shard_map/cond/branch_0_fun/rd,rqc->qdc/dot_general | solution.py:239
  590.5 9.5 %conditional.22 = (f32[4,3584,128]{1,2,0:T(8,128)}) conditional(s32[]{:T(128)} %convert_element_type.149, (bf16[512,4,128]{0,2,1:T(8,128)(2,1)}, bf16[512,3584]{1,0:T(8,128)(2,1)}, f32[4,3584,128]{1,2,0:T(8,128)}) %tuple.115, f32[4,3584,128]{1,2,0:T(8,128)} %get-tuple-element.318), branch_computations={%region_49.50_spmd, %region_50.51_spmd} | conditional | flops 1880883200 | bytes 18874376 | solution.py:235
  590.5 9.5 %bitcast_add_fusion.1 = f32[4,3584,128]{1,2,0:T(8,128)} fusion(f32[4,3584,128]{1,2,0:T(8,128)} %get-tuple-element.110, bf16[512,4,128]{0,2,1:T(8,128)(2,1)} %get-tuple-element.111, bf16[512,3584]{1,0:T(8,128)(2,1)} %get-tuple-element.112), kind=kOutput, calls=%fused_computation.12 | convolution fusion | flops 1880883200 | bytes 18874368 | tf_op jit(solution)/shard_map/cond/branch_0_fun/rd,rqc->qdc/dot_general | solution.py:239
  601.7 9.4 %conditional.23 = (f32[4,3584,128]{1,2,0:T(8,128)}) conditional(s32[]{:T(128)} %convert_element_type.149, (bf16[512,4,128]{0,2,1:T(8,128)(2,1)S(1)}, bf16[512,3584]{1,0:T(8,128)(2,1)}, f32[4,3584,128]{1,2,0:T(8,128)}) %tuple.116, f32[4,3584,128]{1,2,0:T(8,128)} %get-tuple-element.319), branch_computations={%region_51.52_spmd, %region_52.53_spmd} | conditional | flops 1880883200 | bytes 18874376 | solution.py:235
  601.7 9.4 %bitcast_add_fusion.2 = f32[4,3584,128]{1,2,0:T(8,128)} fusion(f32[4,3584,128]{1,2,0:T(8,128)} %get-tuple-element.113, bf16[512,4,128]{0,2,1:T(8,128)(2,1)S(1)} %get-tuple-element.114, bf16[512,3584]{1,0:T(8,128)(2,1)} %get-tuple-element.115), kind=kOutput, calls=%fused_computation.14 | convolution fusion | flops 1880883200 | bytes 18874368 | tf_op jit(solution)/shard_map/cond/branch_0_fun/rd,rqc->qdc/dot_general | solution.py:239
  611.1 8.4 %copy.52 = f32[4,3584,128]{2,1,0:T(8,128)} copy(f32[4,3584,128]{1,2,0:T(8,128)} %get-tuple-element.320) | data formatting | bytes 14680064 | tf_op jit(solution)/shard_map/cond | solution.py:235
  621.0 6.9 all-to-all-start.14
  628.8 6.7 all-to-all-done.14
  639.8 6.7 all-to-all-done.12
  678.0 6.7 all-to-all-done.15
  688.9 6.7 all-to-all-done.13
  699.9 6.7 all-to-all-done.11
  (325 shorter events, 242.7 us)
Async XLA Ops:
  7.2 99.6 %all-gather.9.cloned.1.call-start = ((), (), s32[]{:S(2)}) async-start(), calls=%async_computation.17 | async-start | bytes 4587520 | tf_op jit(solution)/shard_map/all_gather | solution.py:78
  26.4 46.2 %copy-start.3 = (bf16[1,128,5120]{2,1,0:T(8,128)(2,1)S(1)}, bf16[1,128,5120]{2,1,0:T(8,128)(2,1)}, u32[]{:S(2)}) copy-start(bf16[1,128,5120]{2,1,0:T(8,128)(2,1)} %param.32) | copy-start | bytes 3932164
  26.4 97.7 %all-gather.21.cloned.1.call-start = ((), (), s32[]{:S(2)}) async-start(), calls=%async_computation.23 | async-start | bytes 4587520 | tf_op jit(solution)/shard_map/all_gather | solution.py:78
  26.5 46.5 %copy-start.36 = (f32[5120]{0:T(1024)S(1)}, f32[5120]{0:T(1024)}, u32[]{:S(2)}) copy-start(f32[5120]{0:T(1024)} %param.34) | copy-start | bytes 61444
  43.1 122.9 %all-gather.19.cloned.1.call-start = ((), (), s32[]{:S(2)}) async-start(), calls=%async_computation.22 | async-start | bytes 4587520 | tf_op jit(solution)/shard_map/all_gather | solution.py:78
  58.1 153.6 %all-gather.23.cloned.1.call-start = ((), (), s32[]{:S(2)}) async-start(), calls=%async_computation.24 | async-start | bytes 4587520 | tf_op jit(solution)/shard_map/all_gather | solution.py:78
  72.5 203.5 %all-gather.13.cloned.1.call-start = ((), (), s32[]{:S(2)}) async-start(), calls=%async_computation.19 | async-start | bytes 5570560 | tf_op jit(solution)/shard_map/all_gather | solution.py:166
  74.4 259.7 %all-gather.15.cloned.1.call-start = ((), (), s32[]{:S(2)}) async-start(), calls=%async_computation.20 | async-start | bytes 5570560 | tf_op jit(solution)/shard_map/all_gather | solution.py:166
  75.0 317.4 %all-gather.17.cloned.1.call-start = ((), (), s32[]{:S(2)}) async-start(), calls=%async_computation.21 | async-start | bytes 5570560 | tf_op jit(solution)/shard_map/all_gather | solution.py:166
  75.7 374.9 %all-gather.11.cloned.1.call-start = ((), (), s32[]{:S(2)}) async-start(), calls=%async_computation.18 | async-start | bytes 5570560 | tf_op jit(solution)/shard_map/all_gather | solution.py:166
  119.2 108.2 %all-to-all-start = ((f32[16,1536,4]{1,2,0:T(4,128)}), f32[16,1536,4]{1,2,0:T(4,128)S(1)}, u32[]{:S(2)}, u32[]{:S(2)}) async-start(f32[16,1536,4]{1,2,0:T(4,128)} %broadcast_in_dim.25), calls=%async_computation | async-start | bytes 786432 | tf_op jit(solution)/shard_map/all_to_all | solution.py:30
  229.0 15.9 %all-to-all-start.7 = ((f32[16,1536,4]{1,2,0:T(4,128)}), f32[16,1536,4]{1,2,0:T(4,128)}, u32[]{:S(2)}, u32[]{:S(2)}) async-start(f32[16,1536,4]{1,2,0:T(4,128)} %broadcast_in_dim.32), calls=%async_computation.7 | async-start | bytes 786432 | tf_op jit(solution)/shard_map/all_to_all | solution.py:30
  246.4 17.0 %all-to-all-start.6 = ((f32[16,1536,4]{1,2,0:T(4,128)}), f32[16,1536,4]{1,2,0:T(4,128)S(1)}, u32[]{:S(2)}, u32[]{:S(2)}) async-start(f32[16,1536,4]{1,2,0:T(4,128)} %broadcast_in_dim.31), calls=%async_computation.6 | async-start | bytes 786432 | tf_op jit(solution)/shard_map/all_to_all | solution.py:30
  455.5 13.8 %all-to-all-start.4 = ((f32[16,1024,4]{1,2,0:T(4,128)}), f32[16,1024,4]{1,2,0:T(4,128)S(1)}, u32[]{:S(2)}, u32[]{:S(2)}) async-start(f32[16,1024,4]{1,2,0:T(4,128)} %broadcast_in_dim.29), calls=%async_computation.4 | async-start | bytes 524288 | tf_op jit(solution)/shard_map/all_to_all | solution.py:30
  470.1 12.2 %all-to-all-start.3 = ((f32[16,1024,4]{1,2,0:T(4,128)}), f32[16,1024,4]{1,2,0:T(4,128)S(1)}, u32[]{:S(2)}, u32[]{:S(2)}) async-start(f32[16,1024,4]{1,2,0:T(4,128)} %broadcast_in_dim.28), calls=%async_computation.3 | async-start | bytes 524288 | tf_op jit(solution)/shard_map/all_to_all | solution.py:30
  483.1 12.1 %all-to-all-start.2 = ((f32[16,1024,4]{1,2,0:T(4,128)}), f32[16,1024,4]{1,2,0:T(4,128)S(1)}, u32[]{:S(2)}, u32[]{:S(2)}) async-start(f32[16,1024,4]{1,2,0:T(4,128)} %broadcast_in_dim.27), calls=%async_computation.2 | async-start | bytes 524288 | tf_op jit(solution)/shard_map/all_to_all | solution.py:30
  496.1 12.1 %all-to-all-start.1 = ((f32[16,1024,4]{1,2,0:T(4,128)}), f32[16,1024,4]{1,2,0:T(4,128)S(1)}, u32[]{:S(2)}, u32[]{:S(2)}) async-start(f32[16,1024,4]{1,2,0:T(4,128)} %broadcast_in_dim.26), calls=%async_computation.1 | async-start | bytes 524288 | tf_op jit(solution)/shard_map/all_to_all | solution.py:30
  509.1 14.7 %all-to-all-start.5 = ((f32[16,1536,4]{1,2,0:T(4,128)}), f32[16,1536,4]{1,2,0:T(4,128)S(1)}, u32[]{:S(2)}, u32[]{:S(2)}) async-start(f32[16,1536,4]{1,2,0:T(4,128)} %broadcast_in_dim.30), calls=%async_computation.5 | async-start | bytes 786432 | tf_op jit(solution)/shard_map/all_to_all | solution.py:30
  514.6 204.4 %reduce-scatter.2.cloned.1.call-start = ((), (), s32[]{:S(2)}) async-start(), calls=%async_computation.25 | async-start | bytes 8257536 | tf_op jit(solution)/shard_map/reduce_scatter | solution.py:246
  519.9 51.2 %collective-permute-start = (bf16[4,512,4,128]{1,3,2,0:T(8,128)(2,1)}, bf16[4,512,4,128]{1,3,2,0:T(8,128)(2,1)}, u32[]{:S(2)}, u32[]{:S(2)}) collective-permute-start(bf16[4,512,4,128]{1,3,2,0:T(8,128)(2,1)} %pad_maximum_fusion), channel_id=1, source_target_pairs={{0,64},{1,65},{2,66},{3,67},{4,68},{5,69},{6,70},{7,71},{8,72},{9,... | collective-permute-start | bytes 6291464 | tf_op jit(solution)/shard_map/ppermute | solution.py:85
  523.9 51.8 %copy-start.4 = (bf16[512,3584]{1,0:T(8,128)(2,1)S(1)}, bf16[512,3584]{1,0:T(8,128)(2,1)}, u32[]{:S(2)}) copy-start(bf16[512,3584]{1,0:T(8,128)(2,1)} %all-gather.23.cloned.1.call-done) | copy-start | bytes 11010052
  619.5 49.6 %copy-start.18 = (s32[512,4]{0,1:T(4,128)S(1)}, s32[512,4]{0,1:T(4,128)}, u32[]{:S(2)}) copy-start(s32[512,4]{0,1:T(4,128)} %eq.56) | copy-start | bytes 24580
  619.5 49.5 %copy-start.20 = (s32[512,4]{0,1:T(4,128)S(1)}, s32[512,4]{0,1:T(4,128)}, u32[]{:S(2)}) copy-start(s32[512,4]{0,1:T(4,128)} %eq.52) | copy-start | bytes 24580
  619.5 49.5 %copy-start.24 = (f32[512,4]{0,1:T(4,128)S(1)}, f32[512,4]{0,1:T(4,128)}, u32[]{:S(2)}) copy-start(f32[512,4]{0,1:T(4,128)} %get-tuple-element.281) | copy-start | bytes 24580
  621.0 14.5 %all-to-all-start.14 = ((f32[16,1,128]{2,1,0:T(1,128)}), f32[16,1,128]{2,1,0:T(1,128)S(1)}, u32[]{:S(2)}, u32[]{:S(2)}) async-start(f32[16,1,128]{2,1,0:T(1,128)} %reshape.455), calls=%async_computation.15 | async-start | bytes 16384 | tf_op jit(solution)/shard_map/all_to_all | solution.py:71
  635.5 10.9 %all-to-all-start.12 = ((f32[16,1,128]{2,1,0:T(1,128)}), f32[16,1,128]{2,1,0:T(1,128)S(1)}, u32[]{:S(2)}, u32[]{:S(2)}) async-start(f32[16,1,128]{2,1,0:T(1,128)} %reshape.459), calls=%async_computation.13 | async-start | bytes 16384 | tf_op jit(solution)/shard_map/all_to_all | solution.py:71
  646.4 10.8 %all-to-all-start.10 = ((f32[16,1,128]{2,1,0:T(1,128)}), f32[16,1,128]{2,1,0:T(1,128)S(1)}, u32[]{:S(2)}, u32[]{:S(2)}) async-start(f32[16,1,128]{2,1,0:T(1,128)} %reshape.463), calls=%async_computation.11 | async-start | bytes 16384 | tf_op jit(solution)/shard_map/all_to_all | solution.py:71
  657.3 10.9 %all-to-all-start.8 = ((f32[16,1,128]{2,1,0:T(1,128)}), f32[16,1,128]{2,1,0:T(1,128)S(1)}, u32[]{:S(2)}, u32[]{:S(2)}) async-start(f32[16,1,128]{2,1,0:T(1,128)} %reshape.467), calls=%async_computation.9 | async-start | bytes 16384 | tf_op jit(solution)/shard_map/all_to_all | solution.py:71
  673.7 11.0 %all-to-all-start.15 = ((f32[16,1,128]{2,1,0:T(1,128)}), f32[16,1,128]{2,1,0:T(1,128)S(1)}, u32[]{:S(2)}, u32[]{:S(2)}) async-start(f32[16,1,128]{2,1,0:T(1,128)} %reshape.457), calls=%async_computation.16 | async-start | bytes 16384 | tf_op jit(solution)/shard_map/all_to_all | solution.py:71
  684.7 10.9 %all-to-all-start.13 = ((f32[16,1,128]{2,1,0:T(1,128)}), f32[16,1,128]{2,1,0:T(1,128)S(1)}, u32[]{:S(2)}, u32[]{:S(2)}) async-start(f32[16,1,128]{2,1,0:T(1,128)} %reshape.461), calls=%async_computation.14 | async-start | bytes 16384 | tf_op jit(solution)/shard_map/all_to_all | solution.py:71
  695.6 11.0 %all-to-all-start.11 = ((f32[16,1,128]{2,1,0:T(1,128)}), f32[16,1,128]{2,1,0:T(1,128)S(1)}, u32[]{:S(2)}, u32[]{:S(2)}) async-start(f32[16,1,128]{2,1,0:T(1,128)} %reshape.465), calls=%async_computation.12 | async-start | bytes 16384 | tf_op jit(solution)/shard_map/all_to_all | solution.py:71
  706.6 10.9 %all-to-all-start.9 = ((f32[16,1,128]{2,1,0:T(1,128)}), f32[16,1,128]{2,1,0:T(1,128)S(1)}, u32[]{:S(2)}, u32[]{:S(2)}) async-start(f32[16,1,128]{2,1,0:T(1,128)} %reshape.469), calls=%async_computation.10 | async-start | bytes 16384 | tf_op jit(solution)/shard_map/all_to_all | solution.py:71
  (34 other events, 349.2 us)
Sparse Core Ops, SparseCore 0:
  26.5 45.5 all-gather.8
  73.8 46.2 all-gather.20
  121.8 44.1 all-gather.18
  167.5 44.1 all-gather.22
  213.7 62.2 all-gather.12
  278.0 56.0 all-gather.14
  336.3 56.0 all-gather.16
  394.6 56.0 all-gather.10
  619.7 46.5 reduce-scatter.1
where the time goes:
time: 736 us; the launch traced here: 726 us
  waiting for transfers between devices  378 us (51%)
  blocking collectives  85.7 us (12%)
  starting transfers between devices  69.3 us (9%)
  local copies, waits for them, and re-layouts  65.5 us (9%)
  matrix products  56.1 us (8%)
  other arithmetic  54.6 us (7%)
  between operations  15.2 us (2%)
    all_gather x4, waiting for transfers between devices, on_device(): lax.all_gather(teacher_local_rows, CTX, axis=0, tiled=True)  180 us
    all_gather x4, waiting for transfers between devices, whole_of(): filled = lax.all_gather(filled, axes[number], axis=dim, tiled=True)  62.2 us
    all_gather x4, blocking collectives, whole_of(): filled = lax.all_gather(filled, axes[number], axis=dim, tiled=True)  61.8 us
    all_to_all x8, waiting for transfers between devices, sum_at_owner(): lax.all_to_all(cut_along(array, dim, length), axis, 0, 0, tiled=True)  49.9 us
    ppermute x1, waiting for transfers between devices, shifted(): lax.ppermute(value, axis, [(source, source + steps) for source in range(i...  46.9 us
    all_to_all x8, waiting for transfers between devices, copy_for_each(): return lax.all_to_all(copies, axis, split_axis=0, concat_axis=0, tiled=True)  37.9 us
    all_to_all x8, starting transfers between devices, copy_for_each(): return lax.all_to_all(copies, axis, split_axis=0, concat_axis=0, tiled=True)  36.6 us
    dot_general x4, matrix products, on_device(): jnp.einsum('rd,rqc->qdc', gathered, gradient_scaling, preferred_element_t...  33.5 us
  transfers between devices with their start and end apart: 26, of which 22 were waited for; matrix products, arithmetic and copies ran while one was open for 16% of the time, Pallas kernels for 0%

commit v1 on v0

v1 whole, which is shorter than its diff:
```python
import jax
import jax.numpy as jnp
from jax import lax
from jax.sharding import Mesh
from jax.sharding import PartitionSpec as P

BOOKS = 4
SIDE = 4
CTX = ("cx", "cz")
COLUMN = ("role", "ylo")
TURN = ("core", "cx", "cz")

epsilon = 1e-06
sharpness_divisor = 2.0
blend_ratio = 0.5


def line_pairs(phase, step):
    pairs = []
    for core in range(2):
        for x in range(SIDE):
            for z in range(SIDE):
                along_x = (core + phase) % 2 == 0
                to_x = (x + step) % SIDE if along_x else x
                to_z = z if along_x else (z + step) % SIDE
                pairs.append(
                    ((core * SIDE + x) * SIDE + z, (core * SIDE + to_x) * SIDE + to_z)
                )
    return pairs


def moved(value, phase, step):
    return lax.ppermute(value, TURN, line_pairs(phase, step))


def line_blocks(block, phase, way):
    after = moved(block, phase, -1)
    before = moved(block, phase, 1)
    opposite = moved(after, phase, -1) if way > 0 else moved(before, phase, 1)
    return [block, after, opposite, before]


def normalize(states, gain):
    values = states.astype(jnp.float32)
    factor = lax.rsqrt(jnp.mean(values * values, axis=-1, keepdims=True) + epsilon)
    return (values * factor * gain).astype(jnp.bfloat16)


def turned(array, shift, axis):
    double = jnp.concatenate([array, array], axis=axis)
    return lax.dynamic_slice_in_dim(double, shift, array.shape[axis], axis=axis)


def by_place(array, dim):
    mx, mz, core = (lax.axis_index(name) for name in ("cx", "cz", "core"))
    shape = array.shape
    grid = array.reshape(*shape[:dim], SIDE, SIDE, *shape[dim + 1 :])
    grid = turned(turned(grid, mx, dim), mz, dim + 1)
    grid = jnp.where(core == 0, jnp.swapaxes(grid, dim, dim + 1), grid)
    return grid.reshape(shape)


def by_block(array, dim):
    mx, mz, core = (lax.axis_index(name) for name in ("cx", "cz", "core"))
    shape = array.shape
    grid = array.reshape(*shape[:dim], SIDE, SIDE, *shape[dim + 1 :])
    grid = jnp.where(core == 0, jnp.swapaxes(grid, dim, dim + 1), grid)
    grid = turned(turned(grid, (SIDE - mx) % SIDE, dim), (SIDE - mz) % SIDE, dim + 1)
    return grid.reshape(shape)


def copy_for_each(array, axis):
    copies = jnp.broadcast_to(array, (lax.axis_size(axis), *array.shape))
    return lax.all_to_all(copies, axis, split_axis=0, concat_axis=0, tiled=True)


def log_sum(values, axis):
    peak = jnp.max(values, axis=axis, keepdims=True)
    total = jnp.sum(jnp.exp(values - peak), axis=axis, keepdims=True)
    return jnp.squeeze(peak + jnp.log(total), axis)


def on_device(
    teacher_states,
    student_states,
    teacher_gain,
    student_gain,
    mentor_output_weights,
    student_heads,
    segments,
    targets,
):
    columns = student_heads.shape[2]
    features = student_heads.shape[1]
    count = lax.axis_size(CTX)
    role = lax.axis_index("role")
    core = lax.axis_index("core")
    rows_here = teacher_states.shape[1]
    half = rows_here // 2
    length = rows_here * count

    def own_half(states):
        return lax.dynamic_slice_in_dim(states[0], role * half, half, axis=0)

    teacher_rows = normalize(own_half(teacher_states), teacher_gain)
    student_rows = normalize(own_half(student_states), student_gain)

    student_line = jnp.concatenate(line_blocks(student_rows, 0, -1))
    teacher_line = jnp.concatenate(line_blocks(teacher_rows, 0, -1))
    student_parts = line_blocks(student_line, 1, -1)
    teacher_parts = line_blocks(teacher_line, 1, 1)

    info = jnp.concatenate([segments[0][:, None], targets[0]], axis=1)
    info = copy_for_each(info.T, CTX)
    all_segments = info[:, 0].reshape(-1)
    documents = 2 * count
    members = all_segments[:, None] == jnp.arange(documents, dtype=jnp.int32)[None, :]
    members = members.astype(jnp.float32)
    counts = jnp.sum(members, axis=0)
    row_sizes = jnp.sum(members * counts[None, :], axis=1)
    row_weights = length / (documents * row_sizes)

    def half_rows(array):
        pieces = lax.dynamic_slice_in_dim(array, role * half, half, axis=array.ndim - 1)
        return pieces

    weights = by_place(half_rows(row_weights.reshape(count, rows_here)), 0).reshape(-1)
    own_targets = by_place(half_rows(info[:, 1:]), 0)
    own_targets = jnp.moveaxis(own_targets, 1, 0).reshape(BOOKS, -1)
    own_targets = own_targets - lax.axis_index(CTX) * columns
    hits = jnp.arange(columns)[None, None, :] == own_targets[:, :, None]

    def project(rows, heads):
        return jnp.einsum("rd,qdc->qrc", rows, heads, preferred_element_type=jnp.float32)

    teacher_scaled = []
    student_raw = []
    local = []
    for turn in range(SIDE):
        scaled = project(teacher_parts[turn], mentor_output_weights) / sharpness_divisor
        raw = project(student_parts[turn], student_heads)
        teacher_scaled.append(scaled)
        student_raw.append(raw)
        local.append(
            jnp.stack(
                [log_sum(scaled, 2), log_sum(raw, 2), log_sum(raw / sharpness_divisor, 2)]
            )
        )
    scaled = jnp.concatenate(teacher_scaled, axis=1)
    raw = jnp.concatenate(student_raw, axis=1)
    local = jnp.concatenate(local, axis=2)
    sent = by_block(local.reshape(3, BOOKS, count, half), 2)
    whole = log_sum(copy_for_each(sent, CTX), 0)
    whole = by_place(whole, 2).reshape(3, BOOKS, -1)

    teacher_logp = scaled - whole[0][:, :, None]
    plain_logp = raw - whole[1][:, :, None]
    tempered_logp = raw / sharpness_divisor - whole[2][:, :, None]
    teacher_terms = -jnp.sum(jnp.where(hits, teacher_logp, 0.0), axis=2)
    teacher_sent = lax.reduce_precision(teacher_logp, 8, 7)
    teacher_share = jnp.exp(teacher_sent)
    gap = jnp.sum(teacher_share * (teacher_sent - tempered_logp), axis=2)
    mismatch = -jnp.sum(jnp.where(hits, plain_logp, 0.0), axis=2)
    losses = (
        blend_ratio * sharpness_divisor * sharpness_divisor * gap + (1.0 - blend_ratio) * mismatch
    )
    slope = weights[None, :, None] * (
        blend_ratio * sharpness_divisor * (jnp.exp(tempered_logp) - teacher_share)
        + (1.0 - blend_ratio) * (jnp.exp(plain_logp) - hits.astype(jnp.float32))
    )
    slope = slope.astype(jnp.bfloat16)
    student_all = jnp.concatenate(student_parts)
    gradient = jnp.einsum("rd,qrc->qdc", student_all, slope, preferred_element_type=jnp.float32)

    owners = lax.axis_size(COLUMN)
    gradient = gradient.reshape(BOOKS, owners, 2, features // (2 * owners), columns)
    kept = lax.dynamic_index_in_dim(gradient, core, 2, keepdims=False)
    given = lax.dynamic_index_in_dim(gradient, 1 - core, 2, keepdims=False)
    taken = lax.ppermute(given.astype(jnp.bfloat16), "core", [(0, 1), (1, 0)])
    pair = kept + taken.astype(jnp.float32)
    pieces = jnp.moveaxis(pair, 1, 0).astype(jnp.bfloat16)
    pieces = lax.all_to_all(pieces, COLUMN, 0, 0, tiled=True)
    shares = jnp.sum(pieces.astype(jnp.float32), axis=0)

    terms = jnp.stack([teacher_terms, losses]).reshape(2, BOOKS, count, half)
    terms = jnp.moveaxis(by_block(terms, 2), 2, 1)
    terms = lax.all_to_all(
        terms.reshape(2 * count, BOOKS, half), ("role", *CTX), 0, 0, tiled=True
    )
    terms = jnp.sum(terms.reshape(2, count, BOOKS, half), axis=1)
    frame_terms = jnp.moveaxis(terms, 1, 2).reshape(1, 1, rows_here, BOOKS)
    return (shares, frame_terms)


def solution(mesh):
    finer = Mesh(
        mesh.devices.reshape(2, 2, 2, SIDE, SIDE),
        ("role", "ylo", "core", "cx", "cz"),
    )
    dp = ("ylo", "core")
    placed = (
        P(dp, CTX, None),
        P(dp, CTX, None),
        P(),
        P(),
        P(None, None, CTX),
        P(None, None, CTX),
        P(dp, CTX),
        P(dp, CTX, None),
    )
    return jax.shard_map(
        on_device,
        mesh=finer,
        in_specs=placed,
        out_specs=(P(None, ("role", *dp), CTX), P("role", dp, CTX, None)),
        check_vma=False,
    )
```

time: 736 us -> 231 us (0.31); the launches traced: 726 us -> 228 us
  waiting for transfers between devices: 378 us -> 89.6 us
  blocking collectives: 85.7 us -> 0 us
  matrix products: 56.1 us -> 23.6 us
  other arithmetic: 54.6 us -> 23.3 us
  starting transfers between devices: 69.3 us -> 46.4 us
  local copies, waits for them, and re-layouts: 65.5 us -> 44.3 us
  between operations: 15.2 us -> 1.18 us
    all_gather x8 -> x0, waiting for transfers between devices: 242 us -> none  [the longest x4 180 us: on_device(): lax.all_gather(teacher_local_rows, CTX, axis=0, tiled=True)]
    all_gather x5 -> x0, blocking collectives: 85.7 us -> none  [the longest x4 61.8 us: whole_of(): filled = lax.all_gather(filled, axes[number], axis=dim, tiled=True)]
    all_to_all x8 -> x2, waiting for transfers between devices: 37.9 us -> 7.68 us  [copy_for_each(): return lax.all_to_all(copies, axis, split_axis=0, concat_axis=0, tiled=True)]
    all_to_all x8 -> x2, waiting for transfers between devices: 49.9 us -> 22.1 us  [the longest x1 19.4 us: on_device(): pieces = lax.all_to_all(pieces, COLUMN, 0, 0, tiled=True)]
    another operation x8 -> x2, local copies, waits for them, and re-layouts: 26.3 us -> 0.12 us  [the longest x1 0.11 us: by_block(): grid = array.reshape(*shape[:dim], SIDE, SIDE, *shape[dim + 1:])]
    all_to_all x8 -> x2, starting transfers between devices: 36.6 us -> 11.7 us  [copy_for_each(): return lax.all_to_all(copies, axis, split_axis=0, concat_axis=0, tiled=True)]
    cond x4 -> x0, matrix products: 22.5 us -> none
    dot_general x5 -> x1, matrix products: 33.6 us -> 11.6 us  [on_device(): jnp.einsum('rd,qrc->qdc', student_all, slope, preferred_element_type=jnp....]
  transfers between devices with their start and end apart: 26 -> 17, of which waited for: 22 -> 9; matrix products, arithmetic and copies ran while one was open for 16% -> 22% of each run, Pallas kernels for 0% -> 0%
where the time goes in v1:
time: 231 us; the launch traced here: 228 us
  waiting for transfers between devices  89.6 us (39%)
  starting transfers between devices  46.4 us (20%)
  local copies, waits for them, and re-layouts  44.3 us (19%)
  matrix products  23.6 us (10%)
  other arithmetic  23.3 us (10%)
    ppermute x12, waiting for transfers between devices, moved(): return lax.ppermute(value, TURN, line_pairs(phase, step))  59.8 us
    unnamed x37, local copies, waits for them, and re-layouts  24.9 us
    ppermute x12, starting transfers between devices, moved(): return lax.ppermute(value, TURN, line_pairs(phase, step))  21.7 us
    all_to_all x1, waiting for transfers between devices, on_device(): pieces = lax.all_to_all(pieces, COLUMN, 0, 0, tiled=True)  19.4 us
    unnamed x8, matrix products  11.9 us
    all_to_all x2, starting transfers between devices, copy_for_each(): return lax.all_to_all(copies, axis, split_axis=0, concat_axis=0, tiled=True)  11.7 us
    dot_general x1, matrix products, on_device(): jnp.einsum('rd,qrc->qdc', student_all, slope, preferred_element_type=jnp....  11.6 us
    transpose x1, local copies, waits for them, and re-layouts, on_device(): jnp.einsum('rd,qrc->qdc', student_all, slope, preferred_element_type=jnp....  8.41 us
  transfers between devices with their start and end apart: 17, of which 9 were waited for; matrix products, arithmetic and copies ran while one was open for 22% of the time, Pallas kernels for 0%

profile of v1, /device:TPU:24, one launch (start us, length us, event | category | flops | bytes accessed | tf_op | source)
XLA Modules:
  0.0 228.3 jit_solution(11851880950675775141)
XLA Ops:
  3.4 1.6 collective-permute-start.7
  5.0 1.7 collective-permute-start.6
  8.0 6.7 %all-to-all-start = ((s32[16,5,128]{2,1,0:T(8,128)}), s32[16,5,128]{2,1,0:T(8,128)S(1)}, u32[]{:S(2)}, u32[]{:S(2)}) async-start(s32[16,5,128]{2,1,0:T(8,128)} %broadcast_in_dim.8), calls=%async_computation | async-start | bytes 131072 | tf_op jit(solution)/shard_map/all_to_all | solution.py:74
  15.9 1.9 collective-permute-start.1
  19.1 5.9 %copy.107 = bf16[4,3584,128]{1,2,0:T(8,128)(2,1)} copy(bf16[4,3584,128]{2,1,0:T(8,128)(2,1)} %param.13) | data formatting | bytes 7340032 | tf_op args[5]
  25.0 7.9 %copy.111 = bf16[4,5120,128]{1,2,0:T(8,128)(2,1)} copy(bf16[4,5120,128]{2,1,0:T(8,128)(2,1)} %param.12) | data formatting | bytes 10485760 | tf_op args[4]
  36.8 6.7 %collective-permute-done.2 = bf16[64,3584]{1,0:T(8,128)(2,1)S(1)} collective-permute-done((bf16[64,3584]{1,0:T(8,128)(2,1)S(1)}, bf16[64,3584]{1,0:T(8,128)(2,1)S(1)}, u32[]{:S(2)}, u32[]{:S(2)}) %collective-permute-start.2) | collective-permute-done | bytes 458784 | tf_op jit(solution)/shard_map/ppermute | solution.py:33
  43.6 3.2 %collective-permute-start.3 = (bf16[256,3584]{1,0:T(8,128)(2,1)S(1)}, bf16[256,3584]{1,0:T(8,128)(2,1)S(1)}, u32[]{:S(2)}, u32[]{:S(2)}) collective-permute-start(bf16[256,3584]{1,0:T(8,128)(2,1)S(1)} %pad_maximum_fusion.2), channel_id=1, source_target_pairs={{0,3},{1,0},{2,1},{3,2},{4,7},{5,4},{6,5},{7,6},{8,11},{9,8},{10,9... | collective-permute-start | bytes 5505032 | tf_op jit(solution)/shard_map/ppermute | solution.py:33
  49.9 3.7 %collective-permute-done.8 = bf16[64,5120]{1,0:T(8,128)(2,1)S(1)} collective-permute-done((bf16[64,5120]{1,0:T(8,128)(2,1)S(1)}, bf16[64,5120]{1,0:T(8,128)(2,1)S(1)}, u32[]{:S(2)}, u32[]{:S(2)}) %collective-permute-start.8) | collective-permute-done | bytes 655392 | tf_op jit(solution)/shard_map/ppermute | solution.py:33
  55.0 5.8 %collective-permute-start.9 = (bf16[256,5120]{1,0:T(8,128)(2,1)S(1)}, bf16[256,5120]{1,0:T(8,128)(2,1)S(1)}, u32[]{:S(2)}, u32[]{:S(2)}) collective-permute-start(bf16[256,5120]{1,0:T(8,128)(2,1)S(1)} %pad_maximum_fusion), channel_id=1, source_target_pairs={{0,3},{1,0},{2,1},{3,2},{4,7},{5,4},{6,5},{7,6},{8,11},{9,8},{10,9... | collective-permute-start | bytes 7864328 | tf_op jit(solution)/shard_map/ppermute | solution.py:33
  60.8 2.6 %fusion.38 = f32[256,512]{0,1:S(1)} fusion(bf16[5120,512]{0,1:T(8,128)(2,1)S(1)} %bitcast.181, bf16[64,5120]{1,0:T(8,128)(2,1)S(1)} %collective-permute-done.7, bf16[64,5120]{1,0:T(8,128)(2,1)S(1)} %collective-permute-done.8, bf16[64,5120]{1,0:T(8,128)(2,1)} %collective-permute-done.6, bf16[64,5120]{1,0:T(8,128)(2,1)S(1)} %fusion.10), kind=kOutput, calls=%fused_computation.137 | convolution fusion | flops 1352663040 | bytes 8388608
  64.3 7.0 %collective-permute-done.4 = bf16[256,3584]{1,0:T(8,128)(2,1)S(1)} collective-permute-done((bf16[256,3584]{1,0:T(8,128)(2,1)S(1)}, bf16[256,3584]{1,0:T(8,128)(2,1)S(1)}, u32[]{:S(2)}, u32[]{:S(2)}) %collective-permute-start.4) | collective-permute-done | bytes 1835040 | tf_op jit(solution)/shard_map/ppermute | solution.py:33
  75.5 20.2 %collective-permute-done.9 = bf16[256,5120]{1,0:T(8,128)(2,1)S(1)} collective-permute-done((bf16[256,5120]{1,0:T(8,128)(2,1)S(1)}, bf16[256,5120]{1,0:T(8,128)(2,1)S(1)}, u32[]{:S(2)}, u32[]{:S(2)}) %collective-permute-start.9) | collective-permute-done | bytes 2621472 | tf_op jit(solution)/shard_map/ppermute | solution.py:33
  97.3 3.9 %collective-permute-start.10 = (bf16[256,5120]{1,0:T(8,128)(2,1)S(1)}, bf16[256,5120]{1,0:T(8,128)(2,1)S(1)}, u32[]{:S(2)}, u32[]{:S(2)}) collective-permute-start(bf16[256,5120]{1,0:T(8,128)(2,1)S(1)} %collective-permute-done.9), channel_id=1, source_target_pairs={{0,3},{1,0},{2,1},{3,2},{4,7},{5,4},{6,5},{7,6},{8,11},{9,8},{10,9... | collective-permute-start | bytes 7864328 | tf_op jit(solution)/shard_map/ppermute | solution.py:33
  104.8 14.3 %collective-permute-done.5 = bf16[256,3584]{1,0:T(8,128)(2,1)S(1)} collective-permute-done((bf16[256,3584]{1,0:T(8,128)(2,1)S(1)}, bf16[256,3584]{1,0:T(8,128)(2,1)S(1)}, u32[]{:S(2)}, u32[]{:S(2)}) %collective-permute-start.5) | collective-permute-done | bytes 1835040 | tf_op jit(solution)/shard_map/ppermute | solution.py:33
  122.5 8.0 %collective-permute-done.10 = bf16[256,5120]{1,0:T(8,128)(2,1)S(1)} collective-permute-done((bf16[256,5120]{1,0:T(8,128)(2,1)S(1)}, bf16[256,5120]{1,0:T(8,128)(2,1)S(1)}, u32[]{:S(2)}, u32[]{:S(2)}) %collective-permute-start.10) | collective-permute-done | bytes 2621472 | tf_op jit(solution)/shard_map/ppermute | solution.py:33
  130.4 1.6 fusion.42
  133.6 1.9 reshape.418
  135.5 5.1 %all-to-all-start.1 = ((f32[16,1,12288]{2,1,0:T(1,128)}), f32[16,1,12288]{2,1,0:T(1,128)S(1)}, u32[]{:S(2)}, u32[]{:S(2)}) async-start(f32[16,1,12288]{2,1,0:T(1,128)} %reshape.418), calls=%async_computation.1 | async-start | bytes 1572864 | tf_op jit(solution)/shard_map/all_to_all | solution.py:74
  140.6 3.0 %constant_dynamic-update-slice_fusion = bf16[1024,3584]{1,0:T(8,128)(2,1)} fusion(bf16[1024,3584]{1,0:T(8,128)(2,1)} %constant_dynamic-update-slice_fusion.1, bf16[256,3584]{1,0:T(8,128)(2,1)} %copy-done.7), kind=kLoop, calls=%fused_computation.90 | loop fusion | bytes 3670016 | tf_op jit(solution)/shard_map/concatenate | solution.py:172
  144.4 7.7 %all-to-all-done.1 = f32[16,1,12288]{2,1,0:T(1,128)S(1)} async-done(((f32[16,1,12288]{2,1,0:T(1,128)}), f32[16,1,12288]{2,1,0:T(1,128)S(1)}, u32[]{:S(2)}, u32[]{:S(2)}) %all-to-all-start.1) | async-done | bytes 786464 | tf_op jit(solution)/shard_map/all_to_all | solution.py:74
  152.6 3.6 %reduce = f32[16,12288]{1,0:T(8,128)} reduce(f32[16,1,12288]{2,1,0:T(1,128)S(1)} %all-to-all-done.1, f32[]{:T(128)} %broadcast.136), dimensions={1}, to_apply=%all_to_all.13.reduce_sub_computation | reduce | bytes 1572868 | tf_op jit(solution)/shard_map/all_to_all | solution.py:74
  156.2 1.8 reshape.419
  158.9 11.6 %fusion.2 = f32[4,3584,128]{1,2,0:T(8,128)} fusion(bf16[1024,3584]{1,0:T(8,128)(2,1)} %constant_dynamic-update-slice_fusion, s32[4,1024]{1,0:T(4,128)S(1)} %sub.215, f32[4,1024]{1,0:T(4,128)S(1)} %sub.208, f32[4,1024]{1,0:T(4,128)S(1)} %sub.201, f32[1024]{0:T(1024)S(1)} %mul.118, f32[4,256,128]{1,2,0:T(8,128)S(1)} %bitcast.189, ...), kind=kOutput, calls=%fused_computation.2 | convolution fusion | flops 3768057856 | bytes 18944000 | tf_op jit(solution)/shard_map/rd,qrc->qdc/dot_general | solution.py:173
  170.5 8.4 %copy.119 = f32[4,3584,128]{2,1,0:T(8,128)} copy(f32[4,3584,128]{1,2,0:T(8,128)} %fusion.2) | data formatting | bytes 14680064 | tf_op jit(solution)/shard_map/rd,qrc->qdc/transpose | solution.py:173
  179.0 3.7 %fusion.6 = bf16[4,4,448,128]{3,2,1,0:T(8,128)(2,1)} fusion(f32[4,4,2,448,128]{4,3,2,1,0:T(8,128)} %bitcast.177, s32[]{:T(128)S(6)} %select_n.104), kind=kLoop, calls=%fused_computation.16 | loop fusion | bytes 3670020 | tf_op jit(solution)/shard_map/convert_element_type | solution.py:179
  182.7 2.2 multiply_reduce_fusion
  186.1 6.6 %all-to-all-start.3 = ((f32[32,1,256]{2,1,0:T(1,128)}), f32[32,1,256]{2,1,0:T(1,128)S(1)}, u32[]{:S(2)}, u32[]{:S(2)}) async-start(f32[32,1,256]{2,1,0:T(1,128)} %reshape.420), calls=%async_computation.3 | async-start | bytes 65536 | tf_op jit(solution)/shard_map/all_to_all | solution.py:187
  192.7 3.0 %fusion.7 = bf16[4,4,448,128]{3,2,0,1:T(8,128)(2,1)S(1)} fusion(bf16[4,4,448,128]{3,2,1,0:T(8,128)(2,1)} %collective-permute-done.12, f32[4,4,2,448,128]{4,3,2,1,0:T(8,128)} %bitcast.178, s32[]{:T(128)S(6)} %select_n.103), kind=kLoop, calls=%fused_computation.17 | loop fusion | flops 2752512 | bytes 7340036 | tf_op jit(solution)/shard_map/convert_element_type | solution.py:181
  197.2 2.7 %all-to-all-done.3 = f32[32,1,256]{2,1,0:T(1,128)S(1)} async-done(((f32[32,1,256]{2,1,0:T(1,128)}), f32[32,1,256]{2,1,0:T(1,128)S(1)}, u32[]{:S(2)}, u32[]{:S(2)}) %all-to-all-start.3) | async-done | bytes 32800 | tf_op jit(solution)/shard_map/all_to_all | solution.py:187
  199.8 6.4 %all-to-all-start.2 = ((bf16[4,4,448,128]{3,2,1,0:T(8,128)(2,1)}), bf16[4,4,448,128]{3,2,1,0:T(8,128)(2,1)S(1)}, u32[]{:S(2)}, u32[]{:S(2)}) async-start(bf16[4,4,448,128]{3,2,1,0:T(8,128)(2,1)} %copy.120), calls=%async_computation.2 | async-start | bytes 3670016 | tf_op jit(solution)/shard_map/all_to_all | solution.py:182
  207.7 19.4 %all-to-all-done.2 = bf16[4,4,448,128]{3,2,1,0:T(8,128)(2,1)S(1)} async-done(((bf16[4,4,448,128]{3,2,1,0:T(8,128)(2,1)}), bf16[4,4,448,128]{3,2,1,0:T(8,128)(2,1)S(1)}, u32[]{:S(2)}, u32[]{:S(2)}) %all-to-all-start.2) | async-done | bytes 1835040 | tf_op jit(solution)/shard_map/all_to_all | solution.py:182
  (138 shorter events, 37.5 us)
Async XLA Ops:
  0.6 14.1 %copy-start.8 = (bf16[1,128,3584]{2,1,0:T(8,128)(2,1)S(1)}, bf16[1,128,3584]{2,1,0:T(8,128)(2,1)}, u32[]{:S(2)}) copy-start(bf16[1,128,3584]{2,1,0:T(8,128)(2,1)} %param.9) | copy-start | bytes 2752516
  0.6 14.3 %copy-start.9 = (f32[3584]{0:T(1024)S(1)}, f32[3584]{0:T(1024)}, u32[]{:S(2)}) copy-start(f32[3584]{0:T(1024)} %param.11) | copy-start | bytes 43012
  3.4 32.0 %collective-permute-start.7 = (bf16[64,5120]{1,0:T(8,128)(2,1)S(1)}, bf16[64,5120]{1,0:T(8,128)(2,1)S(1)}, u32[]{:S(2)}, u32[]{:S(2)}) collective-permute-start(bf16[64,5120]{1,0:T(8,128)(2,1)S(1)} %fusion.10), channel_id=1, source_target_pairs={{0,4},{1,5},{2,6},{3,7},{4,8},{5,9},{6,10},{7,11},{8,12},{9,13},{1... | collective-permute-start | bytes 1966088 | tf_op jit(solution)/shard_map/ppermute | solution.py:33
  5.0 44.9 %collective-permute-start.6 = (bf16[64,5120]{1,0:T(8,128)(2,1)S(1)}, bf16[64,5120]{1,0:T(8,128)(2,1)}, u32[]{:S(2)}, u32[]{:S(2)}) collective-permute-start(bf16[64,5120]{1,0:T(8,128)(2,1)S(1)} %fusion.10), channel_id=1, source_target_pairs={{0,12},{1,13},{2,14},{3,15},{4,0},{5,1},{6,2},{7,3},{8,4},{9,5},{1... | collective-permute-start | bytes 1966088 | tf_op jit(solution)/shard_map/ppermute | solution.py:33
  8.0 24.9 %all-to-all-start = ((s32[16,5,128]{2,1,0:T(8,128)}), s32[16,5,128]{2,1,0:T(8,128)S(1)}, u32[]{:S(2)}, u32[]{:S(2)}) async-start(s32[16,5,128]{2,1,0:T(8,128)} %broadcast_in_dim.8), calls=%async_computation | async-start | bytes 131072 | tf_op jit(solution)/shard_map/all_to_all | solution.py:74
  15.9 17.9 %collective-permute-start.1 = (bf16[64,3584]{1,0:T(8,128)(2,1)S(1)}, bf16[64,3584]{1,0:T(8,128)(2,1)S(1)}, u32[]{:S(2)}, u32[]{:S(2)}) collective-permute-start(bf16[64,3584]{1,0:T(8,128)(2,1)S(1)} %get-tuple-element.13), channel_id=1, source_target_pairs={{0,4},{1,5},{2,6},{3,7},{4,8},{5,9},{6,10},{7,11},{8,12},{9,13},{1... | collective-permute-start | bytes 1376264 | tf_op jit(solution)/shard_map/ppermute | solution.py:33
  17.8 16.7 %collective-permute-start = (bf16[64,3584]{1,0:T(8,128)(2,1)S(1)}, bf16[64,3584]{1,0:T(8,128)(2,1)S(1)}, u32[]{:S(2)}, u32[]{:S(2)}) collective-permute-start(bf16[64,3584]{1,0:T(8,128)(2,1)S(1)} %get-tuple-element.13), channel_id=1, source_target_pairs={{0,12},{1,13},{2,14},{3,15},{4,0},{5,1},{6,2},{7,3},{8,4},{9,5},{1... | collective-permute-start | bytes 1376264 | tf_op jit(solution)/shard_map/ppermute | solution.py:33
  33.8 9.7 %collective-permute-start.2 = (bf16[64,3584]{1,0:T(8,128)(2,1)S(1)}, bf16[64,3584]{1,0:T(8,128)(2,1)S(1)}, u32[]{:S(2)}, u32[]{:S(2)}) collective-permute-start(bf16[64,3584]{1,0:T(8,128)(2,1)S(1)} %collective-permute-done.1), channel_id=1, source_target_pairs={{0,4},{1,5},{2,6},{3,7},{4,8},{5,9},{6,10},{7,11},{8,12},{9,13},{1... | collective-permute-start | bytes 1376264 | tf_op jit(solution)/shard_map/ppermute | solution.py:33
  35.4 12.3 %copy-start.4 = (bf16[4,3584,128]{1,2,0:T(8,128)(2,1)S(1)}, bf16[4,3584,128]{1,2,0:T(8,128)(2,1)}, u32[]{:S(2)}) copy-start(bf16[4,3584,128]{1,2,0:T(8,128)(2,1)} %copy.107) | copy-start | bytes 11010052
  35.4 18.3 %collective-permute-start.8 = (bf16[64,5120]{1,0:T(8,128)(2,1)S(1)}, bf16[64,5120]{1,0:T(8,128)(2,1)S(1)}, u32[]{:S(2)}, u32[]{:S(2)}) collective-permute-start(bf16[64,5120]{1,0:T(8,128)(2,1)S(1)} %collective-permute-done.7), channel_id=1, source_target_pairs={{0,4},{1,5},{2,6},{3,7},{4,8},{5,9},{6,10},{7,11},{8,12},{9,13},{1... | collective-permute-start | bytes 1966088 | tf_op jit(solution)/shard_map/ppermute | solution.py:33
  43.6 27.6 %collective-permute-start.3 = (bf16[256,3584]{1,0:T(8,128)(2,1)S(1)}, bf16[256,3584]{1,0:T(8,128)(2,1)S(1)}, u32[]{:S(2)}, u32[]{:S(2)}) collective-permute-start(bf16[256,3584]{1,0:T(8,128)(2,1)S(1)} %pad_maximum_fusion.2), channel_id=1, source_target_pairs={{0,3},{1,0},{2,1},{3,2},{4,7},{5,4},{6,5},{7,6},{8,11},{9,8},{10,9... | collective-permute-start | bytes 5505032 | tf_op jit(solution)/shard_map/ppermute | solution.py:33
  46.8 24.4 %collective-permute-start.4 = (bf16[256,3584]{1,0:T(8,128)(2,1)S(1)}, bf16[256,3584]{1,0:T(8,128)(2,1)S(1)}, u32[]{:S(2)}, u32[]{:S(2)}) collective-permute-start(bf16[256,3584]{1,0:T(8,128)(2,1)S(1)} %pad_maximum_fusion.2), channel_id=1, source_target_pairs={{0,1},{1,2},{2,3},{3,0},{4,5},{5,6},{6,7},{7,4},{8,9},{9,10},{10,1... | collective-permute-start | bytes 5505032 | tf_op jit(solution)/shard_map/ppermute | solution.py:33
  46.8 13.9 %slice-start = ((s8[5242880]{0:T(1024)(128)(4,1)}), s8[4194304]{0:T(1024)(128)(4,1)S(1)}, s32[]{:S(2)}) async-start(s8[5242880]{0:T(1024)(128)(4,1)} %bitcast.179), calls=%async_computation.4 | async-start | bytes 8388608
  47.7 13.1 %slice-start.1 = ((s8[5242880]{0:T(1024)(128)(4,1)}), s8[1048576]{0:T(1024)(128)(4,1)S(1)}, s32[]{:S(2)}) async-start(s8[5242880]{0:T(1024)(128)(4,1)} %bitcast.179), calls=%async_computation.5 | async-start | bytes 2097152
  55.0 40.7 %collective-permute-start.9 = (bf16[256,5120]{1,0:T(8,128)(2,1)S(1)}, bf16[256,5120]{1,0:T(8,128)(2,1)S(1)}, u32[]{:S(2)}, u32[]{:S(2)}) collective-permute-start(bf16[256,5120]{1,0:T(8,128)(2,1)S(1)} %pad_maximum_fusion), channel_id=1, source_target_pairs={{0,3},{1,0},{2,1},{3,2},{4,7},{5,4},{6,5},{7,6},{8,11},{9,8},{10,9... | collective-permute-start | bytes 7864328 | tf_op jit(solution)/shard_map/ppermute | solution.py:33
  60.7 41.6 %collective-permute-start.11 = (bf16[256,5120]{1,0:T(8,128)(2,1)S(1)}, bf16[256,5120]{1,0:T(8,128)(2,1)S(1)}, u32[]{:S(2)}, u32[]{:S(2)}) collective-permute-start(bf16[256,5120]{1,0:T(8,128)(2,1)S(1)} %pad_maximum_fusion), channel_id=1, source_target_pairs={{0,1},{1,2},{2,3},{3,0},{4,5},{5,6},{6,7},{7,4},{8,9},{9,10},{10,1... | collective-permute-start | bytes 7864328 | tf_op jit(solution)/shard_map/ppermute | solution.py:33
  71.3 1.4 copy-start.7
  71.3 47.7 %collective-permute-start.5 = (bf16[256,3584]{1,0:T(8,128)(2,1)S(1)}, bf16[256,3584]{1,0:T(8,128)(2,1)S(1)}, u32[]{:S(2)}, u32[]{:S(2)}) collective-permute-start(bf16[256,3584]{1,0:T(8,128)(2,1)S(1)} %collective-permute-done.4), channel_id=1, source_target_pairs={{0,1},{1,2},{2,3},{3,0},{4,5},{5,6},{6,7},{7,4},{8,9},{9,10},{10,1... | collective-permute-start | bytes 5505032 | tf_op jit(solution)/shard_map/ppermute | solution.py:33
  97.3 33.1 %collective-permute-start.10 = (bf16[256,5120]{1,0:T(8,128)(2,1)S(1)}, bf16[256,5120]{1,0:T(8,128)(2,1)S(1)}, u32[]{:S(2)}, u32[]{:S(2)}) collective-permute-start(bf16[256,5120]{1,0:T(8,128)(2,1)S(1)} %collective-permute-done.9), channel_id=1, source_target_pairs={{0,3},{1,0},{2,1},{3,2},{4,7},{5,4},{6,5},{7,6},{8,11},{9,8},{10,9... | collective-permute-start | bytes 7864328 | tf_op jit(solution)/shard_map/ppermute | solution.py:33
  120.2 0.8 copy-start
  132.0 0.8 copy-start.2
  135.5 16.6 %all-to-all-start.1 = ((f32[16,1,12288]{2,1,0:T(1,128)}), f32[16,1,12288]{2,1,0:T(1,128)S(1)}, u32[]{:S(2)}, u32[]{:S(2)}) async-start(f32[16,1,12288]{2,1,0:T(1,128)} %reshape.418), calls=%async_computation.1 | async-start | bytes 1572864 | tf_op jit(solution)/shard_map/all_to_all | solution.py:74
  140.6 3.0 %copy-start.3 = (f32[256,512]{0,1:S(1)}, f32[256,512]{0,1}, u32[]{:S(2)}) copy-start(f32[256,512]{0,1} %copy-done.2) | copy-start | bytes 1572868
  179.0 3.8 %copy-start.1 = (f32[256,512]{0,1:S(1)}, f32[256,512]{0,1}, u32[]{:S(2)}) copy-start(f32[256,512]{0,1} %copy-done) | copy-start | bytes 1572868
  179.0 3.8 %copy-start.5 = (f32[4,256,128]{1,2,0:T(8,128)S(1)}, f32[4,256,128]{1,2,0:T(8,128)}, u32[]{:S(2)}) copy-start(f32[4,256,128]{1,2,0:T(8,128)} %multiply_bitcast_fusion.3) | copy-start | bytes 1572868
  179.0 3.8 %copy-start.6 = (f32[4,256,128]{1,2,0:T(8,128)S(1)}, f32[4,256,128]{1,2,0:T(8,128)}, u32[]{:S(2)}) copy-start(f32[4,256,128]{1,2,0:T(8,128)} %multiply_bitcast_fusion.2) | copy-start | bytes 1572868
  182.7 10.0 %collective-permute-start.12 = (bf16[4,4,448,128]{3,2,1,0:T(8,128)(2,1)}, bf16[4,4,448,128]{3,2,1,0:T(8,128)(2,1)}, u32[]{:S(2)}, u32[]{:S(2)}) collective-permute-start(bf16[4,4,448,128]{3,2,1,0:T(8,128)(2,1)} %fusion.6), channel_id=1, source_target_pairs={{0,16},{16,0},{1,17},{17,1},{2,18},{18,2},{3,19},{19,3},{4,20},{20... | collective-permute-start | bytes 5505032 | tf_op jit(solution)/shard_map/ppermute | solution.py:179
  186.1 13.7 %all-to-all-start.3 = ((f32[32,1,256]{2,1,0:T(1,128)}), f32[32,1,256]{2,1,0:T(1,128)S(1)}, u32[]{:S(2)}, u32[]{:S(2)}) async-start(f32[32,1,256]{2,1,0:T(1,128)} %reshape.420), calls=%async_computation.3 | async-start | bytes 65536 | tf_op jit(solution)/shard_map/all_to_all | solution.py:187
  199.8 27.3 %all-to-all-start.2 = ((bf16[4,4,448,128]{3,2,1,0:T(8,128)(2,1)}), bf16[4,4,448,128]{3,2,1,0:T(8,128)(2,1)S(1)}, u32[]{:S(2)}, u32[]{:S(2)}) async-start(bf16[4,4,448,128]{3,2,1,0:T(8,128)(2,1)} %copy.120), calls=%async_computation.2 | async-start | bytes 3670016 | tf_op jit(solution)/shard_map/all_to_all | solution.py:182

commit v2 on v1

v2 whole, which is shorter than its diff:
```python
import functools

import jax
import jax.numpy as jnp
from jax import lax
from jax.experimental import pallas as pl
from jax.experimental.pallas import tpu as pltpu
from jax.sharding import Mesh
from jax.sharding import PartitionSpec as P

BOOKS = 4
SIDE = 4
CTX = ("cx", "cz")
COLUMN = ("role", "ylo")
TURN = ("core", "cx", "cz")

epsilon = 1e-06
sharpness_divisor = 2.0
blend_ratio = 0.5


def line_pairs(phase, step):
    pairs = []
    for core in range(2):
        for x in range(SIDE):
            for z in range(SIDE):
                along_x = (core + phase) % 2 == 0
                to_x = (x + step) % SIDE if along_x else x
                to_z = z if along_x else (z + step) % SIDE
                pairs.append(
                    ((core * SIDE + x) * SIDE + z, (core * SIDE + to_x) * SIDE + to_z)
                )
    return pairs


VMEM = pl.BlockSpec(memory_space=pltpu.VMEM)
SMEM = pl.BlockSpec(memory_space=pltpu.SMEM)


def small_kernel(name, flops=0, transcendentals=0, bytes_accessed=0, limit=8 << 20):
    return {
        "compiler_params": pltpu.CompilerParams(vmem_limit_bytes=limit),
        "cost_estimate": pl.CostEstimate(
            flops=flops, transcendentals=transcendentals, bytes_accessed=bytes_accessed
        ),
        "name": name,
    }


def hold_kernel(array_ref, out_ref, semaphore):
    copy = pltpu.make_async_copy(array_ref, out_ref, semaphore)
    copy.start()
    copy.wait()


def held(array):
    return pl.pallas_call(
        hold_kernel,
        in_specs=[pl.BlockSpec(memory_space=pl.ANY)],
        out_specs=VMEM,
        out_shape=pltpu.VMEM(array.shape, array.dtype),
        scratch_shapes=[pltpu.SemaphoreType.DMA(())],
        **small_kernel("held", bytes_accessed=2 * array.size * array.dtype.itemsize),
    )(array)


def moved(value, phase, step):
    return lax.ppermute(value, TURN, line_pairs(phase, step))


def neighbours(block, phase):
    return moved(block, phase, -1), moved(block, phase, 1)


def normalize(states, gain):
    values = states.astype(jnp.float32)
    factor = lax.rsqrt(jnp.mean(values * values, axis=-1, keepdims=True) + epsilon)
    return (values * factor * gain).astype(jnp.bfloat16)


def joined(pieces, span):
    return jnp.concatenate([piece[:, span] for piece in pieces], axis=0)


def project_kernel(is_teacher, *refs):
    *pieces, heads_ref, out_ref, sums_ref = refs
    features, width = heads_ref.shape[1:]
    depth = features // 4
    for pair in range(BOOKS // 2):
        total = None
        for start in range(0, features, depth):
            span = slice(start, start + depth)
            part = jnp.dot(
                joined(pieces, span),
                jnp.concatenate(
                    [heads_ref[2 * pair, span, :], heads_ref[2 * pair + 1, span, :]], axis=1
                ),
                preferred_element_type=jnp.float32,
            )
            total = part if total is None else total + part
        total = total.T
        if is_teacher:
            total = total / sharpness_divisor
        for side in range(2):
            book = 2 * pair + side
            values = total[side * width : (side + 1) * width]
            out_ref[book] = values
            peak = jnp.max(values, axis=0, keepdims=True)
            found = jnp.sum(jnp.exp(values - peak), axis=0, keepdims=True)
            sums_ref[book : book + 1, :] = peak + jnp.log(found)
            if not is_teacher:
                found = jnp.sum(jnp.exp((values - peak) / sharpness_divisor), axis=0, keepdims=True)
                sums_ref[BOOKS + book : BOOKS + book + 1, :] = (
                    peak / sharpness_divisor + jnp.log(found)
                )


def project(pieces, heads, is_teacher):
    count, features = sum(piece.shape[0] for piece in pieces), pieces[0].shape[1]
    columns = heads.shape[2]
    return pl.pallas_call(
        functools.partial(project_kernel, is_teacher),
        in_specs=[VMEM] * (len(pieces) + 1),
        out_specs=[VMEM, VMEM],
        out_shape=[
            pltpu.VMEM((BOOKS, columns, count), jnp.float32),
            pltpu.VMEM((2 * BOOKS, count), jnp.float32),
        ],
        **small_kernel(
            "project_teacher" if is_teacher else "project_student",
            flops=2 * count * features * BOOKS * columns,
            transcendentals=2 * count * BOOKS * columns,
            bytes_accessed=2 * features * (count + BOOKS * columns) + 4 * count * BOOKS * columns,
        ),
    )(*pieces, heads)


def pack_kernel(place_ref, info_ref, *refs):
    teacher, student = refs[:SIDE], refs[SIDE : 2 * SIDE]
    out_ref, held = refs[2 * SIDE :]
    out_ref[3 * BOOKS] = info_ref[...]
    half = teacher[0].shape[1] // SIDE
    for turn in range(SIDE):
        stacked = jnp.concatenate([teacher[turn][:BOOKS, :], student[turn][...]], axis=0)
        for j in range(SIDE):
            held[turn * SIDE + j] = stacked[:, j * half : (j + 1) * half]
    for pair in range(out_ref.shape[1]):
        first = held[place_ref[2 * pair]]
        second = held[place_ref[2 * pair + 1]]
        out_ref[: 3 * BOOKS, pair, :] = jnp.concatenate([first, second], axis=1)


def pack_sums(place, info, teacher_sums, student_sums):
    half = teacher_sums[0].shape[1] // SIDE
    count = SIDE * SIDE
    return pl.pallas_call(
        pack_kernel,
        in_specs=[SMEM] + [VMEM] * (2 * SIDE + 1),
        out_specs=VMEM,
        out_shape=jax.ShapeDtypeStruct((3 * BOOKS + 1, count // 2, 2 * half), jnp.float32),
        scratch_shapes=[pltpu.VMEM((count, 3 * BOOKS, half), jnp.float32)],
        **small_kernel("pack_sums", bytes_accessed=1 << 17, limit=4 << 20),
    )(place, info, *teacher_sums, *student_sums)


def merged(parts):
    peak = parts[0]
    for part in parts[1:]:
        peak = jnp.maximum(peak, part)
    found = jnp.exp(parts[0] - peak)
    for part in parts[1:]:
        found = found + jnp.exp(part - peak)
    return peak + jnp.log(found)


def merge_kernel(*refs):
    out_ref = refs[-1]
    kinds = 3 * BOOKS
    out_ref[:kinds] = merged([part[:kinds] for part in refs[:-1]])
    for number, part in enumerate(refs[:-1]):
        out_ref[kinds + number] = part[kinds]


def merge_sums(parts):
    return pl.pallas_call(
        merge_kernel,
        in_specs=[VMEM] * len(parts),
        out_specs=VMEM,
        out_shape=jax.ShapeDtypeStruct((3 * BOOKS + SIDE, *parts[0].shape[1:]), jnp.float32),
        **small_kernel("merge_sums", bytes_accessed=1 << 18, limit=4 << 20),
    )(*parts)


def slope_kernel(half, order_ref, *refs):
    arrived, refs = refs[:SIDE], refs[SIDE:]
    teacher, student = refs[:SIDE], refs[SIDE : 2 * SIDE]
    slope_ref, terms_ref, whole, placed, found_terms = refs[2 * SIDE :]
    own_half, first_entry = order_ref[SIDE * SIDE], order_ref[SIDE * SIDE + 1]
    turned_round = order_ref[SIDE * SIDE + 2]
    kinds = 3 * BOOKS
    columns, rows = teacher[0].shape[1], teacher[0].shape[2]
    whole[...] = merged([part[:kinds] for part in arrived])
    segments = jnp.concatenate(
        [
            arrived[dz][kinds + dx, BOOKS : BOOKS + 1, :]
            for dz in range(SIDE)
            for dx in range(SIDE)
        ],
        axis=0,
    )
    documents = 2 * SIDE * SIDE
    length = segments.shape[0] * segments.shape[1]
    sizes = []
    for document in range(documents):
        members = jnp.where(segments == document, 1.0, 0.0)
        sizes.append(jnp.sum(jnp.sum(members, axis=0, keepdims=True), axis=1, keepdims=True))
    for turn in range(SIDE):
        span = slice(turn * rows, (turn + 1) * rows)
        lines, infos = [], []
        for j in range(SIDE):
            block = order_ref[turn * SIDE + j]
            line = whole[:, pl.ds(block // 2, 1), :]
            lines.append(jnp.where(block % 2 == 0, line[:, :, :half], line[:, :, half:]))
            line = jnp.where(
                turned_round == 0, arrived[turn][kinds + j], arrived[j][kinds + turn]
            )
            infos.append(jnp.where(own_half == 0, line[:, :half], line[:, half:]))
        placed[:kinds, :, span] = jnp.concatenate(lines, axis=2)
        info = jnp.concatenate(infos, axis=1)
        segment = info[BOOKS : BOOKS + 1]
        row_sizes = jnp.zeros_like(segment)
        for document in range(documents):
            row_sizes = jnp.where(segment == document, sizes[document], row_sizes)
        placed[kinds, :, span] = length / (documents * row_sizes)
        for each in range(BOOKS):
            placed[kinds + 1 + each, :, span] = info[each : each + 1]

    entries = lax.broadcasted_iota(jnp.int32, (columns, rows), 0)
    for turn in range(SIDE):
        span = slice(turn * rows, (turn + 1) * rows)
        weight = placed[kinds, :, span]
        for book in range(BOOKS):
            target = placed[kinds + 1 + book, :, span].astype(jnp.int32) - first_entry
            raw = student[turn][book]
            teacher_logp = teacher[turn][book] - placed[book, :, span]
            plain_logp = raw - placed[BOOKS + book, :, span]
            tempered_logp = raw / sharpness_divisor - placed[2 * BOOKS + book, :, span]
            hits = entries == target
            teacher_sent = teacher_logp.astype(jnp.bfloat16).astype(jnp.float32)
            share = jnp.exp(teacher_sent)
            gap = jnp.sum(share * (teacher_sent - tempered_logp), axis=0, keepdims=True)
            mismatch = -jnp.sum(jnp.where(hits, plain_logp, 0.0), axis=0, keepdims=True)
            found_terms[book : book + 1, span] = -jnp.sum(
                jnp.where(hits, teacher_logp, 0.0), axis=0, keepdims=True
            )
            found_terms[BOOKS + book : BOOKS + book + 1, span] = (
                blend_ratio * sharpness_divisor * sharpness_divisor * gap
                + (1.0 - blend_ratio) * mismatch
            )
            slope = weight * (
                blend_ratio * sharpness_divisor * (jnp.exp(tempered_logp) - share)
                + (1.0 - blend_ratio) * (jnp.exp(plain_logp) - jnp.where(hits, 1.0, 0.0))
            )
            slope_ref[span, book * columns : (book + 1) * columns] = slope.T.astype(jnp.bfloat16)
    for place in range(SIDE * SIDE):
        lines = found_terms[:, place * half : (place + 1) * half]
        terms_ref[0, order_ref[place]] = lines[:BOOKS]
        terms_ref[1, order_ref[place]] = lines[BOOKS:]


def slopes(order, arrived, teacher_scaled, student_raw, half):
    columns, rows = teacher_scaled[0].shape[1:]
    return pl.pallas_call(
        functools.partial(slope_kernel, half),
        in_specs=[SMEM] + [VMEM] * (3 * SIDE),
        out_specs=[VMEM, VMEM],
        out_shape=[
            pltpu.VMEM((SIDE * rows, BOOKS * columns), jnp.bfloat16),
            jax.ShapeDtypeStruct((2, SIDE * SIDE, BOOKS, half), jnp.float32),
        ],
        scratch_shapes=[
            pltpu.VMEM((3 * BOOKS, *arrived[0].shape[1:]), jnp.float32),
            pltpu.VMEM((4 * BOOKS + 1, 1, SIDE * rows), jnp.float32),
            pltpu.VMEM((2 * BOOKS, SIDE * rows), jnp.float32),
        ],
        **small_kernel(
            "slopes",
            flops=40 * BOOKS * columns * SIDE * rows,
            transcendentals=3 * BOOKS * columns * SIDE * rows,
            bytes_accessed=10 * BOOKS * columns * SIDE * rows,
        ),
    )(order, *arrived, *teacher_scaled, *student_raw)


def flip_kernel(*refs):
    *pieces, out_ref = refs
    width = 512
    for start in range(0, out_ref.shape[0], width):
        span = slice(start, start + width)
        out_ref[span, :] = joined(pieces, span).T


def flipped(pieces):
    count, features = sum(piece.shape[0] for piece in pieces), pieces[0].shape[1]
    return pl.pallas_call(
        flip_kernel,
        in_specs=[VMEM] * len(pieces),
        out_specs=VMEM,
        out_shape=pltpu.VMEM((features, count), pieces[0].dtype),
        **small_kernel("flipped", bytes_accessed=4 * count * features),
    )(*pieces)


def gradient_kernel(with_taken, blocks_ref, *refs):
    rows, slope_ref = refs[:SIDE], refs[SIDE]
    outs = refs[SIDE + 2 if with_taken else SIDE + 1 :]
    step = 0
    for out_ref in outs:
        height = out_ref.shape[1]
        for number in range(out_ref.shape[0]):
            start = pl.multiple_of(blocks_ref[0, step] * height, 64)
            found = jnp.dot(
                jnp.concatenate([part[pl.ds(start, height), :] for part in rows], axis=1),
                slope_ref[...],
                preferred_element_type=jnp.float32,
            )
            if with_taken:
                found = found + refs[SIDE + 1][blocks_ref[1, step]].astype(jnp.float32)
            out_ref[number] = found.astype(out_ref.dtype)
            step += 1


def gradient_blocks(blocks, rows, slope, taken, height, dtype, apart=False):
    count = SIDE * rows[0].shape[1]
    entries = slope.shape[1]
    steps = blocks.shape[1]
    operands = [*rows, slope] + ([] if taken is None else [taken])
    shapes = [(1, height, entries)] * steps if apart else [(steps, height, entries)]
    return pl.pallas_call(
        functools.partial(gradient_kernel, taken is not None),
        in_specs=[SMEM] + [VMEM] * len(operands),
        out_specs=[VMEM] * len(shapes),
        out_shape=[jax.ShapeDtypeStruct(shape, dtype) for shape in shapes],
        **small_kernel(
            "gradient_blocks",
            flops=2 * steps * height * entries * count,
            bytes_accessed=2 * steps * height * (count + entries),
        ),
    )(blocks, *operands)


def total_kernel(own_ref, after_ref, before_ref, opposite_ref, out_ref):
    columns = out_ref.shape[2]
    for book in range(BOOKS):
        span = slice(book * columns, (book + 1) * columns)
        total = own_ref[0, :, span] + after_ref[0, :, span].astype(jnp.float32)
        total = total + before_ref[0, :, span].astype(jnp.float32)
        out_ref[book] = total + opposite_ref[0, :, span].astype(jnp.float32)


def total_of(parts):
    _, height, entries = parts[0].shape
    return pl.pallas_call(
        total_kernel,
        in_specs=[VMEM] * len(parts),
        out_specs=VMEM,
        out_shape=jax.ShapeDtypeStruct((BOOKS, height, entries // BOOKS), jnp.float32),
        **small_kernel("total_of", bytes_accessed=14 * height * entries),
    )(*parts)


def places():
    mx, mz, core = (lax.axis_index(name) for name in ("cx", "cz", "core"))
    place = jnp.arange(SIDE * SIDE, dtype=jnp.int32)
    turn, step = place // SIDE, place % SIDE
    x = (mx + jnp.where(core == 0, step, turn)) % SIDE
    z = (mz + jnp.where(core == 0, turn, step)) % SIDE
    order = (x * SIDE + z).astype(jnp.int32)
    dx, dz = (turn - mx) % SIDE, (step - mz) % SIDE
    return order, jnp.where(core == 0, dz * SIDE + dx, dx * SIDE + dz).astype(jnp.int32)


def on_device(
    teacher_states,
    student_states,
    teacher_gain,
    student_gain,
    mentor_output_weights,
    student_heads,
    segments,
    targets,
):
    columns = student_heads.shape[2]
    features = student_heads.shape[1]
    count = lax.axis_size(CTX)
    role = lax.axis_index("role")
    core = lax.axis_index("core")
    rows_here = teacher_states.shape[1]
    half = rows_here // 2

    def own_half(states):
        return lax.dynamic_slice_in_dim(states[0], role * half, half, axis=0)

    order, place = places()
    order = jnp.concatenate(
        [order, jnp.stack([role, lax.axis_index(CTX) * columns, core]).astype(jnp.int32)]
    )
    owners = lax.axis_size(COLUMN)
    height = features // (2 * owners)
    chip = lax.axis_index(COLUMN)

    def blocks_of(offsets, of_core):
        chips = [(chip + offset) % owners for offset in offsets]
        return jnp.stack(
            [jnp.stack([2 * each + of_core for each in chips]), jnp.array(offsets, jnp.int32)]
        ).astype(jnp.int32)

    away = (2, 1, 3)
    blocks = [
        blocks_of((0,), core),
        blocks_of(away, core),
        blocks_of(range(owners), 1 - core),
    ]

    def back(shift):
        return [(source, (source - shift) % SIDE) for source in range(SIDE)]

    info = jnp.concatenate(
        [targets[0].T, segments, jnp.zeros((BOOKS - 1, rows_here), jnp.int32)]
    ).astype(jnp.float32)
    student_rows = normalize(own_half(student_states), student_gain)
    teacher_rows = normalize(own_half(teacher_states), teacher_gain)
    tie = lax.optimization_barrier
    student_rows, teacher_rows = tie((student_rows, teacher_rows))

    student_near = neighbours(student_rows, 0)
    student_after, student_before, order, place, info, *blocks = tie(
        (*student_near, order, place, info, *blocks)
    )
    student_opposite = moved(student_after, 0, -1)
    teacher_near = neighbours(teacher_rows, 0)
    teacher_after, teacher_before, student_after = tie((*teacher_near, student_after))
    teacher_opposite = moved(teacher_before, 0, 1)
    student_line = jnp.concatenate(
        [student_rows, student_after, student_opposite, student_before]
    )
    student_after, student_before, teacher_opposite = tie(
        (*neighbours(student_line, 1), teacher_opposite)
    )
    teacher_line = jnp.concatenate(
        [teacher_rows, teacher_after, teacher_opposite, teacher_before]
    )
    teacher_after, teacher_before = tie(neighbours(teacher_line, 1))

    def relayed(after, before):
        middle = after.shape[0] // 2
        return (moved(after[:middle], 1, -1), moved(before[middle:], 1, 1))

    student_opposite = relayed(student_after, student_before)
    teacher_opposite = relayed(teacher_after, teacher_before)
    student_parts = [(student_line,), (student_after,), student_opposite, (student_before,)]
    teacher_parts = [(teacher_line,), (teacher_after,), teacher_opposite, (teacher_before,)]
    mentor_output_weights, student_heads = held(mentor_output_weights), held(student_heads)

    def project_teacher(turn):
        return project(teacher_parts[turn], mentor_output_weights, True)

    def project_student(turn):
        return project(student_parts[turn], student_heads, False)

    early = (0, 1, 3)
    flipped_rows = [flipped(student_parts[turn]) for turn in early]
    teacher_found = [project_teacher(turn) for turn in early]
    student_found = [project_student(turn) for turn in early]
    (
        student_parts[2],
        teacher_parts[2],
        flipped_rows,
        teacher_found,
        student_found,
    ) = tie((student_parts[2], teacher_parts[2], flipped_rows, teacher_found, student_found))
    flipped_rows.insert(2, flipped(student_parts[2]))
    student_found.insert(2, project_student(2))
    teacher_found.insert(2, project_teacher(2))
    student_raw, student_sums = zip(*student_found)
    teacher_scaled, teacher_sums = zip(*teacher_found)
    sent = pack_sums(place, info, teacher_sums, student_sums)
    for axis in CTX:
        parts = [
            sent if shift == 0 else lax.ppermute(sent, axis, back(shift)) for shift in range(SIDE)
        ]
        if axis == CTX[0]:
            sent = merge_sums(parts)
    slope, terms = slopes(order, parts, teacher_scaled, student_raw, half)
    (given,) = gradient_blocks(blocks[2], flipped_rows, slope, None, height, jnp.bfloat16)
    taken = lax.ppermute(given, "core", [(0, 1), (1, 0)])
    sent = gradient_blocks(blocks[1], flipped_rows, slope, taken, height, jnp.bfloat16, True)
    slope, *sent = tie((slope, *sent))
    (own,) = gradient_blocks(blocks[0], flipped_rows, slope, taken, height, jnp.float32)
    terms, own = tie((terms, own))
    shares = total_of(
        [own]
        + [
            lax.ppermute(piece, COLUMN, [(y, (y + offset) % owners) for y in range(owners)])
            for offset, piece in zip(away, sent)
        ]
    )

    terms = lax.all_to_all(
        terms.reshape(2 * count, 1, BOOKS * half), ("role", *CTX), 0, 0, tiled=True
    )
    terms = jnp.sum(terms.reshape(2, count, BOOKS, half), axis=1)
    frame_terms = jnp.moveaxis(terms, 1, 2).reshape(1, 1, rows_here, BOOKS)
    return (shares, frame_terms)


def solution(mesh):
    finer = Mesh(
        mesh.devices.reshape(2, 2, 2, SIDE, SIDE),
        ("role", "ylo", "core", "cx", "cz"),
    )
    dp = ("ylo", "core")
    placed = (
        P(dp, CTX, None),
        P(dp, CTX, None),
        P(),
        P(),
        P(None, None, CTX),
        P(None, None, CTX),
        P(dp, CTX),
        P(dp, CTX, None),
    )
    return jax.shard_map(
        on_device,
        mesh=finer,
        in_specs=placed,
        out_specs=(P(None, ("role", *dp), CTX), P("role", dp, CTX, None)),
        check_vma=False,
    )
```

time: 231 us -> 184 us (0.80)
  local copies, waits for them, and re-layouts: 44.3 us -> 3.25 us
  Pallas kernels: 0 us -> 26.6 us
  matrix products: 23.6 us -> 0 us
  blocking collectives: 0 us -> 19.8 us
  other arithmetic: 23.3 us -> 4.58 us
  starting transfers between devices: 46.4 us -> 28.7 us
  waiting for transfers between devices: 89.6 us -> 99.1 us
    all_to_all x4 -> x0, waiting for transfers between devices: 29.8 us -> none  [the longest x1 19.4 us: on_device(): pieces = lax.all_to_all(pieces, COLUMN, 0, 0, tiled=True)]
    pallas_call x0 -> x21, Pallas kernels: none -> 26.6 us  [the longest x8 12.8 us: project(): pl.pallas_call(functools.partial(project_kernel, is_teacher), in_specs=[V...]
    ppermute x12 -> x14, waiting for transfers between devices: 59.8 us -> 85.4 us  [moved(): return lax.ppermute(value, TURN, line_pairs(phase, step))]
    all_to_all x4 -> x0, starting transfers between devices: 24.7 us -> none  [the longest x2 11.7 us: copy_for_each(): return lax.all_to_all(copies, axis, split_axis=0, concat_axis=0, tiled=True)]
    unnamed x37 -> x22, local copies, waits for them, and re-layouts: 24.9 us -> 1.93 us
    all_to_all x0 -> x1, blocking collectives: none -> 19.8 us  [on_device(): lax.all_to_all(terms.reshape(2 * count, 1, BOOKS * half), ('role', *CTX),...]
    ppermute x1 -> x10, waiting for transfers between devices: 0.01 us -> 13.7 us  [the longest x6 9.91 us: on_device(): lax.ppermute(sent, axis, back(shift))]
    unnamed x8 -> x0, matrix products: 11.9 us -> none
  transfers between devices with their start and end apart: 17 -> 24, of which waited for: 9 -> 19; matrix products, arithmetic and copies ran while one was open for 22% -> 1% of each run, Pallas kernels for 0% -> 7%
where the time goes in v2:
time: 184 us; the launch traced here: 183 us
  waiting for transfers between devices  99.1 us (54%)
  starting transfers between devices  28.7 us (16%)
  Pallas kernels  26.6 us (14%)
  blocking collectives  19.8 us (11%)
  other arithmetic  4.58 us (2%)
  local copies, waits for them, and re-layouts  3.25 us (2%)
    ppermute x14, waiting for transfers between devices, moved(): return lax.ppermute(value, TURN, line_pairs(phase, step))  85.4 us
    all_to_all x1, blocking collectives, on_device(): lax.all_to_all(terms.reshape(2 * count, 1, BOOKS * half), ('role', *CTX),...  19.8 us
    ppermute x14, starting transfers between devices, moved(): return lax.ppermute(value, TURN, line_pairs(phase, step))  17.7 us
    pallas_call x8, Pallas kernels, project(): pl.pallas_call(functools.partial(project_kernel, is_teacher), in_specs=[V...  12.8 us
    ppermute x6, waiting for transfers between devices, on_device(): lax.ppermute(sent, axis, back(shift))  9.91 us
    ppermute x6, starting transfers between devices, on_device(): lax.ppermute(sent, axis, back(shift))  7.4 us
    pallas_call x3, Pallas kernels, gradient_blocks(): pl.pallas_call(functools.partial(gradient_kernel, taken is not None), in_...  5.93 us
    ppermute x1, waiting for transfers between devices, on_device(): taken = lax.ppermute(given, 'core', [(0, 1), (1, 0)])  3.77 us
  transfers between devices with their start and end apart: 24, of which 19 were waited for; matrix products, arithmetic and copies ran while one was open for 1% of the time, Pallas kernels for 7%

profile of v2, /device:TPU:24, one launch (start us, length us, event | category | flops | bytes accessed | tf_op | source)
XLA Modules:
  0.0 183.1 jit_solution(4388578848969852691)
XLA Ops:
  4.9 2.8 %collective-permute-start = (bf16[64,3584]{1,0:T(8,128)(2,1)S(1)}, bf16[64,3584]{1,0:T(8,128)(2,1)S(1)}, u32[]{:S(2)}, u32[]{:S(2)}) collective-permute-start(bf16[64,3584]{1,0:T(8,128)(2,1)S(1)} %fusion.5), channel_id=1, source_target_pairs={{0,12},{1,13},{2,14},{3,15},{4,0},{5,1},{6,2},{7,3},{8,4},{9,5},{1... | collective-permute-start | bytes 1376264 | tf_op jit(solution)/shard_map/ppermute | solution.py:68
  7.7 3.2 %collective-permute-start.2 = (bf16[64,5120]{1,0:T(8,128)(2,1)S(1)}, bf16[64,5120]{1,0:T(8,128)(2,1)S(1)}, u32[]{:S(2)}, u32[]{:S(2)}) collective-permute-start(bf16[64,5120]{1,0:T(8,128)(2,1)S(1)} %fusion.2), channel_id=1, source_target_pairs={{0,12},{1,13},{2,14},{3,15},{4,0},{5,1},{6,2},{7,3},{8,4},{9,5},{1... | collective-permute-start | bytes 1966088 | tf_op jit(solution)/shard_map/ppermute | solution.py:68
  11.4 2.3 %collective-permute-done = bf16[64,3584]{1,0:T(8,128)(2,1)S(1)} collective-permute-done((bf16[64,3584]{1,0:T(8,128)(2,1)S(1)}, bf16[64,3584]{1,0:T(8,128)(2,1)S(1)}, u32[]{:S(2)}, u32[]{:S(2)}) %collective-permute-start) | collective-permute-done | bytes 458784 | tf_op jit(solution)/shard_map/ppermute | solution.py:68
  13.7 3.7 %collective-permute-done.1 = bf16[64,3584]{1,0:T(8,128)(2,1)S(1)} collective-permute-done((bf16[64,3584]{1,0:T(8,128)(2,1)S(1)}, bf16[64,3584]{1,0:T(8,128)(2,1)S(1)}, u32[]{:S(2)}, u32[]{:S(2)}) %collective-permute-start.1) | collective-permute-done | bytes 458784 | tf_op jit(solution)/shard_map/ppermute | solution.py:68
  17.4 3.3 %collective-permute-done.2 = bf16[64,5120]{1,0:T(8,128)(2,1)S(1)} collective-permute-done((bf16[64,5120]{1,0:T(8,128)(2,1)S(1)}, bf16[64,5120]{1,0:T(8,128)(2,1)S(1)}, u32[]{:S(2)}, u32[]{:S(2)}) %collective-permute-start.2) | collective-permute-done | bytes 655392 | tf_op jit(solution)/shard_map/ppermute | solution.py:68
  20.7 3.7 %collective-permute-done.3 = bf16[64,5120]{1,0:T(8,128)(2,1)S(1)} collective-permute-done((bf16[64,5120]{1,0:T(8,128)(2,1)S(1)}, bf16[64,5120]{1,0:T(8,128)(2,1)S(1)}, u32[]{:S(2)}, u32[]{:S(2)}) %collective-permute-start.3) | collective-permute-done | bytes 655392 | tf_op jit(solution)/shard_map/ppermute | solution.py:68
  25.9 4.1 %collective-permute-start.5 = (bf16[256,3584]{1,0:T(8,128)(2,1)S(1)}, bf16[256,3584]{1,0:T(8,128)(2,1)S(1)}, u32[]{:S(2)}, u32[]{:S(2)}) collective-permute-start(bf16[256,3584]{1,0:T(8,128)(2,1)S(1)} %constant_dynamic-update-slice_fusion.refs_0_), channel_id=1, source_target_pairs={{0,3},{1,0},{2,1},{3,2},{4,7},{5,4},{6,5},{7,6},{8,11},{9,8},{10,9... | collective-permute-start | bytes 5505032 | tf_op jit(solution)/shard_map/ppermute | solution.py:68
  31.1 18.0 %collective-permute-done.7 = bf16[64,5120]{1,0:T(8,128)(2,1)S(1)} collective-permute-done((bf16[64,5120]{1,0:T(8,128)(2,1)S(1)}, bf16[64,5120]{1,0:T(8,128)(2,1)S(1)}, u32[]{:S(2)}, u32[]{:S(2)}) %collective-permute-start.7) | collective-permute-done | bytes 655392 | tf_op jit(solution)/shard_map/ppermute | solution.py:68
  49.2 1.6 collective-permute-done.5.refs_0_
  50.8 9.0 %collective-permute-done.6.refs_0_ = bf16[256,3584]{1,0:T(8,128)(2,1)S(1)} collective-permute-done((bf16[256,3584]{1,0:T(8,128)(2,1)S(1)}, bf16[256,3584]{1,0:T(8,128)(2,1)S(1)}, u32[]{:S(2)}, u32[]{:S(2)}) %collective-permute-start.6) | collective-permute-done | bytes 1835040 | tf_op jit(solution)/shard_map/ppermute | solution.py:68
  62.0 29.6 %collective-permute-done.10.refs_0_ = bf16[256,5120]{1,0:T(8,128)(2,1)S(1)} collective-permute-done((bf16[256,5120]{1,0:T(8,128)(2,1)S(1)}, bf16[256,5120]{1,0:T(8,128)(2,1)S(1)}, u32[]{:S(2)}, u32[]{:S(2)}) %collective-permute-start.10) | collective-permute-done | bytes 2621472 | tf_op jit(solution)/shard_map/ppermute | solution.py:68
  91.6 2.2 %collective-permute-done.11.refs_0_ = bf16[256,5120]{1,0:T(8,128)(2,1)S(1)} collective-permute-done((bf16[256,5120]{1,0:T(8,128)(2,1)S(1)}, bf16[256,5120]{1,0:T(8,128)(2,1)S(1)}, u32[]{:S(2)}, u32[]{:S(2)}) %collective-permute-start.11) | collective-permute-done | bytes 2621472 | tf_op jit(solution)/shard_map/ppermute | solution.py:68
  94.0 2.1 %collective-permute-start.13 = (bf16[128,5120]{1,0:T(8,128)(2,1)S(1)}, bf16[128,5120]{1,0:T(8,128)(2,1)S(1)}, u32[]{:S(2)}, u32[]{:S(2)}) collective-permute-start(bf16[128,5120]{1,0:T(8,128)(2,1)S(1)} %slice.15), channel_id=1, source_target_pairs={{0,1},{1,2},{2,3},{3,0},{4,5},{5,6},{6,7},{7,4},{8,9},{9,10},{10,1... | collective-permute-start | bytes 3932168 | tf_op jit(solution)/shard_map/ppermute | solution.py:68
  98.9 1.7 copy-done
  105.4 1.5 project_student.6
  106.9 1.7 project_teacher.4
  108.7 1.7 project_teacher.5
  110.4 1.7 project_teacher.6
  112.1 9.2 %collective-permute-done.8.refs_0_ = bf16[128,3584]{1,0:T(8,128)(2,1)S(1)} collective-permute-done((bf16[128,3584]{1,0:T(8,128)(2,1)S(1)}, bf16[128,3584]{1,0:T(8,128)(2,1)S(1)}, u32[]{:S(2)}, u32[]{:S(2)}) %collective-permute-start.8) | collective-permute-done | bytes 917536 | tf_op jit(solution)/shard_map/ppermute | solution.py:68
  122.7 1.5 project_student.7
  124.2 1.7 project_teacher.7
  126.7 3.5 %collective-permute-start.14 = (f32[13,8,128]{2,1,0:T(8,128)S(1)}, f32[13,8,128]{2,1,0:T(8,128)S(1)}, u32[]{:S(2)}, u32[]{:S(2)}) collective-permute-start(f32[13,8,128]{2,1,0:T(8,128)S(1)} %pack_sums.1.refs_0_), channel_id=1, source_target_pairs={{0,12},{4,0},{8,4},{12,8},{1,13},{5,1},{9,5},{13,9},{2,14},{6,2},{... | collective-permute-start | bytes 159752 | tf_op jit(solution)/shard_map/ppermute | solution.py:490
  132.0 4.0 %collective-permute-done.15.refs_2_ = f32[13,8,128]{2,1,0:T(8,128)S(1)} collective-permute-done((f32[13,8,128]{2,1,0:T(8,128)S(1)}, f32[13,8,128]{2,1,0:T(8,128)S(1)}, u32[]{:S(2)}, u32[]{:S(2)}) %collective-permute-start.15) | collective-permute-done | bytes 53280 | tf_op jit(solution)/shard_map/ppermute | solution.py:490
  136.3 2.9 %collective-permute-start.18 = (f32[16,8,128]{2,1,0:T(8,128)S(1)}, f32[16,8,128]{2,1,0:T(8,128)S(1)}, u32[]{:S(2)}, u32[]{:S(2)}) collective-permute-start(f32[16,8,128]{2,1,0:T(8,128)S(1)} %merge_sums.1.refs_0_), channel_id=1, source_target_pairs={{0,2},{1,3},{2,0},{3,1},{4,6},{5,7},{6,4},{7,5},{8,10},{9,11},{10,... | collective-permute-start | bytes 196616 | tf_op jit(solution)/shard_map/ppermute | solution.py:490
  140.5 1.6 collective-permute-done.18.refs_2_
  142.1 2.5 %collective-permute-done.19.refs_3_ = f32[16,8,128]{2,1,0:T(8,128)S(1)} collective-permute-done((f32[16,8,128]{2,1,0:T(8,128)S(1)}, f32[16,8,128]{2,1,0:T(8,128)S(1)}, u32[]{:S(2)}, u32[]{:S(2)}) %collective-permute-start.19) | collective-permute-done | bytes 65568 | tf_op jit(solution)/shard_map/ppermute | solution.py:490
  144.6 3.2 %slopes.1 = (bf16[1024,512]{1,0:T(8,128)(2,1)S(1)}, f32[2,16,4,64]{3,2,1,0:T(4,128)S(1)}) custom-call(s32[19]{0:T(128)S(1)} %pad_add_fusion.3.order_ref, f32[16,8,128]{2,1,0:T(8,128)S(1)} %merge_sums.1.refs_0_, f32[16,8,128]{2,1,0:T(8,128)S(1)} %collective-permute-done.17.refs_1_, f32[16,8,128]{2,1,0:T(8,128)S(1)} %collective-permute-done.18.refs_2_, ...), custom_call_target="tpu_custom_call" | custom-call | flops 20971520 | bytes 5242880 | tf_op jit(solution)/shard_map/slopes/pallas_call | solution.py:273
  147.8 2.6 %gradient_blocks.3 = bf16[4,448,512]{2,1,0:T(8,128)(2,1)S(1)} custom-call(s32[2,4]{1,0:T(2,128)S(1)} %pad_add_fusion.2.blocks_ref, bf16[3584,256]{1,0:T(8,128)(2,1)S(1)} %flipped.4.refs_0_, bf16[3584,256]{1,0:T(8,128)(2,1)S(1)} %flipped.5.refs_1_, bf16[3584,256]{1,0:T(8,128)(2,1)S(1)} %flipped.7.refs_2_, bf16[3584,256]{1,0:T(8,128)(2,1)S(1)} %flipped.6.refs_3_, ...), custom_call_target="tpu_custom_call" | custom-call | flops 1879048192 | bytes 5505024 | tf_op jit(solution)/shard_map/gradient_blocks/pallas_call | solution.py:339
  150.5 3.8 %collective-permute-done.20.refs_5_ = bf16[4,448,512]{2,1,0:T(8,128)(2,1)S(1)} collective-permute-done((bf16[4,448,512]{2,1,0:T(8,128)(2,1)S(1)}, bf16[4,448,512]{2,1,0:T(8,128)(2,1)S(1)}, u32[]{:S(2)}, u32[]{:S(2)}) %collective-permute-start.20) | collective-permute-done | bytes 1835040 | tf_op jit(solution)/shard_map/ppermute | solution.py:496
  154.3 2.1 %gradient_blocks.4 = (bf16[1,448,512]{2,1,0:T(8,128)(2,1)}, bf16[1,448,512]{2,1,0:T(8,128)(2,1)S(1)}, bf16[1,448,512]{2,1,0:T(8,128)(2,1)S(1)}) custom-call(s32[2,3]{1,0:T(2,128)S(1)} %pad_add_fusion.1.blocks_ref, bf16[3584,256]{1,0:T(8,128)(2,1)S(1)} %flipped.4.refs_0_, bf16[3584,256]{1,0:T(8,128)(2,1)S(1)} %flipped.5.refs_1_, ...), custom_call_target="tpu_custom_call" | custom-call | flops 1409286144 | bytes 4128768 | tf_op jit(solution)/shard_map/gradient_blocks/pallas_call | solution.py:339
  157.7 2.2 %collective-permute-start.22 = (bf16[1,448,512]{2,1,0:T(8,128)(2,1)S(1)}, bf16[1,448,512]{2,1,0:T(8,128)(2,1)S(1)}, u32[]{:S(2)}, u32[]{:S(2)}) collective-permute-start(bf16[1,448,512]{2,1,0:T(8,128)(2,1)S(1)} %get-tuple-element.127), channel_id=1, source_target_pairs={{0,32},{32,64},{64,96},{96,0},{1,33},{33,65},{65,97},{97,1},{2,34}... | collective-permute-start | bytes 1376264 | tf_op jit(solution)/shard_map/ppermute | solution.py:504
  161.2 19.8 %all_to_all.5 = f32[32,1,256]{2,1,0:T(1,128)S(1)} all-to-all(f32[32,1,256]{2,1,0:T(1,128)S(1)} %reshape.42), channel_id=1, replica_groups=mesh['role'=2,'ylo'=2,'core'=2,'cx'=4,'cz'=4] {'role','cx','cz'}, dimensions={0} | all-to-all | bytes 65536 | tf_op jit(solution)/shard_map/all_to_all | solution.py:509
  (90 shorter events, 27.6 us)
Async XLA Ops:
  0.6 10.6 %copy-start.5 = (s32[1,3]{1,0:T(1,128)S(1)}, s32[1,3]{1,0:T(1,128)}, u32[]{:S(2)}) copy-start(s32[1,3]{1,0:T(1,128)} %constant.133) | copy-start | bytes 40
  0.6 4.0 %copy-start.1 = (bf16[1,128,3584]{2,1,0:T(8,128)(2,1)S(1)}, bf16[1,128,3584]{2,1,0:T(8,128)(2,1)}, u32[]{:S(2)}) copy-start(bf16[1,128,3584]{2,1,0:T(8,128)(2,1)} %param.12) | copy-start | bytes 2752516
  0.7 4.0 %copy-start.2 = (f32[3584]{0:T(1024)S(1)}, f32[3584]{0:T(1024)}, u32[]{:S(2)}) copy-start(f32[3584]{0:T(1024)} %param.14) | copy-start | bytes 43012
  0.7 10.7 %copy-start.3 = (s32[1,128,4]{1,2,0:T(4,128)S(1)}, s32[1,128,4]{1,2,0:T(4,128)}, u32[]{:S(2)}) copy-start(s32[1,128,4]{1,2,0:T(4,128)} %param.18) | copy-start | bytes 6148
  0.7 10.7 %copy-start.4 = (s32[1,128]{1,0:T(1,128)S(1)}, s32[1,128]{1,0:T(1,128)}, u32[]{:S(2)}) copy-start(s32[1,128]{1,0:T(1,128)} %param.17) | copy-start | bytes 1540
  4.9 8.8 %collective-permute-start = (bf16[64,3584]{1,0:T(8,128)(2,1)S(1)}, bf16[64,3584]{1,0:T(8,128)(2,1)S(1)}, u32[]{:S(2)}, u32[]{:S(2)}) collective-permute-start(bf16[64,3584]{1,0:T(8,128)(2,1)S(1)} %fusion.5), channel_id=1, source_target_pairs={{0,12},{1,13},{2,14},{3,15},{4,0},{5,1},{6,2},{7,3},{8,4},{9,5},{1... | collective-permute-start | bytes 1376264 | tf_op jit(solution)/shard_map/ppermute | solution.py:68
  7.7 9.7 %collective-permute-start.1 = (bf16[64,3584]{1,0:T(8,128)(2,1)S(1)}, bf16[64,3584]{1,0:T(8,128)(2,1)S(1)}, u32[]{:S(2)}, u32[]{:S(2)}) collective-permute-start(bf16[64,3584]{1,0:T(8,128)(2,1)S(1)} %fusion.5), channel_id=1, source_target_pairs={{0,4},{1,5},{2,6},{3,7},{4,8},{5,9},{6,10},{7,11},{8,12},{9,13},{1... | collective-permute-start | bytes 1376264 | tf_op jit(solution)/shard_map/ppermute | solution.py:68
  7.7 13.0 %collective-permute-start.2 = (bf16[64,5120]{1,0:T(8,128)(2,1)S(1)}, bf16[64,5120]{1,0:T(8,128)(2,1)S(1)}, u32[]{:S(2)}, u32[]{:S(2)}) collective-permute-start(bf16[64,5120]{1,0:T(8,128)(2,1)S(1)} %fusion.2), channel_id=1, source_target_pairs={{0,12},{1,13},{2,14},{3,15},{4,0},{5,1},{6,2},{7,3},{8,4},{9,5},{1... | collective-permute-start | bytes 1966088 | tf_op jit(solution)/shard_map/ppermute | solution.py:68
  10.9 13.5 %collective-permute-start.3 = (bf16[64,5120]{1,0:T(8,128)(2,1)S(1)}, bf16[64,5120]{1,0:T(8,128)(2,1)S(1)}, u32[]{:S(2)}, u32[]{:S(2)}) collective-permute-start(bf16[64,5120]{1,0:T(8,128)(2,1)S(1)} %fusion.2), channel_id=1, source_target_pairs={{0,4},{1,5},{2,6},{3,7},{4,8},{5,9},{6,10},{7,11},{8,12},{9,13},{1... | collective-permute-start | bytes 1966088 | tf_op jit(solution)/shard_map/ppermute | solution.py:68
  17.4 8.5 %collective-permute-start.4 = (bf16[64,3584]{1,0:T(8,128)(2,1)S(1)}, bf16[64,3584]{1,0:T(8,128)(2,1)S(1)}, u32[]{:S(2)}, u32[]{:S(2)}) collective-permute-start(bf16[64,3584]{1,0:T(8,128)(2,1)S(1)} %collective-permute-done), channel_id=1, source_target_pairs={{0,12},{1,13},{2,14},{3,15},{4,0},{5,1},{6,2},{7,3},{8,4},{9,5},{1... | collective-permute-start | bytes 1376264 | tf_op jit(solution)/shard_map/ppermute | solution.py:68
  25.9 24.8 %collective-permute-start.5 = (bf16[256,3584]{1,0:T(8,128)(2,1)S(1)}, bf16[256,3584]{1,0:T(8,128)(2,1)S(1)}, u32[]{:S(2)}, u32[]{:S(2)}) collective-permute-start(bf16[256,3584]{1,0:T(8,128)(2,1)S(1)} %constant_dynamic-update-slice_fusion.refs_0_), channel_id=1, source_target_pairs={{0,3},{1,0},{2,1},{3,2},{4,7},{5,4},{6,5},{7,6},{8,11},{9,8},{10,9... | collective-permute-start | bytes 5505032 | tf_op jit(solution)/shard_map/ppermute | solution.py:68
  30.0 29.7 %collective-permute-start.6 = (bf16[256,3584]{1,0:T(8,128)(2,1)S(1)}, bf16[256,3584]{1,0:T(8,128)(2,1)S(1)}, u32[]{:S(2)}, u32[]{:S(2)}) collective-permute-start(bf16[256,3584]{1,0:T(8,128)(2,1)S(1)} %constant_dynamic-update-slice_fusion.refs_0_), channel_id=1, source_target_pairs={{0,1},{1,2},{2,3},{3,0},{4,5},{5,6},{6,7},{7,4},{8,9},{9,10},{10,1... | collective-permute-start | bytes 5505032 | tf_op jit(solution)/shard_map/ppermute | solution.py:68
  30.1 19.1 %collective-permute-start.7 = (bf16[64,5120]{1,0:T(8,128)(2,1)S(1)}, bf16[64,5120]{1,0:T(8,128)(2,1)S(1)}, u32[]{:S(2)}, u32[]{:S(2)}) collective-permute-start(bf16[64,5120]{1,0:T(8,128)(2,1)S(1)} %collective-permute-done.3), channel_id=1, source_target_pairs={{0,4},{1,5},{2,6},{3,7},{4,8},{5,9},{6,10},{7,11},{8,12},{9,13},{1... | collective-permute-start | bytes 1966088 | tf_op jit(solution)/shard_map/ppermute | solution.py:68
  31.1 67.5 %slice-start = ((s8[5242880]{0:T(1024)(128)(4,1)}), s8[4194304]{0:T(1024)(128)(4,1)S(1)}, s32[]{:S(2)}) async-start(s8[5242880]{0:T(1024)(128)(4,1)} %bitcast.29), calls=%async_computation.1 | async-start | bytes 8388608
  59.8 38.7 %slice-start.1 = ((s8[5242880]{0:T(1024)(128)(4,1)}), s8[1048576]{0:T(1024)(128)(4,1)S(1)}, s32[]{:S(2)}) async-start(s8[5242880]{0:T(1024)(128)(4,1)} %bitcast.29), calls=%async_computation.2 | async-start | bytes 2097152
  59.9 31.7 %collective-permute-start.10 = (bf16[256,5120]{1,0:T(8,128)(2,1)S(1)}, bf16[256,5120]{1,0:T(8,128)(2,1)S(1)}, u32[]{:S(2)}, u32[]{:S(2)}) collective-permute-start(bf16[256,5120]{1,0:T(8,128)(2,1)S(1)} %constant_dynamic-update-slice_fusion.4.refs_0_), channel_id=1, source_target_pairs={{0,3},{1,0},{2,1},{3,2},{4,7},{5,4},{6,5},{7,6},{8,11},{9,8},{10,9... | collective-permute-start | bytes 7864328 | tf_op jit(solution)/shard_map/ppermute | solution.py:68
  60.9 32.9 %collective-permute-start.11 = (bf16[256,5120]{1,0:T(8,128)(2,1)S(1)}, bf16[256,5120]{1,0:T(8,128)(2,1)S(1)}, u32[]{:S(2)}, u32[]{:S(2)}) collective-permute-start(bf16[256,5120]{1,0:T(8,128)(2,1)S(1)} %constant_dynamic-update-slice_fusion.4.refs_0_), channel_id=1, source_target_pairs={{0,1},{1,2},{2,3},{3,0},{4,5},{5,6},{6,7},{7,4},{8,9},{9,10},{10,1... | collective-permute-start | bytes 7864328 | tf_op jit(solution)/shard_map/ppermute | solution.py:68
  93.8 28.9 %collective-permute-start.12 = (bf16[128,5120]{1,0:T(8,128)(2,1)S(1)}, bf16[128,5120]{1,0:T(8,128)(2,1)S(1)}, u32[]{:S(2)}, u32[]{:S(2)}) collective-permute-start(bf16[128,5120]{1,0:T(8,128)(2,1)S(1)} %slice.14), channel_id=1, source_target_pairs={{0,3},{1,0},{2,1},{3,2},{4,7},{5,4},{6,5},{7,6},{8,11},{9,8},{10,9... | collective-permute-start | bytes 3932168 | tf_op jit(solution)/shard_map/ppermute | solution.py:68
  94.0 28.7 %collective-permute-start.13 = (bf16[128,5120]{1,0:T(8,128)(2,1)S(1)}, bf16[128,5120]{1,0:T(8,128)(2,1)S(1)}, u32[]{:S(2)}, u32[]{:S(2)}) collective-permute-start(bf16[128,5120]{1,0:T(8,128)(2,1)S(1)} %slice.15), channel_id=1, source_target_pairs={{0,1},{1,2},{2,3},{3,0},{4,5},{5,6},{6,7},{7,4},{8,9},{9,10},{10,1... | collective-permute-start | bytes 3932168 | tf_op jit(solution)/shard_map/ppermute | solution.py:68
  96.2 25.2 %collective-permute-start.8 = (bf16[128,3584]{1,0:T(8,128)(2,1)S(1)}, bf16[128,3584]{1,0:T(8,128)(2,1)S(1)}, u32[]{:S(2)}, u32[]{:S(2)}) collective-permute-start(bf16[128,3584]{1,0:T(8,128)(2,1)S(1)} %slice.12), channel_id=1, source_target_pairs={{0,3},{1,0},{2,1},{3,2},{4,7},{5,4},{6,5},{7,6},{8,11},{9,8},{10,9... | collective-permute-start | bytes 2752520 | tf_op jit(solution)/shard_map/ppermute | solution.py:68
  97.5 25.2 %collective-permute-start.9 = (bf16[128,3584]{1,0:T(8,128)(2,1)S(1)}, bf16[128,3584]{1,0:T(8,128)(2,1)S(1)}, u32[]{:S(2)}, u32[]{:S(2)}) collective-permute-start(bf16[128,3584]{1,0:T(8,128)(2,1)S(1)} %slice.13), channel_id=1, source_target_pairs={{0,1},{1,2},{2,3},{3,0},{4,5},{5,6},{6,7},{7,4},{8,9},{9,10},{10,1... | collective-permute-start | bytes 2752520 | tf_op jit(solution)/shard_map/ppermute | solution.py:68
  98.6 2.0 %copy-start = (bf16[4,3584,128]{2,1,0:T(8,128)(2,1)S(1)}, bf16[4,3584,128]{2,1,0:T(8,128)(2,1)}, u32[]{:S(2)}) copy-start(bf16[4,3584,128]{2,1,0:T(8,128)(2,1)} %array_ref.3) | copy-start | bytes 11010052
  126.7 5.3 %collective-permute-start.14 = (f32[13,8,128]{2,1,0:T(8,128)S(1)}, f32[13,8,128]{2,1,0:T(8,128)S(1)}, u32[]{:S(2)}, u32[]{:S(2)}) collective-permute-start(f32[13,8,128]{2,1,0:T(8,128)S(1)} %pack_sums.1.refs_0_), channel_id=1, source_target_pairs={{0,12},{4,0},{8,4},{12,8},{1,13},{5,1},{9,5},{13,9},{2,14},{6,2},{... | collective-permute-start | bytes 159752 | tf_op jit(solution)/shard_map/ppermute | solution.py:490
  130.2 5.7 %collective-permute-start.15 = (f32[13,8,128]{2,1,0:T(8,128)S(1)}, f32[13,8,128]{2,1,0:T(8,128)S(1)}, u32[]{:S(2)}, u32[]{:S(2)}) collective-permute-start(f32[13,8,128]{2,1,0:T(8,128)S(1)} %pack_sums.1.refs_0_), channel_id=1, source_target_pairs={{0,8},{4,12},{8,0},{12,4},{1,9},{5,13},{9,1},{13,5},{2,10},{6,14},... | collective-permute-start | bytes 159752 | tf_op jit(solution)/shard_map/ppermute | solution.py:490
  130.2 5.9 %collective-permute-start.16 = (f32[13,8,128]{2,1,0:T(8,128)S(1)}, f32[13,8,128]{2,1,0:T(8,128)S(1)}, u32[]{:S(2)}, u32[]{:S(2)}) collective-permute-start(f32[13,8,128]{2,1,0:T(8,128)S(1)} %pack_sums.1.refs_0_), channel_id=1, source_target_pairs={{0,4},{4,8},{8,12},{12,0},{1,5},{5,9},{9,13},{13,1},{2,6},{6,10},{... | collective-permute-start | bytes 159752 | tf_op jit(solution)/shard_map/ppermute | solution.py:490
  136.2 4.3 %collective-permute-start.17 = (f32[16,8,128]{2,1,0:T(8,128)S(1)}, f32[16,8,128]{2,1,0:T(8,128)S(1)}, u32[]{:S(2)}, u32[]{:S(2)}) collective-permute-start(f32[16,8,128]{2,1,0:T(8,128)S(1)} %merge_sums.1.refs_0_), channel_id=1, source_target_pairs={{0,3},{1,0},{2,1},{3,2},{4,7},{5,4},{6,5},{7,6},{8,11},{9,8},{10,9... | collective-permute-start | bytes 196616 | tf_op jit(solution)/shard_map/ppermute | solution.py:490
  136.3 5.8 %collective-permute-start.18 = (f32[16,8,128]{2,1,0:T(8,128)S(1)}, f32[16,8,128]{2,1,0:T(8,128)S(1)}, u32[]{:S(2)}, u32[]{:S(2)}) collective-permute-start(f32[16,8,128]{2,1,0:T(8,128)S(1)} %merge_sums.1.refs_0_), channel_id=1, source_target_pairs={{0,2},{1,3},{2,0},{3,1},{4,6},{5,7},{6,4},{7,5},{8,10},{9,11},{10,... | collective-permute-start | bytes 196616 | tf_op jit(solution)/shard_map/ppermute | solution.py:490
  139.1 5.5 %collective-permute-start.19 = (f32[16,8,128]{2,1,0:T(8,128)S(1)}, f32[16,8,128]{2,1,0:T(8,128)S(1)}, u32[]{:S(2)}, u32[]{:S(2)}) collective-permute-start(f32[16,8,128]{2,1,0:T(8,128)S(1)} %merge_sums.1.refs_0_), channel_id=1, source_target_pairs={{0,1},{1,2},{2,3},{3,0},{4,5},{5,6},{6,7},{7,4},{8,9},{9,10},{10,1... | collective-permute-start | bytes 196616 | tf_op jit(solution)/shard_map/ppermute | solution.py:490
  150.4 3.9 %collective-permute-start.20 = (bf16[4,448,512]{2,1,0:T(8,128)(2,1)S(1)}, bf16[4,448,512]{2,1,0:T(8,128)(2,1)S(1)}, u32[]{:S(2)}, u32[]{:S(2)}) collective-permute-start(bf16[4,448,512]{2,1,0:T(8,128)(2,1)S(1)} %gradient_blocks.3), channel_id=1, source_target_pairs={{0,16},{16,0},{1,17},{17,1},{2,18},{18,2},{3,19},{19,3},{4,20},{20... | collective-permute-start | bytes 5505032 | tf_op jit(solution)/shard_map/ppermute | solution.py:496
  156.4 25.5 %collective-permute-start.21 = (bf16[1,448,512]{2,1,0:T(8,128)(2,1)}, bf16[1,448,512]{2,1,0:T(8,128)(2,1)S(1)}, u32[]{:S(2)}, u32[]{:S(2)}) collective-permute-start(bf16[1,448,512]{2,1,0:T(8,128)(2,1)} %get-tuple-element.126), channel_id=1, source_target_pairs={{0,64},{32,96},{64,0},{96,32},{1,65},{33,97},{65,1},{97,33},{2,66}... | collective-permute-start | bytes 1376264 | tf_op jit(solution)/shard_map/ppermute | solution.py:504
  157.7 24.2 %collective-permute-start.22 = (bf16[1,448,512]{2,1,0:T(8,128)(2,1)S(1)}, bf16[1,448,512]{2,1,0:T(8,128)(2,1)S(1)}, u32[]{:S(2)}, u32[]{:S(2)}) collective-permute-start(bf16[1,448,512]{2,1,0:T(8,128)(2,1)S(1)} %get-tuple-element.127), channel_id=1, source_target_pairs={{0,32},{32,64},{64,96},{96,0},{1,33},{33,65},{65,97},{97,1},{2,34}... | collective-permute-start | bytes 1376264 | tf_op jit(solution)/shard_map/ppermute | solution.py:504
  159.9 22.0 %collective-permute-start.23 = (bf16[1,448,512]{2,1,0:T(8,128)(2,1)S(1)}, bf16[1,448,512]{2,1,0:T(8,128)(2,1)S(1)}, u32[]{:S(2)}, u32[]{:S(2)}) collective-permute-start(bf16[1,448,512]{2,1,0:T(8,128)(2,1)S(1)} %get-tuple-element.128), channel_id=1, source_target_pairs={{0,96},{32,0},{64,32},{96,64},{1,97},{33,1},{65,33},{97,65},{2,98}... | collective-permute-start | bytes 1376264 | tf_op jit(solution)/shard_map/ppermute | solution.py:504

commit v3 on v2

--- a/solution.py
+++ b/solution.py
@@ -72,10 +72,55 @@
     return moved(block, phase, -1), moved(block, phase, 1)
 
 
-def normalize(states, gain):
-    values = states.astype(jnp.float32)
-    factor = lax.rsqrt(jnp.mean(values * values, axis=-1, keepdims=True) + epsilon)
-    return (values * factor * gain).astype(jnp.bfloat16)
+def normalized_kernel(role_ref, *refs):
+    for states_ref, gain_ref, out_ref in zip(refs[:2], refs[2:4], refs[4:]):
+        values = states_ref[0].astype(jnp.float32)
+        factor = lax.rsqrt(jnp.mean(values * values, axis=-1, keepdims=True) + epsilon)
+        out_ref[...] = (values * factor * gain_ref[...]).astype(jnp.bfloat16)
+
+
+def normalized(role, student_states, teacher_states, student_gain, teacher_gain):
+    both = (student_states, teacher_states)
+    half = student_states.shape[1] // 2
+    widths = [states.shape[2] for states in both]
+    return pl.pallas_call(
+        normalized_kernel,
+        grid_spec=pltpu.PrefetchScalarGridSpec(
+            num_scalar_prefetch=1,
+            grid=(1,),
+            in_specs=[
+                pl.BlockSpec((1, half, width), lambda step, role: (0, role[0], 0))
+                for width in widths
+            ]
+            + [pl.BlockSpec((1, width), lambda step, role: (0, 0)) for width in widths],
+            out_specs=[pl.BlockSpec((half, width), lambda step, role: (0, 0)) for width in widths],
+        ),
+        out_shape=[jax.ShapeDtypeStruct((half, width), jnp.bfloat16) for width in widths],
+        **small_kernel("normalized", bytes_accessed=4 * half * sum(widths), limit=16 << 20),
+    )(
+        role,
+        *(pltpu.with_memory_space_constraint(states, pltpu.HBM) for states in both),
+        student_gain[None, :],
+        teacher_gain[None, :],
+    )
+
+
+def stack_kernel(*refs):
+    *pieces, out_ref = refs
+    height = pieces[0].shape[0]
+    for number, piece in enumerate(pieces):
+        out_ref[number * height : (number + 1) * height, :] = piece[...]
+
+
+def stacked(pieces):
+    height, width = pieces[0].shape
+    return pl.pallas_call(
+        stack_kernel,
+        in_specs=[VMEM] * len(pieces),
+        out_specs=VMEM,
+        out_shape=pltpu.VMEM((len(pieces) * height, width), pieces[0].dtype),
+        **small_kernel("stacked", bytes_accessed=4 * len(pieces) * height * width),
+    )(*pieces)
 
 
 def joined(pieces, span):
@@ -398,9 +443,6 @@
     rows_here = teacher_states.shape[1]
     half = rows_here // 2
 
-    def own_half(states):
-        return lax.dynamic_slice_in_dim(states[0], role * half, half, axis=0)
-
     order, place = places()
     order = jnp.concatenate(
         [order, jnp.stack([role, lax.axis_index(CTX) * columns, core]).astype(jnp.int32)]
@@ -428,29 +470,22 @@
     info = jnp.concatenate(
         [targets[0].T, segments, jnp.zeros((BOOKS - 1, rows_here), jnp.int32)]
     ).astype(jnp.float32)
-    student_rows = normalize(own_half(student_states), student_gain)
-    teacher_rows = normalize(own_half(teacher_states), teacher_gain)
+    student_rows, teacher_rows = normalized(
+        role.reshape(1), student_states, teacher_states, student_gain, teacher_gain
+    )
     tie = lax.optimization_barrier
-    student_rows, teacher_rows = tie((student_rows, teacher_rows))
 
     student_near = neighbours(student_rows, 0)
+    teacher_after, teacher_before = neighbours(teacher_rows, 0)
+    teacher_opposite = moved(teacher_rows, 0, 2)
     student_after, student_before, order, place, info, *blocks = tie(
         (*student_near, order, place, info, *blocks)
     )
     student_opposite = moved(student_after, 0, -1)
-    teacher_near = neighbours(teacher_rows, 0)
-    teacher_after, teacher_before, student_after = tie((*teacher_near, student_after))
-    teacher_opposite = moved(teacher_before, 0, 1)
-    student_line = jnp.concatenate(
-        [student_rows, student_after, student_opposite, student_before]
-    )
-    student_after, student_before, teacher_opposite = tie(
-        (*neighbours(student_line, 1), teacher_opposite)
-    )
-    teacher_line = jnp.concatenate(
-        [teacher_rows, teacher_after, teacher_opposite, teacher_before]
-    )
+    student_line = stacked([student_rows, student_after, student_opposite, student_before])
+    teacher_line = stacked([teacher_rows, teacher_after, teacher_opposite, teacher_before])
     teacher_after, teacher_before = tie(neighbours(teacher_line, 1))
+    student_after, student_before = tie(neighbours(student_line, 1))
 
     def relayed(after, before):
         middle = after.shape[0] // 2
@@ -472,16 +507,13 @@
     flipped_rows = [flipped(student_parts[turn]) for turn in early]
     teacher_found = [project_teacher(turn) for turn in early]
     student_found = [project_student(turn) for turn in early]
-    (
-        student_parts[2],
-        teacher_parts[2],
-        flipped_rows,
-        teacher_found,
-        student_found,
-    ) = tie((student_parts[2], teacher_parts[2], flipped_rows, teacher_found, student_found))
+    teacher_parts[2], flipped_rows, teacher_found, student_found = tie(
+        (teacher_parts[2], flipped_rows, teacher_found, student_found)
+    )
+    teacher_found.insert(2, project_teacher(2))
+    teacher_found[2], student_parts[2] = tie((teacher_found[2], student_parts[2]))
+    student_found.insert(2, project_student(2))
     flipped_rows.insert(2, flipped(student_parts[2]))
-    student_found.insert(2, project_student(2))
-    teacher_found.insert(2, project_teacher(2))
     student_raw, student_sums = zip(*student_found)
     teacher_scaled, teacher_sums = zip(*teacher_found)
     sent = pack_sums(place, info, teacher_sums, student_sums)

time: 184 us -> 167 us (0.908)
  waiting for transfers between devices: 99.1 us -> 74.4 us
  starting transfers between devices: 28.7 us -> 35.7 us
  other arithmetic: 4.58 us -> 0.45 us
  Pallas kernels: 26.6 us -> 29.7 us
    ppermute x14, waiting for transfers between devices: 85.4 us -> 61.1 us  [moved(): return lax.ppermute(value, TURN, line_pairs(phase, step))]
    ppermute x14, starting transfers between devices: 17.7 us -> 25.3 us  [moved(): return lax.ppermute(value, TURN, line_pairs(phase, step))]
    pallas_call x0 -> x3, Pallas kernels: none -> 3.15 us  [the longest x1 1.84 us: normalized(): pl.pallas_call(normalized_kernel, grid_spec=pltpu.PrefetchScalarGridSpec(...]
    reduce_sum x2 -> x0, other arithmetic: 2.61 us -> none  [normalize(): jnp.mean(values * values, axis=-1, keepdims=True) + epsilon]
  transfers between devices with their start and end apart: 24 -> 24, of which waited for: 19 -> 14; matrix products, arithmetic and copies ran while one was open for 1% -> 1% of each run, Pallas kernels for 7% -> 10%
where the time goes in v3:
time: 167 us; the launch traced here: 166 us
  waiting for transfers between devices  74.4 us (45%)
  starting transfers between devices  35.7 us (21%)
  Pallas kernels  29.7 us (18%)
  blocking collectives  20.8 us (12%)
  local copies, waits for them, and re-layouts  4.38 us (3%)
    ppermute x14, waiting for transfers between devices, moved(): return lax.ppermute(value, TURN, line_pairs(phase, step))  61.1 us
    ppermute x14, starting transfers between devices, moved(): return lax.ppermute(value, TURN, line_pairs(phase, step))  25.3 us
    all_to_all x1, blocking collectives, on_device(): lax.all_to_all(terms.reshape(2 * count, 1, BOOKS * half), ('role', *CTX),...  20.8 us
    pallas_call x8, Pallas kernels, project(): pl.pallas_call(functools.partial(project_kernel, is_teacher), in_specs=[V...  12.8 us
    ppermute x6, waiting for transfers between devices, on_device(): lax.ppermute(sent, axis, back(shift))  9.53 us
    ppermute x6, starting transfers between devices, on_device(): lax.ppermute(sent, axis, back(shift))  6.76 us
    pallas_call x3, Pallas kernels, gradient_blocks(): pl.pallas_call(functools.partial(gradient_kernel, taken is not None), in_...  5.93 us
    ppermute x1, waiting for transfers between devices, on_device(): taken = lax.ppermute(given, 'core', [(0, 1), (1, 0)])  3.77 us
  transfers between devices with their start and end apart: 24, of which 14 were waited for; matrix products, arithmetic and copies ran while one was open for 1% of the time, Pallas kernels for 10%

profile of v3, /device:TPU:24, one launch (start us, length us, event | category | flops | bytes accessed | tf_op | source)
XLA Modules:
  0.0 166.4 jit_solution(14183002921983727239)
XLA Ops:
  2.1 1.8 %normalized.1 = (bf16[64,3584]{1,0:T(8,128)(2,1)S(1)}, bf16[64,5120]{1,0:T(8,128)(2,1)S(1)}) custom-call(s32[1]{0:T(128)} %bitcast.role_ref, bf16[1,128,3584]{2,1,0:T(8,128)(2,1)} %refs_0_.1, bf16[1,128,5120]{2,1,0:T(8,128)(2,1)} %refs_1_.1, f32[1,3584]{1,0:T(1,128)S(1)} %broadcast_in_dim.9.refs_2_, f32[1,5120]{1,0:T(1,128)S(1)} %bitcast.24), custom_call_target="tpu_custom_call" | custom-call | bytes 2228224 | tf_op jit(solution)/shard_map/normalized/pallas_call | solution.py:86
  3.9 2.8 %collective-permute-start.2 = (bf16[64,5120]{1,0:T(8,128)(2,1)S(1)}, bf16[64,5120]{1,0:T(8,128)(2,1)S(1)}, u32[]{:S(2)}, u32[]{:S(2)}) collective-permute-start(bf16[64,5120]{1,0:T(8,128)(2,1)S(1)} %get-tuple-element.68.refs_0_), channel_id=1, source_target_pairs={{0,12},{1,13},{2,14},{3,15},{4,0},{5,1},{6,2},{7,3},{8,4},{9,5},{1... | collective-permute-start | bytes 1966088 | tf_op jit(solution)/shard_map/ppermute | solution.py:68
  8.5 2.4 %collective-permute-start = (bf16[64,3584]{1,0:T(8,128)(2,1)S(1)}, bf16[64,3584]{1,0:T(8,128)(2,1)S(1)}, u32[]{:S(2)}, u32[]{:S(2)}) collective-permute-start(bf16[64,3584]{1,0:T(8,128)(2,1)S(1)} %get-tuple-element.64.refs_0_), channel_id=1, source_target_pairs={{0,12},{1,13},{2,14},{3,15},{4,0},{5,1},{6,2},{7,3},{8,4},{9,5},{1... | collective-permute-start | bytes 1376264 | tf_op jit(solution)/shard_map/ppermute | solution.py:68
  10.9 11.1 %collective-permute-done.2.refs_1_ = bf16[64,5120]{1,0:T(8,128)(2,1)S(1)} collective-permute-done((bf16[64,5120]{1,0:T(8,128)(2,1)S(1)}, bf16[64,5120]{1,0:T(8,128)(2,1)S(1)}, u32[]{:S(2)}, u32[]{:S(2)}) %collective-permute-start.2) | collective-permute-done | bytes 655392 | tf_op jit(solution)/shard_map/ppermute | solution.py:68
  21.9 3.9 %collective-permute-done.4.refs_3_ = bf16[64,5120]{1,0:T(8,128)(2,1)S(1)} collective-permute-done((bf16[64,5120]{1,0:T(8,128)(2,1)S(1)}, bf16[64,5120]{1,0:T(8,128)(2,1)S(1)}, u32[]{:S(2)}, u32[]{:S(2)}) %collective-permute-start.4) | collective-permute-done | bytes 655392 | tf_op jit(solution)/shard_map/ppermute | solution.py:68
  26.1 4.1 %collective-permute-start.5 = (bf16[256,5120]{1,0:T(8,128)(2,1)S(1)}, bf16[256,5120]{1,0:T(8,128)(2,1)S(1)}, u32[]{:S(2)}, u32[]{:S(2)}) collective-permute-start(bf16[256,5120]{1,0:T(8,128)(2,1)S(1)} %stacked.2.refs_0_), channel_id=1, source_target_pairs={{0,3},{1,0},{2,1},{3,2},{4,7},{5,4},{6,5},{7,6},{8,11},{9,8},{10,9... | collective-permute-start | bytes 7864328 | tf_op jit(solution)/shard_map/ppermute | solution.py:68
  31.5 12.8 %collective-permute-done.9.refs_2_ = bf16[64,3584]{1,0:T(8,128)(2,1)S(1)} collective-permute-done((bf16[64,3584]{1,0:T(8,128)(2,1)S(1)}, bf16[64,3584]{1,0:T(8,128)(2,1)S(1)}, u32[]{:S(2)}, u32[]{:S(2)}) %collective-permute-start.9) | collective-permute-done | bytes 458784 | tf_op jit(solution)/shard_map/ppermute | solution.py:68
  45.5 5.9 %collective-permute-start.10 = (bf16[256,3584]{1,0:T(8,128)(2,1)S(1)}, bf16[256,3584]{1,0:T(8,128)(2,1)S(1)}, u32[]{:S(2)}, u32[]{:S(2)}) collective-permute-start(bf16[256,3584]{1,0:T(8,128)(2,1)S(1)} %stacked.3.refs_0_), channel_id=1, source_target_pairs={{0,3},{1,0},{2,1},{3,2},{4,7},{5,4},{6,5},{7,6},{8,11},{9,8},{10,9... | collective-permute-start | bytes 5505032 | tf_op jit(solution)/shard_map/ppermute | solution.py:68
  51.4 12.9 %collective-permute-done.5.refs_0_ = bf16[256,5120]{1,0:T(8,128)(2,1)S(1)} collective-permute-done((bf16[256,5120]{1,0:T(8,128)(2,1)S(1)}, bf16[256,5120]{1,0:T(8,128)(2,1)S(1)}, u32[]{:S(2)}, u32[]{:S(2)}) %collective-permute-start.5) | collective-permute-done | bytes 2621472 | tf_op jit(solution)/shard_map/ppermute | solution.py:68
  64.3 3.8 %collective-permute-start.7 = (bf16[128,5120]{1,0:T(8,128)(2,1)S(1)}, bf16[128,5120]{1,0:T(8,128)(2,1)S(1)}, u32[]{:S(2)}, u32[]{:S(2)}) collective-permute-start(bf16[128,5120]{1,0:T(8,128)(2,1)S(1)} %slice.12), channel_id=1, source_target_pairs={{0,3},{1,0},{2,1},{3,2},{4,7},{5,4},{6,5},{7,6},{8,11},{9,8},{10,9... | collective-permute-start | bytes 3932168 | tf_op jit(solution)/shard_map/ppermute | solution.py:68
  68.3 15.6 %collective-permute-done.10.refs_0_ = bf16[256,3584]{1,0:T(8,128)(2,1)S(1)} collective-permute-done((bf16[256,3584]{1,0:T(8,128)(2,1)S(1)}, bf16[256,3584]{1,0:T(8,128)(2,1)S(1)}, u32[]{:S(2)}, u32[]{:S(2)}) %collective-permute-start.10) | collective-permute-done | bytes 1835040 | tf_op jit(solution)/shard_map/ppermute | solution.py:68
  84.0 3.8 %collective-permute-start.12 = (bf16[128,3584]{1,0:T(8,128)(2,1)S(1)}, bf16[128,3584]{1,0:T(8,128)(2,1)S(1)}, u32[]{:S(2)}, u32[]{:S(2)}) collective-permute-start(bf16[128,3584]{1,0:T(8,128)(2,1)S(1)} %slice.14), channel_id=1, source_target_pairs={{0,3},{1,0},{2,1},{3,2},{4,7},{5,4},{6,5},{7,6},{8,11},{9,8},{10,9... | collective-permute-start | bytes 2752520 | tf_op jit(solution)/shard_map/ppermute | solution.py:68
  88.5 1.7 copy-done
  90.4 1.7 %project_teacher.4 = (f32[4,128,256]{2,1,0:T(8,128)S(1)}, f32[8,256]{1,0:T(8,128)S(1)}) custom-call(bf16[256,5120]{1,0:T(8,128)(2,1)S(1)} %stacked.2.refs_0_, bf16[4,5120,128]{2,1,0:T(8,128)(2,1)S(1)} %held.2.refs_1_.refs_2_), custom_call_target="tpu_custom_call" | custom-call | flops 1342177280 | bytes 8388608 | tf_op jit(solution)/shard_map/project_teacher/pallas_call | solution.py:166
  92.7 1.5 project_student.4
  95.2 1.5 project_student.5
  96.7 1.5 project_student.6
  98.2 1.7 %project_teacher.5 = (f32[4,128,256]{2,1,0:T(8,128)S(1)}, f32[8,256]{1,0:T(8,128)S(1)}) custom-call(bf16[256,5120]{1,0:T(8,128)(2,1)S(1)} %collective-permute-done.5.refs_0_, bf16[4,5120,128]{2,1,0:T(8,128)(2,1)S(1)} %held.2.refs_1_.refs_2_), custom_call_target="tpu_custom_call" | custom-call | flops 1342177280 | bytes 8388608 | tf_op jit(solution)/shard_map/project_teacher/pallas_call | solution.py:166
  99.9 1.7 %project_teacher.6 = (f32[4,128,256]{2,1,0:T(8,128)S(1)}, f32[8,256]{1,0:T(8,128)S(1)}) custom-call(bf16[256,5120]{1,0:T(8,128)(2,1)S(1)} %collective-permute-done.6.refs_0_, bf16[4,5120,128]{2,1,0:T(8,128)(2,1)S(1)} %held.2.refs_1_.refs_2_), custom_call_target="tpu_custom_call" | custom-call | flops 1342177280 | bytes 8388608 | tf_op jit(solution)/shard_map/project_teacher/pallas_call | solution.py:166
  101.7 1.7 %project_teacher.7 = (f32[4,128,256]{2,1,0:T(8,128)S(1)}, f32[8,256]{1,0:T(8,128)S(1)}) custom-call(bf16[128,5120]{1,0:T(8,128)(2,1)S(1)} %collective-permute-done.7.refs_0_, bf16[128,5120]{1,0:T(8,128)(2,1)S(1)} %collective-permute-done.8.refs_1_, bf16[4,5120,128]{2,1,0:T(8,128)(2,1)S(1)} %held.2.refs_1_.refs_2_), custom_call_target="tpu_custom_call" | custom-call | flops 1342177280 | bytes 8388608 | tf_op jit(solution)/shard_map/project_teacher/pallas_call | solution.py:166
  103.4 4.4 %collective-permute-done.12.refs_0_ = bf16[128,3584]{1,0:T(8,128)(2,1)S(1)} collective-permute-done((bf16[128,3584]{1,0:T(8,128)(2,1)S(1)}, bf16[128,3584]{1,0:T(8,128)(2,1)S(1)}, u32[]{:S(2)}, u32[]{:S(2)}) %collective-permute-start.12) | collective-permute-done | bytes 917536 | tf_op jit(solution)/shard_map/ppermute | solution.py:68
  107.8 1.5 project_student.7
  112.3 1.9 %collective-permute-done.14.refs_1_ = f32[13,8,128]{2,1,0:T(8,128)S(1)} collective-permute-done((f32[13,8,128]{2,1,0:T(8,128)S(1)}, f32[13,8,128]{2,1,0:T(8,128)S(1)}, u32[]{:S(2)}, u32[]{:S(2)}) %collective-permute-start.14) | collective-permute-done | bytes 53280 | tf_op jit(solution)/shard_map/ppermute | solution.py:522
  114.2 2.4 %collective-permute-done.15.refs_2_ = f32[13,8,128]{2,1,0:T(8,128)S(1)} collective-permute-done((f32[13,8,128]{2,1,0:T(8,128)S(1)}, f32[13,8,128]{2,1,0:T(8,128)S(1)}, u32[]{:S(2)}, u32[]{:S(2)}) %collective-permute-start.15) | collective-permute-done | bytes 53280 | tf_op jit(solution)/shard_map/ppermute | solution.py:522
  117.2 3.5 %collective-permute-start.17 = (f32[16,8,128]{2,1,0:T(8,128)S(1)}, f32[16,8,128]{2,1,0:T(8,128)S(1)}, u32[]{:S(2)}, u32[]{:S(2)}) collective-permute-start(f32[16,8,128]{2,1,0:T(8,128)S(1)} %merge_sums.1.refs_0_), channel_id=1, source_target_pairs={{0,3},{1,0},{2,1},{3,2},{4,7},{5,4},{6,5},{7,6},{8,11},{9,8},{10,9... | collective-permute-start | bytes 196616 | tf_op jit(solution)/shard_map/ppermute | solution.py:522
  123.2 3.4 %collective-permute-done.18.refs_2_ = f32[16,8,128]{2,1,0:T(8,128)S(1)} collective-permute-done((f32[16,8,128]{2,1,0:T(8,128)S(1)}, f32[16,8,128]{2,1,0:T(8,128)S(1)}, u32[]{:S(2)}, u32[]{:S(2)}) %collective-permute-start.18) | collective-permute-done | bytes 65568 | tf_op jit(solution)/shard_map/ppermute | solution.py:522
  126.9 3.2 %slopes.1 = (bf16[1024,512]{1,0:T(8,128)(2,1)S(1)}, f32[2,16,4,64]{3,2,1,0:T(4,128)S(1)}) custom-call(s32[19]{0:T(128)S(1)} %pad_add_fusion.3.order_ref, f32[16,8,128]{2,1,0:T(8,128)S(1)} %merge_sums.1.refs_0_, f32[16,8,128]{2,1,0:T(8,128)S(1)} %collective-permute-done.17.refs_1_, f32[16,8,128]{2,1,0:T(8,128)S(1)} %collective-permute-done.18.refs_2_, ...), custom_call_target="tpu_custom_call" | custom-call | flops 20971520 | bytes 5242880 | tf_op jit(solution)/shard_map/slopes/pallas_call | solution.py:318
  130.1 2.6 %gradient_blocks.3 = bf16[4,448,512]{2,1,0:T(8,128)(2,1)S(1)} custom-call(s32[2,4]{1,0:T(2,128)S(1)} %pad_add_fusion.2.blocks_ref, bf16[3584,256]{1,0:T(8,128)(2,1)S(1)} %flipped.4.refs_0_, bf16[3584,256]{1,0:T(8,128)(2,1)S(1)} %flipped.5.refs_1_, bf16[3584,256]{1,0:T(8,128)(2,1)S(1)} %flipped.7.refs_2_, bf16[3584,256]{1,0:T(8,128)(2,1)S(1)} %flipped.6.refs_3_, ...), custom_call_target="tpu_custom_call" | custom-call | flops 1879048192 | bytes 5505024 | tf_op jit(solution)/shard_map/gradient_blocks/pallas_call | solution.py:384
  132.8 3.8 %collective-permute-done.20.refs_5_ = bf16[4,448,512]{2,1,0:T(8,128)(2,1)S(1)} collective-permute-done((bf16[4,448,512]{2,1,0:T(8,128)(2,1)S(1)}, bf16[4,448,512]{2,1,0:T(8,128)(2,1)S(1)}, u32[]{:S(2)}, u32[]{:S(2)}) %collective-permute-start.20) | collective-permute-done | bytes 1835040 | tf_op jit(solution)/shard_map/ppermute | solution.py:528
  136.6 2.1 %gradient_blocks.4 = (bf16[1,448,512]{2,1,0:T(8,128)(2,1)}, bf16[1,448,512]{2,1,0:T(8,128)(2,1)S(1)}, bf16[1,448,512]{2,1,0:T(8,128)(2,1)S(1)}) custom-call(s32[2,3]{1,0:T(2,128)S(1)} %pad_add_fusion.1.blocks_ref, bf16[3584,256]{1,0:T(8,128)(2,1)S(1)} %flipped.4.refs_0_, bf16[3584,256]{1,0:T(8,128)(2,1)S(1)} %flipped.5.refs_1_, ...), custom_call_target="tpu_custom_call" | custom-call | flops 1409286144 | bytes 4128768 | tf_op jit(solution)/shard_map/gradient_blocks/pallas_call | solution.py:384
  140.0 2.2 %collective-permute-start.22 = (bf16[1,448,512]{2,1,0:T(8,128)(2,1)S(1)}, bf16[1,448,512]{2,1,0:T(8,128)(2,1)S(1)}, u32[]{:S(2)}, u32[]{:S(2)}) collective-permute-start(bf16[1,448,512]{2,1,0:T(8,128)(2,1)S(1)} %get-tuple-element.123), channel_id=1, source_target_pairs={{0,32},{32,64},{64,96},{96,0},{1,33},{33,65},{65,97},{97,1},{2,34}... | collective-permute-start | bytes 1376264 | tf_op jit(solution)/shard_map/ppermute | solution.py:536
  143.5 20.8 %all_to_all.5 = f32[32,1,256]{2,1,0:T(1,128)S(1)} all-to-all(f32[32,1,256]{2,1,0:T(1,128)S(1)} %reshape.20), channel_id=1, replica_groups=mesh['role'=2,'ylo'=2,'core'=2,'cx'=4,'cz'=4] {'role','cx','cz'}, dimensions={0} | all-to-all | bytes 65536 | tf_op jit(solution)/shard_map/all_to_all | solution.py:541
  (78 shorter events, 19.8 us)
Async XLA Ops:
  1.4 0.7 copy-start.1
  3.9 18.0 %collective-permute-start.2 = (bf16[64,5120]{1,0:T(8,128)(2,1)S(1)}, bf16[64,5120]{1,0:T(8,128)(2,1)S(1)}, u32[]{:S(2)}, u32[]{:S(2)}) collective-permute-start(bf16[64,5120]{1,0:T(8,128)(2,1)S(1)} %get-tuple-element.68.refs_0_), channel_id=1, source_target_pairs={{0,12},{1,13},{2,14},{3,15},{4,0},{5,1},{6,2},{7,3},{8,4},{9,5},{1... | collective-permute-start | bytes 1966088 | tf_op jit(solution)/shard_map/ppermute | solution.py:68
  6.8 15.2 %collective-permute-start.3 = (bf16[64,5120]{1,0:T(8,128)(2,1)S(1)}, bf16[64,5120]{1,0:T(8,128)(2,1)S(1)}, u32[]{:S(2)}, u32[]{:S(2)}) collective-permute-start(bf16[64,5120]{1,0:T(8,128)(2,1)S(1)} %get-tuple-element.68.refs_0_), channel_id=1, source_target_pairs={{0,8},{1,9},{2,10},{3,11},{4,12},{5,13},{6,14},{7,15},{8,0},{9,1},... | collective-permute-start | bytes 1966088 | tf_op jit(solution)/shard_map/ppermute | solution.py:68
  7.6 18.3 %collective-permute-start.4 = (bf16[64,5120]{1,0:T(8,128)(2,1)S(1)}, bf16[64,5120]{1,0:T(8,128)(2,1)S(1)}, u32[]{:S(2)}, u32[]{:S(2)}) collective-permute-start(bf16[64,5120]{1,0:T(8,128)(2,1)S(1)} %get-tuple-element.68.refs_0_), channel_id=1, source_target_pairs={{0,4},{1,5},{2,6},{3,7},{4,8},{5,9},{6,10},{7,11},{8,12},{9,13},{1... | collective-permute-start | bytes 1966088 | tf_op jit(solution)/shard_map/ppermute | solution.py:68
  8.5 22.2 %collective-permute-start = (bf16[64,3584]{1,0:T(8,128)(2,1)S(1)}, bf16[64,3584]{1,0:T(8,128)(2,1)S(1)}, u32[]{:S(2)}, u32[]{:S(2)}) collective-permute-start(bf16[64,3584]{1,0:T(8,128)(2,1)S(1)} %get-tuple-element.64.refs_0_), channel_id=1, source_target_pairs={{0,12},{1,13},{2,14},{3,15},{4,0},{5,1},{6,2},{7,3},{8,4},{9,5},{1... | collective-permute-start | bytes 1376264 | tf_op jit(solution)/shard_map/ppermute | solution.py:68
  10.8 20.1 %collective-permute-start.1 = (bf16[64,3584]{1,0:T(8,128)(2,1)S(1)}, bf16[64,3584]{1,0:T(8,128)(2,1)}, u32[]{:S(2)}, u32[]{:S(2)}) collective-permute-start(bf16[64,3584]{1,0:T(8,128)(2,1)S(1)} %get-tuple-element.64.refs_0_), channel_id=1, source_target_pairs={{0,4},{1,5},{2,6},{3,7},{4,8},{5,9},{6,10},{7,11},{8,12},{9,13},{1... | collective-permute-start | bytes 1376264 | tf_op jit(solution)/shard_map/ppermute | solution.py:68
  10.8 19.7 %copy-start.4 = (s32[1,3]{1,0:T(1,128)S(1)}, s32[1,3]{1,0:T(1,128)}, u32[]{:S(2)}) copy-start(s32[1,3]{1,0:T(1,128)} %constant.121) | copy-start | bytes 40
  10.8 19.7 %copy-start.2 = (s32[1,128,4]{1,2,0:T(4,128)S(1)}, s32[1,128,4]{1,2,0:T(4,128)}, u32[]{:S(2)}) copy-start(s32[1,128,4]{1,2,0:T(4,128)} %param.18) | copy-start | bytes 6148
  10.9 19.7 %copy-start.3 = (s32[1,128]{1,0:T(1,128)S(1)}, s32[1,128]{1,0:T(1,128)}, u32[]{:S(2)}) copy-start(s32[1,128]{1,0:T(1,128)} %param.17) | copy-start | bytes 1540
  25.9 62.2 %slice-start = ((s8[5242880]{0:T(1024)(128)(4,1)}), s8[4194304]{0:T(1024)(128)(4,1)S(1)}, s32[]{:S(2)}) async-start(s8[5242880]{0:T(1024)(128)(4,1)} %bitcast.22), calls=%async_computation.1 | async-start | bytes 8388608
  26.1 38.2 %collective-permute-start.5 = (bf16[256,5120]{1,0:T(8,128)(2,1)S(1)}, bf16[256,5120]{1,0:T(8,128)(2,1)S(1)}, u32[]{:S(2)}, u32[]{:S(2)}) collective-permute-start(bf16[256,5120]{1,0:T(8,128)(2,1)S(1)} %stacked.2.refs_0_), channel_id=1, source_target_pairs={{0,3},{1,0},{2,1},{3,2},{4,7},{5,4},{6,5},{7,6},{8,11},{9,8},{10,9... | collective-permute-start | bytes 7864328 | tf_op jit(solution)/shard_map/ppermute | solution.py:68
  30.2 34.1 %collective-permute-start.6 = (bf16[256,5120]{1,0:T(8,128)(2,1)S(1)}, bf16[256,5120]{1,0:T(8,128)(2,1)S(1)}, u32[]{:S(2)}, u32[]{:S(2)}) collective-permute-start(bf16[256,5120]{1,0:T(8,128)(2,1)S(1)} %stacked.2.refs_0_), channel_id=1, source_target_pairs={{0,1},{1,2},{2,3},{3,0},{4,5},{5,6},{6,7},{7,4},{8,9},{9,10},{10,1... | collective-permute-start | bytes 7864328 | tf_op jit(solution)/shard_map/ppermute | solution.py:68
  30.9 57.2 %slice-start.1 = ((s8[5242880]{0:T(1024)(128)(4,1)}), s8[1048576]{0:T(1024)(128)(4,1)S(1)}, s32[]{:S(2)}) async-start(s8[5242880]{0:T(1024)(128)(4,1)} %bitcast.22), calls=%async_computation.2 | async-start | bytes 2097152
  30.9 13.5 %collective-permute-start.9 = (bf16[64,3584]{1,0:T(8,128)(2,1)S(1)}, bf16[64,3584]{1,0:T(8,128)(2,1)S(1)}, u32[]{:S(2)}, u32[]{:S(2)}) collective-permute-start(bf16[64,3584]{1,0:T(8,128)(2,1)S(1)} %collective-permute-done.refs_1_), channel_id=1, source_target_pairs={{0,12},{1,13},{2,14},{3,15},{4,0},{5,1},{6,2},{7,3},{8,4},{9,5},{1... | collective-permute-start | bytes 1376264 | tf_op jit(solution)/shard_map/ppermute | solution.py:68
  45.5 38.4 %collective-permute-start.10 = (bf16[256,3584]{1,0:T(8,128)(2,1)S(1)}, bf16[256,3584]{1,0:T(8,128)(2,1)S(1)}, u32[]{:S(2)}, u32[]{:S(2)}) collective-permute-start(bf16[256,3584]{1,0:T(8,128)(2,1)S(1)} %stacked.3.refs_0_), channel_id=1, source_target_pairs={{0,3},{1,0},{2,1},{3,2},{4,7},{5,4},{6,5},{7,6},{8,11},{9,8},{10,9... | collective-permute-start | bytes 5505032 | tf_op jit(solution)/shard_map/ppermute | solution.py:68
  51.4 32.5 %collective-permute-start.11 = (bf16[256,3584]{1,0:T(8,128)(2,1)S(1)}, bf16[256,3584]{1,0:T(8,128)(2,1)S(1)}, u32[]{:S(2)}, u32[]{:S(2)}) collective-permute-start(bf16[256,3584]{1,0:T(8,128)(2,1)S(1)} %stacked.3.refs_0_), channel_id=1, source_target_pairs={{0,1},{1,2},{2,3},{3,0},{4,5},{5,6},{6,7},{7,4},{8,9},{9,10},{10,1... | collective-permute-start | bytes 5505032 | tf_op jit(solution)/shard_map/ppermute | solution.py:68
  64.3 37.3 %collective-permute-start.7 = (bf16[128,5120]{1,0:T(8,128)(2,1)S(1)}, bf16[128,5120]{1,0:T(8,128)(2,1)S(1)}, u32[]{:S(2)}, u32[]{:S(2)}) collective-permute-start(bf16[128,5120]{1,0:T(8,128)(2,1)S(1)} %slice.12), channel_id=1, source_target_pairs={{0,3},{1,0},{2,1},{3,2},{4,7},{5,4},{6,5},{7,6},{8,11},{9,8},{10,9... | collective-permute-start | bytes 3932168 | tf_op jit(solution)/shard_map/ppermute | solution.py:68
  68.2 33.4 %collective-permute-start.8 = (bf16[128,5120]{1,0:T(8,128)(2,1)S(1)}, bf16[128,5120]{1,0:T(8,128)(2,1)S(1)}, u32[]{:S(2)}, u32[]{:S(2)}) collective-permute-start(bf16[128,5120]{1,0:T(8,128)(2,1)S(1)} %slice.13), channel_id=1, source_target_pairs={{0,1},{1,2},{2,3},{3,0},{4,5},{5,6},{6,7},{7,4},{8,9},{9,10},{10,1... | collective-permute-start | bytes 3932168 | tf_op jit(solution)/shard_map/ppermute | solution.py:68
  84.0 23.8 %collective-permute-start.12 = (bf16[128,3584]{1,0:T(8,128)(2,1)S(1)}, bf16[128,3584]{1,0:T(8,128)(2,1)S(1)}, u32[]{:S(2)}, u32[]{:S(2)}) collective-permute-start(bf16[128,3584]{1,0:T(8,128)(2,1)S(1)} %slice.14), channel_id=1, source_target_pairs={{0,3},{1,0},{2,1},{3,2},{4,7},{5,4},{6,5},{7,6},{8,11},{9,8},{10,9... | collective-permute-start | bytes 2752520 | tf_op jit(solution)/shard_map/ppermute | solution.py:68
  87.8 20.0 %collective-permute-start.13 = (bf16[128,3584]{1,0:T(8,128)(2,1)S(1)}, bf16[128,3584]{1,0:T(8,128)(2,1)S(1)}, u32[]{:S(2)}, u32[]{:S(2)}) collective-permute-start(bf16[128,3584]{1,0:T(8,128)(2,1)S(1)} %slice.15), channel_id=1, source_target_pairs={{0,1},{1,2},{2,3},{3,0},{4,5},{5,6},{6,7},{7,4},{8,9},{9,10},{10,1... | collective-permute-start | bytes 2752520 | tf_op jit(solution)/shard_map/ppermute | solution.py:68
  88.1 2.0 %copy-start = (bf16[4,3584,128]{2,1,0:T(8,128)(2,1)S(1)}, bf16[4,3584,128]{2,1,0:T(8,128)(2,1)}, u32[]{:S(2)}) copy-start(bf16[4,3584,128]{2,1,0:T(8,128)(2,1)} %array_ref.3) | copy-start | bytes 11010052
  110.0 4.2 %collective-permute-start.14 = (f32[13,8,128]{2,1,0:T(8,128)S(1)}, f32[13,8,128]{2,1,0:T(8,128)S(1)}, u32[]{:S(2)}, u32[]{:S(2)}) collective-permute-start(f32[13,8,128]{2,1,0:T(8,128)S(1)} %pack_sums.1.refs_0_), channel_id=1, source_target_pairs={{0,12},{4,0},{8,4},{12,8},{1,13},{5,1},{9,5},{13,9},{2,14},{6,2},{... | collective-permute-start | bytes 159752 | tf_op jit(solution)/shard_map/ppermute | solution.py:522
  110.7 5.9 %collective-permute-start.15 = (f32[13,8,128]{2,1,0:T(8,128)S(1)}, f32[13,8,128]{2,1,0:T(8,128)S(1)}, u32[]{:S(2)}, u32[]{:S(2)}) collective-permute-start(f32[13,8,128]{2,1,0:T(8,128)S(1)} %pack_sums.1.refs_0_), channel_id=1, source_target_pairs={{0,8},{4,12},{8,0},{12,4},{1,9},{5,13},{9,1},{13,5},{2,10},{6,14},... | collective-permute-start | bytes 159752 | tf_op jit(solution)/shard_map/ppermute | solution.py:522
  111.5 5.6 %collective-permute-start.16 = (f32[13,8,128]{2,1,0:T(8,128)S(1)}, f32[13,8,128]{2,1,0:T(8,128)S(1)}, u32[]{:S(2)}, u32[]{:S(2)}) collective-permute-start(f32[13,8,128]{2,1,0:T(8,128)S(1)} %pack_sums.1.refs_0_), channel_id=1, source_target_pairs={{0,4},{4,8},{8,12},{12,0},{1,5},{5,9},{9,13},{13,1},{2,6},{6,10},{... | collective-permute-start | bytes 159752 | tf_op jit(solution)/shard_map/ppermute | solution.py:522
  117.2 6.0 %collective-permute-start.17 = (f32[16,8,128]{2,1,0:T(8,128)S(1)}, f32[16,8,128]{2,1,0:T(8,128)S(1)}, u32[]{:S(2)}, u32[]{:S(2)}) collective-permute-start(f32[16,8,128]{2,1,0:T(8,128)S(1)} %merge_sums.1.refs_0_), channel_id=1, source_target_pairs={{0,3},{1,0},{2,1},{3,2},{4,7},{5,4},{6,5},{7,6},{8,11},{9,8},{10,9... | collective-permute-start | bytes 196616 | tf_op jit(solution)/shard_map/ppermute | solution.py:522
  120.7 5.9 %collective-permute-start.18 = (f32[16,8,128]{2,1,0:T(8,128)S(1)}, f32[16,8,128]{2,1,0:T(8,128)S(1)}, u32[]{:S(2)}, u32[]{:S(2)}) collective-permute-start(f32[16,8,128]{2,1,0:T(8,128)S(1)} %merge_sums.1.refs_0_), channel_id=1, source_target_pairs={{0,2},{1,3},{2,0},{3,1},{4,6},{5,7},{6,4},{7,5},{8,10},{9,11},{10,... | collective-permute-start | bytes 196616 | tf_op jit(solution)/shard_map/ppermute | solution.py:522
  120.7 6.2 %collective-permute-start.19 = (f32[16,8,128]{2,1,0:T(8,128)S(1)}, f32[16,8,128]{2,1,0:T(8,128)S(1)}, u32[]{:S(2)}, u32[]{:S(2)}) collective-permute-start(f32[16,8,128]{2,1,0:T(8,128)S(1)} %merge_sums.1.refs_0_), channel_id=1, source_target_pairs={{0,1},{1,2},{2,3},{3,0},{4,5},{5,6},{6,7},{7,4},{8,9},{9,10},{10,1... | collective-permute-start | bytes 196616 | tf_op jit(solution)/shard_map/ppermute | solution.py:522
  132.7 3.9 %collective-permute-start.20 = (bf16[4,448,512]{2,1,0:T(8,128)(2,1)S(1)}, bf16[4,448,512]{2,1,0:T(8,128)(2,1)S(1)}, u32[]{:S(2)}, u32[]{:S(2)}) collective-permute-start(bf16[4,448,512]{2,1,0:T(8,128)(2,1)S(1)} %gradient_blocks.3), channel_id=1, source_target_pairs={{0,16},{16,0},{1,17},{17,1},{2,18},{18,2},{3,19},{19,3},{4,20},{20... | collective-permute-start | bytes 5505032 | tf_op jit(solution)/shard_map/ppermute | solution.py:528
  138.7 26.5 %collective-permute-start.21 = (bf16[1,448,512]{2,1,0:T(8,128)(2,1)}, bf16[1,448,512]{2,1,0:T(8,128)(2,1)S(1)}, u32[]{:S(2)}, u32[]{:S(2)}) collective-permute-start(bf16[1,448,512]{2,1,0:T(8,128)(2,1)} %get-tuple-element.122), channel_id=1, source_target_pairs={{0,64},{32,96},{64,0},{96,32},{1,65},{33,97},{65,1},{97,33},{2,66}... | collective-permute-start | bytes 1376264 | tf_op jit(solution)/shard_map/ppermute | solution.py:536
  140.0 25.2 %collective-permute-start.22 = (bf16[1,448,512]{2,1,0:T(8,128)(2,1)S(1)}, bf16[1,448,512]{2,1,0:T(8,128)(2,1)S(1)}, u32[]{:S(2)}, u32[]{:S(2)}) collective-permute-start(bf16[1,448,512]{2,1,0:T(8,128)(2,1)S(1)} %get-tuple-element.123), channel_id=1, source_target_pairs={{0,32},{32,64},{64,96},{96,0},{1,33},{33,65},{65,97},{97,1},{2,34}... | collective-permute-start | bytes 1376264 | tf_op jit(solution)/shard_map/ppermute | solution.py:536
  142.2 23.0 %collective-permute-start.23 = (bf16[1,448,512]{2,1,0:T(8,128)(2,1)S(1)}, bf16[1,448,512]{2,1,0:T(8,128)(2,1)S(1)}, u32[]{:S(2)}, u32[]{:S(2)}) collective-permute-start(bf16[1,448,512]{2,1,0:T(8,128)(2,1)S(1)} %get-tuple-element.124), channel_id=1, source_target_pairs={{0,96},{32,0},{64,32},{96,64},{1,97},{33,1},{65,33},{97,65},{2,98}... | collective-permute-start | bytes 1376264 | tf_op jit(solution)/shard_map/ppermute | solution.py:536

commit v4 on v3

--- a/solution.py
+++ b/solution.py
@@ -356,42 +356,53 @@
     )(*pieces)
 
 
-def gradient_kernel(with_taken, blocks_ref, *refs):
-    rows, slope_ref = refs[:SIDE], refs[SIDE]
-    outs = refs[SIDE + 2 if with_taken else SIDE + 1 :]
-    step = 0
-    for out_ref in outs:
-        height = out_ref.shape[1]
-        for number in range(out_ref.shape[0]):
-            start = pl.multiple_of(blocks_ref[0, step] * height, 64)
-            found = jnp.dot(
-                jnp.concatenate([part[pl.ds(start, height), :] for part in rows], axis=1),
-                slope_ref[...],
-                preferred_element_type=jnp.float32,
-            )
-            if with_taken:
-                found = found + refs[SIDE + 1][blocks_ref[1, step]].astype(jnp.float32)
-            out_ref[number] = found.astype(out_ref.dtype)
-            step += 1
-
-
-def gradient_blocks(blocks, rows, slope, taken, height, dtype, apart=False):
+def gradient_kernel(blocks_ref, *refs):
+    *rows, slope_ref, out_ref = refs
+    height = out_ref.shape[1]
+    for step in range(out_ref.shape[0]):
+        start = pl.multiple_of(blocks_ref[0, step] * height, 64)
+        found = jnp.dot(
+            jnp.concatenate([part[pl.ds(start, height), :] for part in rows], axis=1),
+            slope_ref[...],
+            preferred_element_type=jnp.float32,
+        )
+        out_ref[step] = found.astype(out_ref.dtype)
+
+
+def gradient_blocks(blocks, rows, slope, height, dtype):
     count = SIDE * rows[0].shape[1]
     entries = slope.shape[1]
     steps = blocks.shape[1]
-    operands = [*rows, slope] + ([] if taken is None else [taken])
-    shapes = [(1, height, entries)] * steps if apart else [(steps, height, entries)]
-    return pl.pallas_call(
-        functools.partial(gradient_kernel, taken is not None),
-        in_specs=[SMEM] + [VMEM] * len(operands),
-        out_specs=[VMEM] * len(shapes),
-        out_shape=[jax.ShapeDtypeStruct(shape, dtype) for shape in shapes],
+    return pl.pallas_call(
+        gradient_kernel,
+        in_specs=[SMEM] + [VMEM] * (SIDE + 1),
+        out_specs=VMEM,
+        out_shape=pltpu.VMEM((steps, height, entries), dtype),
         **small_kernel(
             "gradient_blocks",
             flops=2 * steps * height * entries * count,
             bytes_accessed=2 * steps * height * (count + entries),
         ),
-    )(blocks, *operands)
+    )(blocks, *rows, slope)
+
+
+def pair_kernel(order, own_ref, mine_ref, taken_ref, total_ref, *outs):
+    total_ref[0] = own_ref[0] + taken_ref[0].astype(jnp.float32)
+    for number, (offset, out_ref) in enumerate(zip(order, outs)):
+        total = mine_ref[number] + taken_ref[offset].astype(jnp.float32)
+        out_ref[0] = total.astype(out_ref.dtype)
+
+
+def pair_sums(order, own, mine, taken):
+    shape = (1, *mine.shape[1:])
+    return pl.pallas_call(
+        functools.partial(pair_kernel, order),
+        in_specs=[VMEM, VMEM, VMEM],
+        out_specs=[VMEM] * (len(order) + 1),
+        out_shape=[jax.ShapeDtypeStruct(shape, jnp.float32)]
+        + [jax.ShapeDtypeStruct(shape, taken.dtype)] * len(order),
+        **small_kernel("pair_sums", bytes_accessed=8 * mine.size),
+    )(own, mine, taken)
 
 
 def total_kernel(own_ref, after_ref, before_ref, opposite_ref, out_ref):
@@ -524,11 +535,12 @@
         if axis == CTX[0]:
             sent = merge_sums(parts)
     slope, terms = slopes(order, parts, teacher_scaled, student_raw, half)
-    (given,) = gradient_blocks(blocks[2], flipped_rows, slope, None, height, jnp.bfloat16)
+    given = gradient_blocks(blocks[2], flipped_rows, slope, height, jnp.bfloat16)
+    given, slope = tie((given, slope))
     taken = lax.ppermute(given, "core", [(0, 1), (1, 0)])
-    sent = gradient_blocks(blocks[1], flipped_rows, slope, taken, height, jnp.bfloat16, True)
-    slope, *sent = tie((slope, *sent))
-    (own,) = gradient_blocks(blocks[0], flipped_rows, slope, taken, height, jnp.float32)
+    mine = gradient_blocks(blocks[1], flipped_rows, slope, height, jnp.float32)
+    own = gradient_blocks(blocks[0], flipped_rows, slope, height, jnp.float32)
+    own, *sent = pair_sums(away, own, mine, taken)
     terms, own = tie((terms, own))
     shares = total_of(
         [own]

time: 167 us -> 166 us (level)
  waiting for transfers between devices: 74.4 us -> 71.1 us
    ppermute x1, waiting for transfers between devices: 3.77 us -> 0.45 us  [on_device(): taken = lax.ppermute(given, 'core', [(0, 1), (1, 0)])]
    pallas_call x3 -> x4, Pallas kernels: 5.93 us -> 7.05 us  [the longest x3 5.92 us: gradient_blocks(): pl.pallas_call(gradient_kernel, in_specs=[SMEM] + [VMEM] * (SIDE + 1), ou...]
  transfers between devices with their start and end apart: 24 -> 24, of which waited for: 14 -> 14; matrix products, arithmetic and copies ran while one was open for 1% -> 1% of each run, Pallas kernels for 10% -> 11%
where the time goes in v4:
time: 166 us; the launch traced here: 165 us
  waiting for transfers between devices  71.1 us (43%)
  starting transfers between devices  35.6 us (21%)
  Pallas kernels  30.9 us (19%)
  blocking collectives  22 us (13%)
  local copies, waits for them, and re-layouts  4.38 us (3%)
    ppermute x14, waiting for transfers between devices, moved(): return lax.ppermute(value, TURN, line_pairs(phase, step))  61.1 us
    ppermute x14, starting transfers between devices, moved(): return lax.ppermute(value, TURN, line_pairs(phase, step))  25.3 us
    all_to_all x1, blocking collectives, on_device(): lax.all_to_all(terms.reshape(2 * count, 1, BOOKS * half), ('role', *CTX),...  22 us
    pallas_call x8, Pallas kernels, project(): pl.pallas_call(functools.partial(project_kernel, is_teacher), in_specs=[V...  12.8 us
    ppermute x6, waiting for transfers between devices, on_device(): lax.ppermute(sent, axis, back(shift))  9.53 us
    ppermute x6, starting transfers between devices, on_device(): lax.ppermute(sent, axis, back(shift))  6.76 us
    pallas_call x3, Pallas kernels, gradient_blocks(): pl.pallas_call(gradient_kernel, in_specs=[SMEM] + [VMEM] * (SIDE + 1), ou...  5.92 us
    ppermute x3, starting transfers between devices, on_device(): lax.ppermute(piece, COLUMN, [(y, (y + offset) % owners) for y in range(ow...  3.42 us
  transfers between devices with their start and end apart: 24, of which 14 were waited for; matrix products, arithmetic and copies ran while one was open for 1% of the time, Pallas kernels for 11%

profile of v4, /device:TPU:24, one launch (start us, length us, event | category | flops | bytes accessed | tf_op | source)
XLA Modules:
  0.0 165.3 jit_solution(747232486495137918)
XLA Ops:
  2.1 1.8 %normalized.1 = (bf16[64,3584]{1,0:T(8,128)(2,1)S(1)}, bf16[64,5120]{1,0:T(8,128)(2,1)S(1)}) custom-call(s32[1]{0:T(128)} %bitcast.role_ref, bf16[1,128,3584]{2,1,0:T(8,128)(2,1)} %refs_0_.1, bf16[1,128,5120]{2,1,0:T(8,128)(2,1)} %refs_1_.1, f32[1,3584]{1,0:T(1,128)S(1)} %broadcast_in_dim.9.refs_2_, f32[1,5120]{1,0:T(1,128)S(1)} %bitcast.24), custom_call_target="tpu_custom_call" | custom-call | bytes 2228224 | tf_op jit(solution)/shard_map/normalized/pallas_call | solution.py:86
  3.9 2.8 %collective-permute-start.2 = (bf16[64,5120]{1,0:T(8,128)(2,1)S(1)}, bf16[64,5120]{1,0:T(8,128)(2,1)S(1)}, u32[]{:S(2)}, u32[]{:S(2)}) collective-permute-start(bf16[64,5120]{1,0:T(8,128)(2,1)S(1)} %get-tuple-element.67.refs_0_), channel_id=1, source_target_pairs={{0,12},{1,13},{2,14},{3,15},{4,0},{5,1},{6,2},{7,3},{8,4},{9,5},{1... | collective-permute-start | bytes 1966088 | tf_op jit(solution)/shard_map/ppermute | solution.py:68
  8.5 2.4 %collective-permute-start = (bf16[64,3584]{1,0:T(8,128)(2,1)S(1)}, bf16[64,3584]{1,0:T(8,128)(2,1)S(1)}, u32[]{:S(2)}, u32[]{:S(2)}) collective-permute-start(bf16[64,3584]{1,0:T(8,128)(2,1)S(1)} %get-tuple-element.63.refs_0_), channel_id=1, source_target_pairs={{0,12},{1,13},{2,14},{3,15},{4,0},{5,1},{6,2},{7,3},{8,4},{9,5},{1... | collective-permute-start | bytes 1376264 | tf_op jit(solution)/shard_map/ppermute | solution.py:68
  10.9 11.1 %collective-permute-done.2.refs_1_ = bf16[64,5120]{1,0:T(8,128)(2,1)S(1)} collective-permute-done((bf16[64,5120]{1,0:T(8,128)(2,1)S(1)}, bf16[64,5120]{1,0:T(8,128)(2,1)S(1)}, u32[]{:S(2)}, u32[]{:S(2)}) %collective-permute-start.2) | collective-permute-done | bytes 655392 | tf_op jit(solution)/shard_map/ppermute | solution.py:68
  21.9 3.9 %collective-permute-done.4.refs_3_ = bf16[64,5120]{1,0:T(8,128)(2,1)S(1)} collective-permute-done((bf16[64,5120]{1,0:T(8,128)(2,1)S(1)}, bf16[64,5120]{1,0:T(8,128)(2,1)S(1)}, u32[]{:S(2)}, u32[]{:S(2)}) %collective-permute-start.4) | collective-permute-done | bytes 655392 | tf_op jit(solution)/shard_map/ppermute | solution.py:68
  26.1 4.1 %collective-permute-start.5 = (bf16[256,5120]{1,0:T(8,128)(2,1)S(1)}, bf16[256,5120]{1,0:T(8,128)(2,1)S(1)}, u32[]{:S(2)}, u32[]{:S(2)}) collective-permute-start(bf16[256,5120]{1,0:T(8,128)(2,1)S(1)} %stacked.2.refs_0_), channel_id=1, source_target_pairs={{0,3},{1,0},{2,1},{3,2},{4,7},{5,4},{6,5},{7,6},{8,11},{9,8},{10,9... | collective-permute-start | bytes 7864328 | tf_op jit(solution)/shard_map/ppermute | solution.py:68
  31.5 12.8 %collective-permute-done.9.refs_2_ = bf16[64,3584]{1,0:T(8,128)(2,1)S(1)} collective-permute-done((bf16[64,3584]{1,0:T(8,128)(2,1)S(1)}, bf16[64,3584]{1,0:T(8,128)(2,1)S(1)}, u32[]{:S(2)}, u32[]{:S(2)}) %collective-permute-start.9) | collective-permute-done | bytes 458784 | tf_op jit(solution)/shard_map/ppermute | solution.py:68
  45.5 5.9 %collective-permute-start.10 = (bf16[256,3584]{1,0:T(8,128)(2,1)S(1)}, bf16[256,3584]{1,0:T(8,128)(2,1)S(1)}, u32[]{:S(2)}, u32[]{:S(2)}) collective-permute-start(bf16[256,3584]{1,0:T(8,128)(2,1)S(1)} %stacked.3.refs_0_), channel_id=1, source_target_pairs={{0,3},{1,0},{2,1},{3,2},{4,7},{5,4},{6,5},{7,6},{8,11},{9,8},{10,9... | collective-permute-start | bytes 5505032 | tf_op jit(solution)/shard_map/ppermute | solution.py:68
  51.4 12.9 %collective-permute-done.5.refs_0_ = bf16[256,5120]{1,0:T(8,128)(2,1)S(1)} collective-permute-done((bf16[256,5120]{1,0:T(8,128)(2,1)S(1)}, bf16[256,5120]{1,0:T(8,128)(2,1)S(1)}, u32[]{:S(2)}, u32[]{:S(2)}) %collective-permute-start.5) | collective-permute-done | bytes 2621472 | tf_op jit(solution)/shard_map/ppermute | solution.py:68
  64.3 3.8 %collective-permute-start.7 = (bf16[128,5120]{1,0:T(8,128)(2,1)S(1)}, bf16[128,5120]{1,0:T(8,128)(2,1)S(1)}, u32[]{:S(2)}, u32[]{:S(2)}) collective-permute-start(bf16[128,5120]{1,0:T(8,128)(2,1)S(1)} %slice.12), channel_id=1, source_target_pairs={{0,3},{1,0},{2,1},{3,2},{4,7},{5,4},{6,5},{7,6},{8,11},{9,8},{10,9... | collective-permute-start | bytes 3932168 | tf_op jit(solution)/shard_map/ppermute | solution.py:68
  68.3 15.6 %collective-permute-done.10.refs_0_ = bf16[256,3584]{1,0:T(8,128)(2,1)S(1)} collective-permute-done((bf16[256,3584]{1,0:T(8,128)(2,1)S(1)}, bf16[256,3584]{1,0:T(8,128)(2,1)S(1)}, u32[]{:S(2)}, u32[]{:S(2)}) %collective-permute-start.10) | collective-permute-done | bytes 1835040 | tf_op jit(solution)/shard_map/ppermute | solution.py:68
  84.0 3.8 %collective-permute-start.12 = (bf16[128,3584]{1,0:T(8,128)(2,1)S(1)}, bf16[128,3584]{1,0:T(8,128)(2,1)S(1)}, u32[]{:S(2)}, u32[]{:S(2)}) collective-permute-start(bf16[128,3584]{1,0:T(8,128)(2,1)S(1)} %slice.14), channel_id=1, source_target_pairs={{0,3},{1,0},{2,1},{3,2},{4,7},{5,4},{6,5},{7,6},{8,11},{9,8},{10,9... | collective-permute-start | bytes 2752520 | tf_op jit(solution)/shard_map/ppermute | solution.py:68
  88.5 1.7 %copy-done = bf16[4,3584,128]{2,1,0:T(8,128)(2,1)S(1)} copy-done((bf16[4,3584,128]{2,1,0:T(8,128)(2,1)S(1)}, bf16[4,3584,128]{2,1,0:T(8,128)(2,1)}, u32[]{:S(2)}) %copy-start) | copy-done | bytes 3670040
  90.4 1.7 %project_teacher.4 = (f32[4,128,256]{2,1,0:T(8,128)S(1)}, f32[8,256]{1,0:T(8,128)S(1)}) custom-call(bf16[256,5120]{1,0:T(8,128)(2,1)S(1)} %stacked.2.refs_0_, bf16[4,5120,128]{2,1,0:T(8,128)(2,1)S(1)} %held.2.refs_1_.refs_2_), custom_call_target="tpu_custom_call" | custom-call | flops 1342177280 | bytes 8388608 | tf_op jit(solution)/shard_map/project_teacher/pallas_call | solution.py:166
  92.7 1.5 project_student.4
  95.2 1.5 project_student.5
  96.7 1.5 project_student.6
  98.2 1.7 %project_teacher.5 = (f32[4,128,256]{2,1,0:T(8,128)S(1)}, f32[8,256]{1,0:T(8,128)S(1)}) custom-call(bf16[256,5120]{1,0:T(8,128)(2,1)S(1)} %collective-permute-done.5.refs_0_, bf16[4,5120,128]{2,1,0:T(8,128)(2,1)S(1)} %held.2.refs_1_.refs_2_), custom_call_target="tpu_custom_call" | custom-call | flops 1342177280 | bytes 8388608 | tf_op jit(solution)/shard_map/project_teacher/pallas_call | solution.py:166
  99.9 1.7 %project_teacher.6 = (f32[4,128,256]{2,1,0:T(8,128)S(1)}, f32[8,256]{1,0:T(8,128)S(1)}) custom-call(bf16[256,5120]{1,0:T(8,128)(2,1)S(1)} %collective-permute-done.6.refs_0_, bf16[4,5120,128]{2,1,0:T(8,128)(2,1)S(1)} %held.2.refs_1_.refs_2_), custom_call_target="tpu_custom_call" | custom-call | flops 1342177280 | bytes 8388608 | tf_op jit(solution)/shard_map/project_teacher/pallas_call | solution.py:166
  101.7 1.7 %project_teacher.7 = (f32[4,128,256]{2,1,0:T(8,128)S(1)}, f32[8,256]{1,0:T(8,128)S(1)}) custom-call(bf16[128,5120]{1,0:T(8,128)(2,1)S(1)} %collective-permute-done.7.refs_0_, bf16[128,5120]{1,0:T(8,128)(2,1)S(1)} %collective-permute-done.8.refs_1_, bf16[4,5120,128]{2,1,0:T(8,128)(2,1)S(1)} %held.2.refs_1_.refs_2_), custom_call_target="tpu_custom_call" | custom-call | flops 1342177280 | bytes 8388608 | tf_op jit(solution)/shard_map/project_teacher/pallas_call | solution.py:166
  103.4 4.4 %collective-permute-done.12.refs_0_ = bf16[128,3584]{1,0:T(8,128)(2,1)S(1)} collective-permute-done((bf16[128,3584]{1,0:T(8,128)(2,1)S(1)}, bf16[128,3584]{1,0:T(8,128)(2,1)S(1)}, u32[]{:S(2)}, u32[]{:S(2)}) %collective-permute-start.12) | collective-permute-done | bytes 917536 | tf_op jit(solution)/shard_map/ppermute | solution.py:68
  107.8 1.5 project_student.7
  112.3 1.9 %collective-permute-done.14.refs_1_ = f32[13,8,128]{2,1,0:T(8,128)S(1)} collective-permute-done((f32[13,8,128]{2,1,0:T(8,128)S(1)}, f32[13,8,128]{2,1,0:T(8,128)S(1)}, u32[]{:S(2)}, u32[]{:S(2)}) %collective-permute-start.14) | collective-permute-done | bytes 53280 | tf_op jit(solution)/shard_map/ppermute | solution.py:533
  114.2 2.4 %collective-permute-done.15.refs_2_ = f32[13,8,128]{2,1,0:T(8,128)S(1)} collective-permute-done((f32[13,8,128]{2,1,0:T(8,128)S(1)}, f32[13,8,128]{2,1,0:T(8,128)S(1)}, u32[]{:S(2)}, u32[]{:S(2)}) %collective-permute-start.15) | collective-permute-done | bytes 53280 | tf_op jit(solution)/shard_map/ppermute | solution.py:533
  117.2 3.5 %collective-permute-start.17 = (f32[16,8,128]{2,1,0:T(8,128)S(1)}, f32[16,8,128]{2,1,0:T(8,128)S(1)}, u32[]{:S(2)}, u32[]{:S(2)}) collective-permute-start(f32[16,8,128]{2,1,0:T(8,128)S(1)} %merge_sums.1.refs_0_), channel_id=1, source_target_pairs={{0,3},{1,0},{2,1},{3,2},{4,7},{5,4},{6,5},{7,6},{8,11},{9,8},{10,9... | collective-permute-start | bytes 196616 | tf_op jit(solution)/shard_map/ppermute | solution.py:533
  123.2 3.4 %collective-permute-done.18.refs_2_ = f32[16,8,128]{2,1,0:T(8,128)S(1)} collective-permute-done((f32[16,8,128]{2,1,0:T(8,128)S(1)}, f32[16,8,128]{2,1,0:T(8,128)S(1)}, u32[]{:S(2)}, u32[]{:S(2)}) %collective-permute-start.18) | collective-permute-done | bytes 65568 | tf_op jit(solution)/shard_map/ppermute | solution.py:533
  126.9 3.2 %slopes.1 = (bf16[1024,512]{1,0:T(8,128)(2,1)S(1)}, f32[2,16,4,64]{3,2,1,0:T(4,128)S(1)}) custom-call(s32[19]{0:T(128)S(1)} %pad_add_fusion.3.order_ref, f32[16,8,128]{2,1,0:T(8,128)S(1)} %merge_sums.1.refs_0_, f32[16,8,128]{2,1,0:T(8,128)S(1)} %collective-permute-done.17.refs_1_, f32[16,8,128]{2,1,0:T(8,128)S(1)} %collective-permute-done.18.refs_2_, ...), custom_call_target="tpu_custom_call" | custom-call | flops 20971520 | bytes 5242880 | tf_op jit(solution)/shard_map/slopes/pallas_call | solution.py:318
  130.1 2.6 %gradient_blocks.3 = bf16[4,448,512]{2,1,0:T(8,128)(2,1)S(1)} custom-call(s32[2,4]{1,0:T(2,128)S(1)} %pad_add_fusion.2.blocks_ref, bf16[3584,256]{1,0:T(8,128)(2,1)S(1)} %flipped.4.refs_0_, bf16[3584,256]{1,0:T(8,128)(2,1)S(1)} %flipped.5.refs_1_, bf16[3584,256]{1,0:T(8,128)(2,1)S(1)} %flipped.7.refs_2_, bf16[3584,256]{1,0:T(8,128)(2,1)S(1)} %flipped.6.refs_3_, ...), custom_call_target="tpu_custom_call" | custom-call | flops 1879048192 | bytes 5505024 | tf_op jit(solution)/shard_map/gradient_blocks/pallas_call | solution.py:376
  134.0 2.1 %gradient_blocks.5.mine_ref = f32[3,448,512]{2,1,0:T(8,128)S(1)} custom-call(s32[2,3]{1,0:T(2,128)S(1)} %pad_add_fusion.1.blocks_ref, bf16[3584,256]{1,0:T(8,128)(2,1)S(1)} %flipped.4.refs_0_, bf16[3584,256]{1,0:T(8,128)(2,1)S(1)} %flipped.5.refs_1_, bf16[3584,256]{1,0:T(8,128)(2,1)S(1)} %flipped.7.refs_2_, bf16[3584,256]{1,0:T(8,128)(2,1)S(1)} %flipped.6.refs_3_, ...), custom_call_target="tpu_custom_call" | custom-call | flops 1409286144 | bytes 4128768 | tf_op jit(solution)/shard_map/gradient_blocks/pallas_call | solution.py:376
  137.7 1.2 collective-permute-start.21
  138.9 2.2 %collective-permute-start.22 = (bf16[1,448,512]{2,1,0:T(8,128)(2,1)S(1)}, bf16[1,448,512]{2,1,0:T(8,128)(2,1)S(1)}, u32[]{:S(2)}, u32[]{:S(2)}) collective-permute-start(bf16[1,448,512]{2,1,0:T(8,128)(2,1)S(1)} %get-tuple-element.121), channel_id=1, source_target_pairs={{0,32},{32,64},{64,96},{96,0},{1,33},{33,65},{65,97},{97,1},{2,34}... | collective-permute-start | bytes 1376264 | tf_op jit(solution)/shard_map/ppermute | solution.py:548
  141.2 22.0 %all_to_all.5 = f32[32,1,256]{2,1,0:T(1,128)S(1)} all-to-all(f32[32,1,256]{2,1,0:T(1,128)S(1)} %reshape.20), channel_id=1, replica_groups=mesh['role'=2,'ylo'=2,'core'=2,'cx'=4,'cz'=4] {'role','cx','cz'}, dimensions={0} | all-to-all | bytes 65536 | tf_op jit(solution)/shard_map/all_to_all | solution.py:553
  (79 shorter events, 20.0 us)
Async XLA Ops:
  1.4 0.7 copy-start.1
  3.9 18.0 %collective-permute-start.2 = (bf16[64,5120]{1,0:T(8,128)(2,1)S(1)}, bf16[64,5120]{1,0:T(8,128)(2,1)S(1)}, u32[]{:S(2)}, u32[]{:S(2)}) collective-permute-start(bf16[64,5120]{1,0:T(8,128)(2,1)S(1)} %get-tuple-element.67.refs_0_), channel_id=1, source_target_pairs={{0,12},{1,13},{2,14},{3,15},{4,0},{5,1},{6,2},{7,3},{8,4},{9,5},{1... | collective-permute-start | bytes 1966088 | tf_op jit(solution)/shard_map/ppermute | solution.py:68
  6.8 15.2 %collective-permute-start.3 = (bf16[64,5120]{1,0:T(8,128)(2,1)S(1)}, bf16[64,5120]{1,0:T(8,128)(2,1)S(1)}, u32[]{:S(2)}, u32[]{:S(2)}) collective-permute-start(bf16[64,5120]{1,0:T(8,128)(2,1)S(1)} %get-tuple-element.67.refs_0_), channel_id=1, source_target_pairs={{0,8},{1,9},{2,10},{3,11},{4,12},{5,13},{6,14},{7,15},{8,0},{9,1},... | collective-permute-start | bytes 1966088 | tf_op jit(solution)/shard_map/ppermute | solution.py:68
  7.6 18.3 %collective-permute-start.4 = (bf16[64,5120]{1,0:T(8,128)(2,1)S(1)}, bf16[64,5120]{1,0:T(8,128)(2,1)S(1)}, u32[]{:S(2)}, u32[]{:S(2)}) collective-permute-start(bf16[64,5120]{1,0:T(8,128)(2,1)S(1)} %get-tuple-element.67.refs_0_), channel_id=1, source_target_pairs={{0,4},{1,5},{2,6},{3,7},{4,8},{5,9},{6,10},{7,11},{8,12},{9,13},{1... | collective-permute-start | bytes 1966088 | tf_op jit(solution)/shard_map/ppermute | solution.py:68
  8.5 22.2 %collective-permute-start = (bf16[64,3584]{1,0:T(8,128)(2,1)S(1)}, bf16[64,3584]{1,0:T(8,128)(2,1)S(1)}, u32[]{:S(2)}, u32[]{:S(2)}) collective-permute-start(bf16[64,3584]{1,0:T(8,128)(2,1)S(1)} %get-tuple-element.63.refs_0_), channel_id=1, source_target_pairs={{0,12},{1,13},{2,14},{3,15},{4,0},{5,1},{6,2},{7,3},{8,4},{9,5},{1... | collective-permute-start | bytes 1376264 | tf_op jit(solution)/shard_map/ppermute | solution.py:68
  10.8 20.1 %collective-permute-start.1 = (bf16[64,3584]{1,0:T(8,128)(2,1)S(1)}, bf16[64,3584]{1,0:T(8,128)(2,1)}, u32[]{:S(2)}, u32[]{:S(2)}) collective-permute-start(bf16[64,3584]{1,0:T(8,128)(2,1)S(1)} %get-tuple-element.63.refs_0_), channel_id=1, source_target_pairs={{0,4},{1,5},{2,6},{3,7},{4,8},{5,9},{6,10},{7,11},{8,12},{9,13},{1... | collective-permute-start | bytes 1376264 | tf_op jit(solution)/shard_map/ppermute | solution.py:68
  10.8 19.7 %copy-start.4 = (s32[1,3]{1,0:T(1,128)S(1)}, s32[1,3]{1,0:T(1,128)}, u32[]{:S(2)}) copy-start(s32[1,3]{1,0:T(1,128)} %constant.121) | copy-start | bytes 40
  10.8 19.7 %copy-start.2 = (s32[1,128,4]{1,2,0:T(4,128)S(1)}, s32[1,128,4]{1,2,0:T(4,128)}, u32[]{:S(2)}) copy-start(s32[1,128,4]{1,2,0:T(4,128)} %param.18) | copy-start | bytes 6148
  10.9 19.7 %copy-start.3 = (s32[1,128]{1,0:T(1,128)S(1)}, s32[1,128]{1,0:T(1,128)}, u32[]{:S(2)}) copy-start(s32[1,128]{1,0:T(1,128)} %param.17) | copy-start | bytes 1540
  25.9 62.2 %slice-start = ((s8[5242880]{0:T(1024)(128)(4,1)}), s8[4194304]{0:T(1024)(128)(4,1)S(1)}, s32[]{:S(2)}) async-start(s8[5242880]{0:T(1024)(128)(4,1)} %bitcast.22), calls=%async_computation.1 | async-start | bytes 8388608
  26.1 38.2 %collective-permute-start.5 = (bf16[256,5120]{1,0:T(8,128)(2,1)S(1)}, bf16[256,5120]{1,0:T(8,128)(2,1)S(1)}, u32[]{:S(2)}, u32[]{:S(2)}) collective-permute-start(bf16[256,5120]{1,0:T(8,128)(2,1)S(1)} %stacked.2.refs_0_), channel_id=1, source_target_pairs={{0,3},{1,0},{2,1},{3,2},{4,7},{5,4},{6,5},{7,6},{8,11},{9,8},{10,9... | collective-permute-start | bytes 7864328 | tf_op jit(solution)/shard_map/ppermute | solution.py:68
  30.2 34.1 %collective-permute-start.6 = (bf16[256,5120]{1,0:T(8,128)(2,1)S(1)}, bf16[256,5120]{1,0:T(8,128)(2,1)S(1)}, u32[]{:S(2)}, u32[]{:S(2)}) collective-permute-start(bf16[256,5120]{1,0:T(8,128)(2,1)S(1)} %stacked.2.refs_0_), channel_id=1, source_target_pairs={{0,1},{1,2},{2,3},{3,0},{4,5},{5,6},{6,7},{7,4},{8,9},{9,10},{10,1... | collective-permute-start | bytes 7864328 | tf_op jit(solution)/shard_map/ppermute | solution.py:68
  30.9 57.2 %slice-start.1 = ((s8[5242880]{0:T(1024)(128)(4,1)}), s8[1048576]{0:T(1024)(128)(4,1)S(1)}, s32[]{:S(2)}) async-start(s8[5242880]{0:T(1024)(128)(4,1)} %bitcast.22), calls=%async_computation.2 | async-start | bytes 2097152
  30.9 13.5 %collective-permute-start.9 = (bf16[64,3584]{1,0:T(8,128)(2,1)S(1)}, bf16[64,3584]{1,0:T(8,128)(2,1)S(1)}, u32[]{:S(2)}, u32[]{:S(2)}) collective-permute-start(bf16[64,3584]{1,0:T(8,128)(2,1)S(1)} %collective-permute-done.refs_1_), channel_id=1, source_target_pairs={{0,12},{1,13},{2,14},{3,15},{4,0},{5,1},{6,2},{7,3},{8,4},{9,5},{1... | collective-permute-start | bytes 1376264 | tf_op jit(solution)/shard_map/ppermute | solution.py:68
  45.5 38.4 %collective-permute-start.10 = (bf16[256,3584]{1,0:T(8,128)(2,1)S(1)}, bf16[256,3584]{1,0:T(8,128)(2,1)S(1)}, u32[]{:S(2)}, u32[]{:S(2)}) collective-permute-start(bf16[256,3584]{1,0:T(8,128)(2,1)S(1)} %stacked.3.refs_0_), channel_id=1, source_target_pairs={{0,3},{1,0},{2,1},{3,2},{4,7},{5,4},{6,5},{7,6},{8,11},{9,8},{10,9... | collective-permute-start | bytes 5505032 | tf_op jit(solution)/shard_map/ppermute | solution.py:68
  51.4 32.5 %collective-permute-start.11 = (bf16[256,3584]{1,0:T(8,128)(2,1)S(1)}, bf16[256,3584]{1,0:T(8,128)(2,1)S(1)}, u32[]{:S(2)}, u32[]{:S(2)}) collective-permute-start(bf16[256,3584]{1,0:T(8,128)(2,1)S(1)} %stacked.3.refs_0_), channel_id=1, source_target_pairs={{0,1},{1,2},{2,3},{3,0},{4,5},{5,6},{6,7},{7,4},{8,9},{9,10},{10,1... | collective-permute-start | bytes 5505032 | tf_op jit(solution)/shard_map/ppermute | solution.py:68
  64.3 37.3 %collective-permute-start.7 = (bf16[128,5120]{1,0:T(8,128)(2,1)S(1)}, bf16[128,5120]{1,0:T(8,128)(2,1)S(1)}, u32[]{:S(2)}, u32[]{:S(2)}) collective-permute-start(bf16[128,5120]{1,0:T(8,128)(2,1)S(1)} %slice.12), channel_id=1, source_target_pairs={{0,3},{1,0},{2,1},{3,2},{4,7},{5,4},{6,5},{7,6},{8,11},{9,8},{10,9... | collective-permute-start | bytes 3932168 | tf_op jit(solution)/shard_map/ppermute | solution.py:68
  68.2 33.4 %collective-permute-start.8 = (bf16[128,5120]{1,0:T(8,128)(2,1)S(1)}, bf16[128,5120]{1,0:T(8,128)(2,1)S(1)}, u32[]{:S(2)}, u32[]{:S(2)}) collective-permute-start(bf16[128,5120]{1,0:T(8,128)(2,1)S(1)} %slice.13), channel_id=1, source_target_pairs={{0,1},{1,2},{2,3},{3,0},{4,5},{5,6},{6,7},{7,4},{8,9},{9,10},{10,1... | collective-permute-start | bytes 3932168 | tf_op jit(solution)/shard_map/ppermute | solution.py:68
  84.0 23.8 %collective-permute-start.12 = (bf16[128,3584]{1,0:T(8,128)(2,1)S(1)}, bf16[128,3584]{1,0:T(8,128)(2,1)S(1)}, u32[]{:S(2)}, u32[]{:S(2)}) collective-permute-start(bf16[128,3584]{1,0:T(8,128)(2,1)S(1)} %slice.14), channel_id=1, source_target_pairs={{0,3},{1,0},{2,1},{3,2},{4,7},{5,4},{6,5},{7,6},{8,11},{9,8},{10,9... | collective-permute-start | bytes 2752520 | tf_op jit(solution)/shard_map/ppermute | solution.py:68
  87.8 20.0 %collective-permute-start.13 = (bf16[128,3584]{1,0:T(8,128)(2,1)S(1)}, bf16[128,3584]{1,0:T(8,128)(2,1)S(1)}, u32[]{:S(2)}, u32[]{:S(2)}) collective-permute-start(bf16[128,3584]{1,0:T(8,128)(2,1)S(1)} %slice.15), channel_id=1, source_target_pairs={{0,1},{1,2},{2,3},{3,0},{4,5},{5,6},{6,7},{7,4},{8,9},{9,10},{10,1... | collective-permute-start | bytes 2752520 | tf_op jit(solution)/shard_map/ppermute | solution.py:68
  88.1 2.0 %copy-start = (bf16[4,3584,128]{2,1,0:T(8,128)(2,1)S(1)}, bf16[4,3584,128]{2,1,0:T(8,128)(2,1)}, u32[]{:S(2)}) copy-start(bf16[4,3584,128]{2,1,0:T(8,128)(2,1)} %array_ref.3) | copy-start | bytes 11010052
  110.0 4.2 %collective-permute-start.14 = (f32[13,8,128]{2,1,0:T(8,128)S(1)}, f32[13,8,128]{2,1,0:T(8,128)S(1)}, u32[]{:S(2)}, u32[]{:S(2)}) collective-permute-start(f32[13,8,128]{2,1,0:T(8,128)S(1)} %pack_sums.1.refs_0_), channel_id=1, source_target_pairs={{0,12},{4,0},{8,4},{12,8},{1,13},{5,1},{9,5},{13,9},{2,14},{6,2},{... | collective-permute-start | bytes 159752 | tf_op jit(solution)/shard_map/ppermute | solution.py:533
  110.7 5.9 %collective-permute-start.15 = (f32[13,8,128]{2,1,0:T(8,128)S(1)}, f32[13,8,128]{2,1,0:T(8,128)S(1)}, u32[]{:S(2)}, u32[]{:S(2)}) collective-permute-start(f32[13,8,128]{2,1,0:T(8,128)S(1)} %pack_sums.1.refs_0_), channel_id=1, source_target_pairs={{0,8},{4,12},{8,0},{12,4},{1,9},{5,13},{9,1},{13,5},{2,10},{6,14},... | collective-permute-start | bytes 159752 | tf_op jit(solution)/shard_map/ppermute | solution.py:533
  111.5 5.6 %collective-permute-start.16 = (f32[13,8,128]{2,1,0:T(8,128)S(1)}, f32[13,8,128]{2,1,0:T(8,128)S(1)}, u32[]{:S(2)}, u32[]{:S(2)}) collective-permute-start(f32[13,8,128]{2,1,0:T(8,128)S(1)} %pack_sums.1.refs_0_), channel_id=1, source_target_pairs={{0,4},{4,8},{8,12},{12,0},{1,5},{5,9},{9,13},{13,1},{2,6},{6,10},{... | collective-permute-start | bytes 159752 | tf_op jit(solution)/shard_map/ppermute | solution.py:533
  117.2 6.0 %collective-permute-start.17 = (f32[16,8,128]{2,1,0:T(8,128)S(1)}, f32[16,8,128]{2,1,0:T(8,128)S(1)}, u32[]{:S(2)}, u32[]{:S(2)}) collective-permute-start(f32[16,8,128]{2,1,0:T(8,128)S(1)} %merge_sums.1.refs_0_), channel_id=1, source_target_pairs={{0,3},{1,0},{2,1},{3,2},{4,7},{5,4},{6,5},{7,6},{8,11},{9,8},{10,9... | collective-permute-start | bytes 196616 | tf_op jit(solution)/shard_map/ppermute | solution.py:533
  120.7 5.9 %collective-permute-start.18 = (f32[16,8,128]{2,1,0:T(8,128)S(1)}, f32[16,8,128]{2,1,0:T(8,128)S(1)}, u32[]{:S(2)}, u32[]{:S(2)}) collective-permute-start(f32[16,8,128]{2,1,0:T(8,128)S(1)} %merge_sums.1.refs_0_), channel_id=1, source_target_pairs={{0,2},{1,3},{2,0},{3,1},{4,6},{5,7},{6,4},{7,5},{8,10},{9,11},{10,... | collective-permute-start | bytes 196616 | tf_op jit(solution)/shard_map/ppermute | solution.py:533
  120.7 6.2 %collective-permute-start.19 = (f32[16,8,128]{2,1,0:T(8,128)S(1)}, f32[16,8,128]{2,1,0:T(8,128)S(1)}, u32[]{:S(2)}, u32[]{:S(2)}) collective-permute-start(f32[16,8,128]{2,1,0:T(8,128)S(1)} %merge_sums.1.refs_0_), channel_id=1, source_target_pairs={{0,1},{1,2},{2,3},{3,0},{4,5},{5,6},{6,7},{7,4},{8,9},{9,10},{10,1... | collective-permute-start | bytes 196616 | tf_op jit(solution)/shard_map/ppermute | solution.py:533
  132.7 3.9 %collective-permute-start.20 = (bf16[4,448,512]{2,1,0:T(8,128)(2,1)S(1)}, bf16[4,448,512]{2,1,0:T(8,128)(2,1)S(1)}, u32[]{:S(2)}, u32[]{:S(2)}) collective-permute-start(bf16[4,448,512]{2,1,0:T(8,128)(2,1)S(1)} %gradient_blocks.3), channel_id=1, source_target_pairs={{0,16},{16,0},{1,17},{17,1},{2,18},{18,2},{3,19},{19,3},{4,20},{20... | collective-permute-start | bytes 5505032 | tf_op jit(solution)/shard_map/ppermute | solution.py:540
  137.7 26.4 %collective-permute-start.21 = (bf16[1,448,512]{2,1,0:T(8,128)(2,1)}, bf16[1,448,512]{2,1,0:T(8,128)(2,1)S(1)}, u32[]{:S(2)}, u32[]{:S(2)}) collective-permute-start(bf16[1,448,512]{2,1,0:T(8,128)(2,1)} %get-tuple-element.120), channel_id=1, source_target_pairs={{0,64},{32,96},{64,0},{96,32},{1,65},{33,97},{65,1},{97,33},{2,66}... | collective-permute-start | bytes 1376264 | tf_op jit(solution)/shard_map/ppermute | solution.py:548
  138.9 25.2 %collective-permute-start.22 = (bf16[1,448,512]{2,1,0:T(8,128)(2,1)S(1)}, bf16[1,448,512]{2,1,0:T(8,128)(2,1)S(1)}, u32[]{:S(2)}, u32[]{:S(2)}) collective-permute-start(bf16[1,448,512]{2,1,0:T(8,128)(2,1)S(1)} %get-tuple-element.121), channel_id=1, source_target_pairs={{0,32},{32,64},{64,96},{96,0},{1,33},{33,65},{65,97},{97,1},{2,34}... | collective-permute-start | bytes 1376264 | tf_op jit(solution)/shard_map/ppermute | solution.py:548
  141.1 23.0 %collective-permute-start.23 = (bf16[1,448,512]{2,1,0:T(8,128)(2,1)S(1)}, bf16[1,448,512]{2,1,0:T(8,128)(2,1)S(1)}, u32[]{:S(2)}, u32[]{:S(2)}) collective-permute-start(bf16[1,448,512]{2,1,0:T(8,128)(2,1)S(1)} %get-tuple-element.122), channel_id=1, source_target_pairs={{0,96},{32,0},{64,32},{96,64},{1,97},{33,1},{65,33},{97,65},{2,98}... | collective-permute-start | bytes 1376264 | tf_op jit(solution)/shard_map/ppermute | solution.py:548
